TPU v7x, 512 devices: a whole 4x8x8 slice. The times are simulated.
512 devices in a mesh: rows: 32 (over z, y_hi), cols: 16 (over x, y_lo, core).
Axes of the slice: x: 4, y: 8 (y_hi: 4, y_lo: 2; y = y_hi * 2 + y_lo), z: 8, core: 2. Of those that a mesh axis runs over, the one named last changes fastest.
Arguments:
- adjoint: float32 [3, 128, 384, 256], P(None, 'cols', 'rows'), may hold values from -6 to 6
- base_flow: bfloat16 [3, 128, 384, 256], P(None, 'cols', 'rows'), may hold values from -6 to 6
- stream_pair: bfloat16 [512, 256], replicated, may hold values from -0.375 to 0.375
- normal_pair: bfloat16 [768, 384], replicated, may hold values from -0.3125 to 0.3125
- span_pair: bfloat16 [256, 128], replicated, may hold values from -0.5 to 0.5
Outputs:
- adjoint_next: float32 [3, 128, 384, 256], P(None, 'cols', 'rows')
All inputs are finite; a program needn't handle non-finite values.
Results may differ from a plain program's by a relative error of at most 0.0023.
Values may be sent and summed in bfloat16 or wider, within the bound.
No kernel may reach another device: no remote copies, remote signals or barrier semaphores. Data moves between devices by JAX's collectives and lax.ppermute only.
A program may use at most 64 MiB of HBM per device.

v0:
```python
import jax
import jax.numpy as jnp
from jax import lax
from jax.sharding import PartitionSpec as P

viscosity = 0.5
section_step = 0.5


def pack_lines(fields, pieces):
    count, outer, inner, length = fields.shape
    block = length // pieces
    split = fields.reshape(count, outer, inner, pieces, block)
    return split.transpose(0, 3, 1, 4, 2).reshape(count, pieces, outer, block * inner)


def unpack_lines(received, inner, outer_first):
    count, pieces, outer, merged = received.shape
    block = merged // inner
    split = received.reshape(count, pieces, outer, block, inner)
    if outer_first:
        return split.transpose(0, 2, 3, 1, 4).reshape(count, outer, block, pieces * inner)
    return split.transpose(0, 3, 2, 1, 4).reshape(count, block, outer, pieces * inner)


def direction_terms(lines, matrices, axis_index):
    length = lines.shape[3]
    adjoint_b = lines[:3]
    base_b = lines[3:]
    derivs = jnp.einsum("fabn,mn->fabm", adjoint_b, matrices, preferred_element_type=jnp.float32)
    first_deriv = derivs[..., :length]
    second = derivs[..., length:]
    base_deriv = jnp.einsum(
        "fabn,mn->fabm", base_b, matrices[:length], preferred_element_type=jnp.float32
    )
    adjoint_f = adjoint_b.astype(jnp.float32)
    base_f = base_b.astype(jnp.float32)
    transfer = jnp.sum(adjoint_f * base_deriv, axis=0)
    result = base_f[axis_index][None] * first_deriv + viscosity * second
    listing = [
        result[component] - transfer if component == axis_index else result[component]
        for component in range(3)
    ]
    return jnp.stack(listing)


def local(adjoint, base_flow, stream_pair, normal_pair, span_pair):
    row_count = lax.axis_size("rows")
    col_count = lax.axis_size("cols")
    stacked = jnp.concatenate([adjoint.astype(jnp.bfloat16), base_flow], axis=0)
    planes = stacked.shape[1]
    y_local = stacked.shape[2]
    terms_x = direction_terms(stacked, stream_pair, 0)

    def span_lines(portion):
        lines = unpack_lines(portion, planes, True)
        return direction_terms(lines, span_pair, 2)

    lines = unpack_lines(
        lax.all_to_all(
            pack_lines(stacked, row_count), "rows", split_axis=1, concat_axis=1, tiled=True
        ),
        y_local,
        False,
    )
    terms_y = direction_terms(lines, normal_pair, 1)
    terms_z = span_lines(
        lax.all_to_all(
            pack_lines(lines, col_count), "cols", split_axis=1, concat_axis=1, tiled=True
        )
    )
    returned = lax.all_to_all(
        pack_lines(terms_z, col_count), "cols", split_axis=1, concat_axis=1, tiled=True
    )
    gathered_y = terms_y + unpack_lines(returned, terms_z.shape[2], True)
    back = lax.all_to_all(
        pack_lines(gathered_y.transpose(0, 2, 1, 3), row_count),
        "rows",
        split_axis=1,
        concat_axis=1,
        tiled=True,
    )
    total = terms_x + unpack_lines(back, gathered_y.shape[1], True)
    return adjoint + section_step * total


def solution(mesh):
    placed = (P(None, "cols", "rows", None), P(None, "cols", "rows", None), P(), P(), P())
    return jax.shard_map(
        local, mesh=mesh, in_specs=placed, out_specs=P(None, "cols", "rows", None), check_vma=False
    )
```

profile of v0, /device:TPU:8, one launch (start us, length us, event | category | flops | bytes accessed | tf_op | source)
XLA Modules:
  0.0 151.8 jit_solution(6348005578658559588)
XLA Ops:
  2.2 6.5 %reshape.52 = bf16[6,8,12,32,8]{4,3,1,2,0:T(8,128)(2,1)} reshape(bf16[6,8,12,256]{3,1,2,0:T(8,128)(2,1)S(1)} %copy.114) | data formatting | bytes 589824 | tf_op jit(solution)/shard_map/reshape | solution.py:13
  8.8 4.0 %copy.115 = bf16[6,32,8,8,12]{1,2,4,3,0:T(8,128)(2,1)S(1)} copy(bf16[6,32,8,8,12]{3,1,2,4,0:T(8,128)(2,1)} %bitcast.99) | data formatting | bytes 589824 | tf_op jit(solution)/shard_map/transpose | solution.py:14
  14.4 15.1 %all-to-all-start = ((bf16[6,32,8,96]{3,2,0,1:T(8,128)(2,1)}), bf16[6,32,8,96]{3,2,0,1:T(8,128)(2,1)S(1)}, u32[]{:S(2)}, u32[]{:S(2)}) async-start(bf16[6,32,8,96]{3,2,0,1:T(8,128)(2,1)} %copy.116), calls=%async_computation | async-start | bytes 786432 | tf_op jit(solution)/shard_map/all_to_all | solution.py:60
  32.1 13.3 %all-to-all-done = bf16[6,32,8,96]{3,2,0,1:T(8,128)(2,1)S(1)} async-done(((bf16[6,32,8,96]{3,2,0,1:T(8,128)(2,1)}), bf16[6,32,8,96]{3,2,0,1:T(8,128)(2,1)S(1)}, u32[]{:S(2)}, u32[]{:S(2)}) %all-to-all-start) | async-done | bytes 294944 | tf_op jit(solution)/shard_map/all_to_all | solution.py:60
  45.3 1.7 %copy.117 = bf16[6,32,8,96]{1,2,3,0:T(8,128)(2,1)} copy(bf16[6,32,8,96]{3,2,0,1:T(8,128)(2,1)S(1)} %all-to-all-done) | data formatting | bytes 589824 | tf_op jit(solution)/shard_map/all_to_all | solution.py:60
  47.0 3.7 %copy.121 = bf16[6,8,8,32,12]{4,3,2,1,0:T(8,128)(2,1)S(1)} copy(bf16[6,8,8,32,12]{3,2,4,1,0:T(8,128)(2,1)} %bitcast.101) | data formatting | bytes 589824 | tf_op jit(solution)/shard_map/transpose | solution.py:23
  50.8 2.6 %reshape_reshape.3 = bf16[6,8,8,16,24]{4,3,2,1,0:T(8,128)(2,1)} reshape(bf16[6,8,8,32,12]{4,3,2,1,0:T(8,128)(2,1)S(1)} %copy.121) | data formatting | bytes 589824 | tf_op jit(solution)/shard_map/reshape;reshape | solution.py:13
  53.4 3.1 %copy.122 = bf16[6,16,8,24,8]{1,4,3,2,0:T(8,128)(2,1)S(1)} copy(bf16[6,16,8,24,8]{3,1,4,2,0:T(8,128)(2,1)} %bitcast.111) | data formatting | bytes 589824 | tf_op jit(solution)/shard_map/transpose | solution.py:14
  56.5 1.9 %copy.123 = bf16[6,16,8,192]{3,2,0,1:T(8,128)(2,1)} copy(bf16[6,16,8,192]{1,3,2,0:T(8,128)(2,1)S(1)} %bitcast.104) | data formatting | bytes 589824 | tf_op jit(solution)/shard_map/reshape | solution.py:14
  58.4 6.5 %all-to-all-start.1 = ((bf16[6,16,8,192]{3,2,0,1:T(8,128)(2,1)}), bf16[6,16,8,192]{3,2,0,1:T(8,128)(2,1)}, u32[]{:S(2)}, u32[]{:S(2)}) async-start(bf16[6,16,8,192]{3,2,0,1:T(8,128)(2,1)} %copy.123), calls=%async_computation.1 | async-start | bytes 786432 | tf_op jit(solution)/shard_map/all_to_all | solution.py:68
  65.8 2.3 %copy.119 = bf16[3,8,8,32,12]{4,3,2,1,0:T(8,128)(2,1)S(1)} copy(bf16[3,8,8,32,12]{3,2,4,1,0:T(8,128)(2,1)} %get-tuple-element.6) | data formatting | bytes 294912 | tf_op jit(solution)/shard_map/slice | solution.py:28
  68.2 3.7 %slice.100 = bf16[3,8,8,384]{3,2,1,0:T(8,128)(2,1)} reshape(bf16[3,8,8,32,12]{4,3,2,1,0:T(8,128)(2,1)S(1)} %copy.119) | data formatting | bytes 294912 | tf_op jit(solution)/shard_map/slice | solution.py:28
  73.3 3.7 %slice.106 = bf16[3,8,8,384]{3,2,1,0:T(8,128)(2,1)} reshape(bf16[3,8,8,32,12]{4,3,2,1,0:T(8,128)(2,1)S(1)} %copy.120) | data formatting | bytes 294912 | tf_op jit(solution)/shard_map/slice | solution.py:29
  79.2 2.0 %copy.124 = bf16[6,16,8,192]{1,3,2,0:T(8,128)(2,1)S(1)} copy(bf16[6,16,8,192]{3,2,0,1:T(8,128)(2,1)} %all-to-all-done.1) | data formatting | bytes 589824 | tf_op jit(solution)/shard_map/all_to_all | solution.py:68
  81.2 2.7 %copy.125 = bf16[6,16,8,24,8]{3,4,1,2,0:T(8,128)(2,1)} copy(bf16[6,16,8,24,8]{1,4,3,2,0:T(8,128)(2,1)S(1)} %bitcast.105) | data formatting | bytes 589824 | tf_op jit(solution)/shard_map/reshape | solution.py:20
  95.5 5.7 %all-to-all-start.2 = ((f32[3,16,8,192]{3,2,0,1:T(8,128)}), f32[3,16,8,192]{3,2,0,1:T(8,128)S(1)}, u32[]{:S(2)}, u32[]{:S(2)}) async-start(f32[3,16,8,192]{3,2,0,1:T(8,128)} %copy.133), calls=%async_computation.2 | async-start | bytes 786432 | tf_op jit(solution)/shard_map/all_to_all | solution.py:72
  101.6 7.9 %all-to-all-done.2 = f32[3,16,8,192]{3,2,0,1:T(8,128)S(1)} async-done(((f32[3,16,8,192]{3,2,0,1:T(8,128)}), f32[3,16,8,192]{3,2,0,1:T(8,128)S(1)}, u32[]{:S(2)}, u32[]{:S(2)}) %all-to-all-start.2) | async-done | bytes 294944 | tf_op jit(solution)/shard_map/all_to_all | solution.py:72
  111.9 3.4 %reshape.60 = f32[3,8,8,32,12]{4,3,2,1,0:T(8,128)S(1)} reshape(f32[3,8,8,384]{3,2,1,0:T(8,128)S(1)} %copy.136) | data formatting | bytes 589824 | tf_op jit(solution)/shard_map/reshape | solution.py:13
  115.3 2.4 %copy.137 = f32[3,32,8,12,8]{1,4,3,2,0:T(8,128)} copy(f32[3,32,8,12,8]{3,1,4,2,0:T(8,128)S(1)} %bitcast.100) | data formatting | bytes 589824 | tf_op jit(solution)/shard_map/transpose | solution.py:14
  117.7 2.5 %copy.138 = f32[3,32,8,96]{3,2,0,1:T(8,128)} copy(f32[3,32,8,96]{1,3,2,0:T(8,128)} %bitcast.113) | data formatting | bytes 589824 | tf_op jit(solution)/shard_map/reshape | solution.py:14
  120.2 5.5 %all-to-all-start.3 = ((f32[3,32,8,96]{3,2,0,1:T(8,128)}), f32[3,32,8,96]{3,2,0,1:T(8,128)S(1)}, u32[]{:S(2)}, u32[]{:S(2)}) async-start(f32[3,32,8,96]{3,2,0,1:T(8,128)} %copy.138), calls=%async_computation.3 | async-start | bytes 786432 | tf_op jit(solution)/shard_map/all_to_all | solution.py:76
  126.2 17.1 %all-to-all-done.3 = f32[3,32,8,96]{3,2,0,1:T(8,128)S(1)} async-done(((f32[3,32,8,96]{3,2,0,1:T(8,128)}), f32[3,32,8,96]{3,2,0,1:T(8,128)S(1)}, u32[]{:S(2)}, u32[]{:S(2)}) %all-to-all-start.3) | async-done | bytes 294944 | tf_op jit(solution)/shard_map/all_to_all | solution.py:76
  143.6 3.0 %copy.140 = f32[3,8,12,32,8]{4,3,1,2,0:T(8,128)} copy(f32[3,8,12,32,8]{3,4,2,1,0:T(8,128)S(1)} %bitcast.114) | data formatting | bytes 589824 | tf_op jit(solution)/shard_map/transpose | solution.py:22
  146.6 4.4 %reshape.63 = f32[3,8,12,256]{3,1,2,0:T(8,128)S(1)} reshape(f32[3,8,12,32,8]{4,3,1,2,0:T(8,128)} %copy.140) | data formatting | bytes 589824 | tf_op jit(solution)/shard_map/reshape | solution.py:22
  (75 shorter events, 26.5 us)
Async XLA Ops:
  1.0 29.9 %copy-start.3 = (bf16[3,8,12,256]{3,2,1,0:T(8,128)(2,1)}, bf16[3,8,12,256]{3,2,1,0:T(8,128)(2,1)S(1)}, u32[]{:S(2)}) copy-start(bf16[3,8,12,256]{3,2,1,0:T(8,128)(2,1)S(1)} %copy.159) | copy-start | bytes 442372
  12.8 18.1 %copy-start.13 = (bf16[512,256]{1,0:T(8,128)(2,1)S(1)}, bf16[512,256]{1,0:T(8,128)(2,1)}, u32[]{:S(2)}) copy-start(bf16[512,256]{1,0:T(8,128)(2,1)} %param.7) | copy-start | bytes 786436
  14.4 30.9 %all-to-all-start = ((bf16[6,32,8,96]{3,2,0,1:T(8,128)(2,1)}), bf16[6,32,8,96]{3,2,0,1:T(8,128)(2,1)S(1)}, u32[]{:S(2)}, u32[]{:S(2)}) async-start(bf16[6,32,8,96]{3,2,0,1:T(8,128)(2,1)} %copy.116), calls=%async_computation | async-start | bytes 786432 | tf_op jit(solution)/shard_map/all_to_all | solution.py:60
  56.5 8.4 %copy-start = (bf16[6,32,8,96]{1,2,3,0:T(8,128)(2,1)S(1)}, bf16[6,32,8,96]{1,2,3,0:T(8,128)(2,1)}, u32[]{:S(2)}) copy-start(bf16[6,32,8,96]{1,2,3,0:T(8,128)(2,1)} %copy.117) | copy-start | bytes 884740
  58.4 20.8 %all-to-all-start.1 = ((bf16[6,16,8,192]{3,2,0,1:T(8,128)(2,1)}), bf16[6,16,8,192]{3,2,0,1:T(8,128)(2,1)}, u32[]{:S(2)}, u32[]{:S(2)}) async-start(bf16[6,16,8,192]{3,2,0,1:T(8,128)(2,1)} %copy.123), calls=%async_computation.1 | async-start | bytes 786432 | tf_op jit(solution)/shard_map/all_to_all | solution.py:68
  77.1 1.8 %copy-start.6 = (bf16[768,384]{1,0:T(8,128)(2,1)S(1)}, bf16[768,384]{1,0:T(8,128)(2,1)}, u32[]{:S(2)}) copy-start(bf16[768,384]{1,0:T(8,128)(2,1)} %param.8) | copy-start | bytes 1769476
  77.1 1.8 %copy-start.8 = (bf16[3,8,8,384]{3,2,1,0:T(8,128)(2,1)S(1)}, bf16[3,8,8,384]{3,2,1,0:T(8,128)(2,1)}, u32[]{:S(2)}) copy-start(bf16[3,8,8,384]{3,2,1,0:T(8,128)(2,1)} %slice.100) | copy-start | bytes 442372
  84.0 3.1 %copy-start.1 = (bf16[6,16,8,24,8]{3,4,1,2,0:T(8,128)(2,1)S(1)}, bf16[6,16,8,24,8]{3,4,1,2,0:T(8,128)(2,1)}, u32[]{:S(2)}) copy-start(bf16[6,16,8,24,8]{3,4,1,2,0:T(8,128)(2,1)} %copy.125) | copy-start | bytes 884740
  94.0 7.2 %copy-start.7 = (bf16[768,384]{1,0:T(8,128)(2,1)S(1)}, bf16[768,384]{1,0:T(8,128)(2,1)}, u32[]{:S(2)}) copy-start(bf16[768,384]{1,0:T(8,128)(2,1)} %param.8) | copy-start | bytes 1769476
  94.0 7.2 %copy-start.9 = (bf16[3,8,8,384]{3,2,1,0:T(8,128)(2,1)S(1)}, bf16[3,8,8,384]{3,2,1,0:T(8,128)(2,1)}, u32[]{:S(2)}) copy-start(bf16[3,8,8,384]{3,2,1,0:T(8,128)(2,1)} %slice.100) | copy-start | bytes 442372
  94.0 7.2 %copy-start.15 = (bf16[3,8,8,384]{3,2,1,0:T(8,128)(2,1)S(1)}, bf16[3,8,8,384]{3,2,1,0:T(8,128)(2,1)}, u32[]{:S(2)}) copy-start(bf16[3,8,8,384]{3,2,1,0:T(8,128)(2,1)} %slice.106) | copy-start | bytes 442372
  94.5 7.0 %copy-start.10 = (f32[8,8,384]{2,1,0:T(8,128)S(1)}, f32[8,8,384]{2,1,0:T(8,128)}, u32[]{:S(2)}) copy-start(f32[8,8,384]{2,1,0:T(8,128)} %reshape.65) | copy-start | bytes 294916
  95.5 14.0 %all-to-all-start.2 = ((f32[3,16,8,192]{3,2,0,1:T(8,128)}), f32[3,16,8,192]{3,2,0,1:T(8,128)S(1)}, u32[]{:S(2)}, u32[]{:S(2)}) async-start(f32[3,16,8,192]{3,2,0,1:T(8,128)} %copy.133), calls=%async_computation.2 | async-start | bytes 786432 | tf_op jit(solution)/shard_map/all_to_all | solution.py:72
  117.7 8.0 %copy-start.2 = (f32[3,8,12,512]{3,1,2,0:T(8,128)S(1)}, f32[3,8,12,512]{3,1,2,0:T(8,128)}, u32[]{:S(2)}) copy-start(f32[3,8,12,512]{3,1,2,0:T(8,128)} %fusion.14) | copy-start | bytes 1769476
  117.7 8.0 %copy-start.11 = (f32[8,12,256]{2,0,1:T(8,128)S(1)}, f32[8,12,256]{2,0,1:T(8,128)}, u32[]{:S(2)}) copy-start(f32[8,12,256]{2,0,1:T(8,128)} %bitcast_convert_fusion) | copy-start | bytes 294916
  117.7 8.1 %copy-start.4 = (bf16[3,8,12,256]{3,2,1,0:T(8,128)(2,1)S(1)}, bf16[3,8,12,256]{3,2,1,0:T(8,128)(2,1)}, u32[]{:S(2)}) copy-start(bf16[3,8,12,256]{3,2,1,0:T(8,128)(2,1)} %copy-done.3) | copy-start | bytes 442372
  117.7 8.1 %copy-start.12 = (bf16[3,8,12,256]{3,1,2,0:T(8,128)(2,1)S(1)}, bf16[3,8,12,256]{3,1,2,0:T(8,128)(2,1)}, u32[]{:S(2)}) copy-start(bf16[3,8,12,256]{3,1,2,0:T(8,128)(2,1)} %param.6) | copy-start | bytes 442372
  117.7 8.1 %copy-start.14 = (bf16[512,256]{1,0:T(8,128)(2,1)S(1)}, bf16[512,256]{1,0:T(8,128)(2,1)}, u32[]{:S(2)}) copy-start(bf16[512,256]{1,0:T(8,128)(2,1)} %param.7) | copy-start | bytes 786436
  120.2 23.0 %all-to-all-start.3 = ((f32[3,32,8,96]{3,2,0,1:T(8,128)}), f32[3,32,8,96]{3,2,0,1:T(8,128)S(1)}, u32[]{:S(2)}, u32[]{:S(2)}) async-start(f32[3,32,8,96]{3,2,0,1:T(8,128)} %copy.138), calls=%async_computation.3 | async-start | bytes 786432 | tf_op jit(solution)/shard_map/all_to_all | solution.py:76
  146.6 4.4 %copy-start.5 = (f32[3,8,12,256]{3,1,2,0:T(8,128)S(1)}, f32[3,8,12,256]{3,1,2,0:T(8,128)}, u32[]{:S(2)}) copy-start(f32[3,8,12,256]{3,1,2,0:T(8,128)} %param.5) | copy-start | bytes 884740
where the time goes:
time: 153 us; the launch traced here: 152 us
  local copies, waits for them, and re-layouts  70 us (46%)
  waiting for transfers between devices  38.3 us (25%)
  starting transfers between devices  32.8 us (21%)
  other arithmetic  5.74 us (4%)
  matrix products  4.48 us (3%)
    all_to_all x1, waiting for transfers between devices, local(): lax.all_to_all(pack_lines(gathered_y.transpose(0, 2, 1, 3), row_count), '...  17.1 us
    all_to_all x1, starting transfers between devices, local(): lax.all_to_all(pack_lines(stacked, row_count), 'rows', split_axis=1, conc...  15.1 us
    all_to_all x1, waiting for transfers between devices, local(): lax.all_to_all(pack_lines(stacked, row_count), 'rows', split_axis=1, conc...  13.3 us
    reshape x2, local copies, waits for them, and re-layouts, pack_lines(): split = fields.reshape(count, outer, inner, pieces, block)  9.98 us
    transpose x3, local copies, waits for them, and re-layouts, pack_lines(): split.transpose(0, 3, 1, 4, 2).reshape(count, pieces, outer, block * inner)  9.51 us
    slice x4, local copies, waits for them, and re-layouts, direction_terms(): adjoint_b = lines[:3]  8.18 us
    all_to_all x1, waiting for transfers between devices, local(): lax.all_to_all(pack_lines(terms_z, col_count), 'cols', split_axis=1, conc...  7.91 us
    reshape x5, local copies, waits for them, and re-layouts, pack_lines(): split.transpose(0, 3, 1, 4, 2).reshape(count, pieces, outer, block * inner)  7.39 us
  transfers between devices with their start and end apart: 4, of which 3 were waited for; matrix products, arithmetic and copies ran while one was open for 12% of the time, Pallas kernels for 0%

commit v1 on v0

v1 whole, which is shorter than its diff:
```python
import functools

import jax
import jax.numpy as jnp
from jax import lax
from jax.experimental import pallas as pl
from jax.experimental.pallas import tpu as pltpu
from jax.sharding import PartitionSpec as P

viscosity = 0.5
section_step = 0.5
LANES = 128
HALF = 64
PITCH = 40


def left_half(shape):
    return lax.broadcasted_iota(jnp.int32, shape, len(shape) - 1) < HALF


def swap(value):
    return pltpu.roll(value, HALF, value.ndim - 1)


def pack_kernel(a_ref, u_ref, sz_ref, sy_ref, stage):
    comps, y_own, z_own = a_ref.shape[:3]
    left = left_half((y_own, z_own, LANES))
    for j in range(comps):
        for t in range(2):
            a = a_ref[j, :, :, pl.ds(t * LANES, LANES)]
            u = u_ref[j, :, :, pl.ds(t * LANES, LANES)].astype(jnp.float32)
            for h in range(2):
                q = 2 * t + h
                pair = jnp.where(left, a, swap(u)) if h == 0 else jnp.where(left, swap(a), u)
                for group in range(4):
                    sz_ref[group * 4 + q, pl.ds(3 * j, 3)] = pair[3 * group : 3 * group + 3].astype(jnp.bfloat16)
                for y in range(y_own):
                    stage[pl.ds(q * PITCH + j * y_own + y, z_own, stride=4 * PITCH), :] = pair[y]
    rows = comps * y_own
    for p in range(4 * z_own):
        sy_ref[p] = stage[pl.ds(p * PITCH, rows), :].astype(jnp.bfloat16)


def x_kernel(a_ref, u_ref, px_ref, out_ref):
    comps, y_own, z_own, length = a_ref.shape
    rows = y_own * z_own
    px = px_ref[...]
    dims = (((1,), (1,)), ((), ()))
    adjoint = a_ref[...].reshape(comps * rows, length)
    a_b = adjoint.astype(jnp.bfloat16)
    u_f = u_ref[...].astype(jnp.float32).reshape(comps * rows, length)
    derivs = lax.dot_general(a_b, px, dims, preferred_element_type=jnp.float32)
    base_deriv = lax.dot_general(
        u_f.astype(jnp.bfloat16), px[:length], dims, preferred_element_type=jnp.float32
    )
    a_f = a_b.astype(jnp.float32)
    products = a_f * base_deriv
    transfer = products[:rows] + products[rows : 2 * rows] + products[2 * rows :]
    u_dir = u_f[:rows]
    for c in range(comps):
        part = slice(c * rows, (c + 1) * rows)
        term = u_dir * derivs[part, :length] + viscosity * derivs[part, length:]
        if c == 0:
            term = term - transfer
        out_ref[c] = (adjoint[part] + section_step * term).reshape(y_own, z_own, length)


def z_kernel(rz_ref, pz_ref, oz_ref, result):
    peers, slabs, z_own = rz_ref.shape[:3]
    length = peers * z_own
    lines = [rz_ref[:, k].astype(jnp.float32).reshape(length, LANES) for k in range(slabs)]
    packed = jnp.concatenate([v.astype(jnp.bfloat16) for v in lines], axis=1)
    result[...] = jnp.dot(pz_ref[...], packed, preferred_element_type=jnp.float32)
    left = left_half((length, LANES))
    last = []
    for y in range(3):
        vs = [lines[3 * j + y] for j in range(3)]
        ds = [result[:length, pl.ds((3 * j + y) * LANES, LANES)] for j in range(3)]
        ss = [result[length:, pl.ds((3 * j + y) * LANES, LANES)] for j in range(3)]
        u_dir = swap(vs[2])
        transfer = vs[0] * swap(ds[0]) + vs[1] * swap(ds[1]) + vs[2] * swap(ds[2])
        terms = [u_dir * ds[c] + viscosity * ss[c] for c in range(3)]
        last.append(terms[2] - transfer)
        both = jnp.where(left, terms[0], swap(terms[1]))
        oz_ref[:, y] = both.reshape(peers, z_own, LANES).astype(jnp.bfloat16)
    both = jnp.where(left, last[0], swap(last[1]))
    oz_ref[:, 3] = both.reshape(peers, z_own, LANES).astype(jnp.bfloat16)
    oz_ref[:, 4] = last[2].reshape(peers, z_own, LANES).astype(jnp.bfloat16)


def y_kernel(ry_ref, py_ref, oy_ref, stage, lines, result, terms_ref, back):
    peers, rows = ry_ref.shape[:2]
    y_own = rows // 3
    length = peers * y_own
    for p in range(peers):
        stage[pl.ds(p * PITCH, rows), :] = ry_ref[p].astype(jnp.float32)
    for j in range(3):
        for y in range(y_own):
            for g in range(peers // 8):
                lines[j, pl.ds(8 * g * y_own + y, 8, stride=y_own), :] = stage[
                    pl.ds(8 * g * PITCH + j * y_own + y, 8, stride=PITCH), :
                ]
    packed = jnp.concatenate([lines[j].astype(jnp.bfloat16) for j in range(3)], axis=1)
    result[...] = jnp.dot(py_ref[...], packed, preferred_element_type=jnp.float32)
    block = 48
    left = left_half((block, LANES))
    for b in range(length // block):
        at = pl.ds(b * block, block)
        vs = [lines[j, at, :] for j in range(3)]
        ds = [result[at, pl.ds(j * LANES, LANES)] for j in range(3)]
        ss = [result[pl.ds(length + b * block, block), pl.ds(j * LANES, LANES)] for j in range(3)]
        u_dir = swap(vs[1])
        transfer = vs[0] * swap(ds[0]) + vs[1] * swap(ds[1]) + vs[2] * swap(ds[2])
        terms = [u_dir * ds[c] + viscosity * ss[c] for c in range(3)]
        terms_ref[0, at, :] = jnp.where(left, terms[0], swap(terms[1] - transfer))
        terms_ref[1, at, :] = terms[2]
    for h in range(2):
        for y in range(y_own):
            for g in range(peers // 8):
                back[pl.ds(8 * g * 2 * y_own + h * y_own + y, 8, stride=2 * y_own), :] = terms_ref[
                    h, pl.ds(8 * g * y_own + y, 8, stride=y_own), :
                ]
    oy_ref[...] = back[...].reshape(peers, 2 * y_own, LANES).astype(jnp.bfloat16)


def final_kernel(base_ref, rz_ref, ry_ref, out_ref, stage):
    comps, y_own, z_own, _ = base_ref.shape
    left = left_half((z_own, LANES))
    pitch = 2 * y_own
    stage[...] = ry_ref[...].astype(jnp.float32).reshape(stage.shape)

    def y_piece(q, h, y):
        return stage[pl.ds(q * pitch + h * y_own + y, z_own, stride=4 * pitch), :]

    def z_piece(q, y, m):
        return rz_ref[(y // 3) * 4 + q, m].astype(jnp.float32)

    for y in range(y_own):
        w = y % 3
        for t in range(2):
            at = pl.ds(t * LANES, LANES)
            even = y_piece(2 * t, 0, y) + z_piece(2 * t, y, w)
            odd = y_piece(2 * t + 1, 0, y) + z_piece(2 * t + 1, y, w)
            even_last, odd_last = z_piece(2 * t, y, 3 + w // 2), z_piece(2 * t + 1, y, 3 + w // 2)
            if w == 1:
                even_last, odd_last = swap(even_last), swap(odd_last)
            even_last = even_last + y_piece(2 * t, 1, y)
            odd_last = odd_last + y_piece(2 * t + 1, 1, y)
            sums = (
                jnp.where(left, even, swap(odd)),
                jnp.where(left, swap(even), odd),
                jnp.where(left, even_last, swap(odd_last)),
            )
            for c in range(comps):
                out_ref[c, y, :, at] = base_ref[c, y, :, at] + section_step * sums[c]


def local(adjoint, base_flow, stream_pair, normal_pair, span_pair):
    f32, bf16 = jnp.float32, jnp.bfloat16
    rows = lax.axis_size("rows")
    cols = lax.axis_size("cols")
    comps, z_own, y_own, length_x = adjoint.shape
    length_y = rows * y_own
    length_z = cols * z_own
    a = adjoint.transpose(0, 2, 1, 3)
    u = base_flow.transpose(0, 2, 1, 3)
    shape = jax.ShapeDtypeStruct
    exchange = functools.partial(lax.all_to_all, split_axis=0, concat_axis=0, tiled=True)

    send_z, send_y = pl.pallas_call(
        pack_kernel,
        name="pack",
        out_shape=(
            shape((cols, 3 * comps, z_own, LANES), bf16),
            shape((rows, comps * y_own, LANES), bf16),
        ),
        scratch_shapes=[pltpu.VMEM((rows * PITCH, LANES), f32)],
    )(a, u)
    with jax.named_scope("z_out"):
        recv_z = exchange(send_z, "cols")
    with jax.named_scope("y_out"):
        recv_y = exchange(send_y, "rows")
    base = pl.pallas_call(
        x_kernel, name="x_terms", out_shape=shape(a.shape, f32)
    )(a, u, stream_pair)
    terms_z = pl.pallas_call(
        z_kernel,
        name="z_terms",
        out_shape=shape((cols, 5, z_own, LANES), bf16),
        scratch_shapes=[pltpu.VMEM((2 * length_z, 3 * comps * LANES), f32)],
    )(recv_z, span_pair)
    with jax.named_scope("z_back"):
        back_z = exchange(terms_z, "cols")
    terms_y = pl.pallas_call(
        y_kernel,
        name="y_terms",
        out_shape=shape((rows, 2 * y_own, LANES), bf16),
        scratch_shapes=[
            pltpu.VMEM((rows * PITCH, LANES), f32),
            pltpu.VMEM((comps, length_y, LANES), f32),
            pltpu.VMEM((2 * length_y, comps * LANES), f32),
            pltpu.VMEM((2, length_y, LANES), f32),
            pltpu.VMEM((rows * 2 * y_own, LANES), f32),
        ],
    )(recv_y, normal_pair)
    with jax.named_scope("y_back"):
        back_y = exchange(terms_y, "rows")
    out = pl.pallas_call(
        final_kernel,
        name="final",
        out_shape=shape(a.shape, f32),
        scratch_shapes=[pltpu.VMEM((rows * 2 * y_own, LANES), f32)],
    )(base, back_z, back_y)
    return out.transpose(0, 2, 1, 3)


def solution(mesh):
    placed = (P(None, "cols", "rows", None), P(None, "cols", "rows", None), P(), P(), P())
    return jax.shard_map(
        local, mesh=mesh, in_specs=placed, out_specs=P(None, "cols", "rows", None), check_vma=False
    )
```

time: 153 us -> 78 us (0.51)
  the two profiles are of different devices: /device:TPU:8 before, /device:TPU:1 now
where the time goes in v1:
time: 78 us; the launch traced here: 77 us
  waiting for transfers between devices  23.1 us (30%)
  starting transfers between devices  22.9 us (29%)
  blocking collectives  18.4 us (24%)
  Pallas kernels  11.3 us (14%)
  local copies, waits for them, and re-layouts  1.33 us (2%)
    all_to_all x1, blocking collectives, local(): recv_z = exchange(send_z, 'cols')  18.4 us
    all_to_all x1, starting transfers between devices, local(): recv_y = exchange(send_y, 'rows')  10.8 us
    all_to_all x1, waiting for transfers between devices, local(): recv_y = exchange(send_y, 'rows')  10 us
    all_to_all x1, waiting for transfers between devices, local(): back_y = exchange(terms_y, 'rows')  9.34 us
    all_to_all x1, starting transfers between devices, local(): back_z = exchange(terms_z, 'cols')  7.24 us
    all_to_all x1, starting transfers between devices, local(): back_y = exchange(terms_y, 'rows')  4.85 us
    all_to_all x1, waiting for transfers between devices, local(): back_z = exchange(terms_z, 'cols')  3.72 us
    pallas_call x1, Pallas kernels, local(): pl.pallas_call(y_kernel, name='y_terms', out_shape=shape((rows, 2 * y_own...  2.68 us
  transfers between devices with their start and end apart: 3, of which 3 were waited for; matrix products, arithmetic and copies ran while one was open for 0% of the time, Pallas kernels for 9%

profile of v1, /device:TPU:1, one launch (start us, length us, event | category | flops | bytes accessed | tf_op | source)
XLA Modules:
  0.0 77.0 jit_solution(8812898673314031501)
XLA Ops:
  0.0 2.3 %pack.1 = (bf16[16,9,8,128]{3,2,1,0:T(8,128)(2,1)}, bf16[32,36,128]{2,1,0:T(8,128)(2,1)}) custom-call(f32[3,12,8,256]{3,2,1,0:T(8,128)} %bitcast.3, bf16[3,12,8,256]{3,2,1,0:T(8,128)(2,1)} %bitcast.5), custom_call_target="tpu_custom_call" | custom-call | tf_op jit(solution)/shard_map/pack/pallas_call | solution.py:170
  2.3 18.4 %all_to_all.20.rz_ref = bf16[16,9,8,128]{3,2,1,0:T(8,128)(2,1)} all-to-all(bf16[16,9,8,128]{3,2,1,0:T(8,128)(2,1)} %get-tuple-element.7), channel_id=1, replica_groups=mesh['rows'=32,'cols'=16] {'cols'}, dimensions={0} | all-to-all | bytes 589824 | tf_op jit(solution)/shard_map/z_out/all_to_all | solution.py:180
  20.7 10.8 %all-to-all-start.2 = ((bf16[32,36,128]{2,1,0:T(8,128)(2,1)}), bf16[32,36,128]{2,1,0:T(8,128)(2,1)S(1)}, u32[]{:S(2)}, u32[]{:S(2)}) async-start(bf16[32,36,128]{2,1,0:T(8,128)(2,1)} %get-tuple-element.8), calls=%async_computation.2 | async-start | bytes 655360 | tf_op jit(solution)/shard_map/y_out/all_to_all | solution.py:182
  31.5 2.1 %z_terms.1 = bf16[16,5,8,128]{3,2,1,0:T(8,128)(2,1)} custom-call(bf16[16,9,8,128]{3,2,1,0:T(8,128)(2,1)} %all_to_all.20.rz_ref, bf16[256,128]{1,0:T(8,128)(2,1)} %pz_ref.1), custom_call_target="tpu_custom_call" | custom-call | tf_op jit(solution)/shard_map/z_terms/pallas_call | solution.py:186
  33.5 10.0 %all-to-all-done.2.ry_ref = bf16[32,36,128]{2,1,0:T(8,128)(2,1)S(1)} async-done(((bf16[32,36,128]{2,1,0:T(8,128)(2,1)}), bf16[32,36,128]{2,1,0:T(8,128)(2,1)S(1)}, u32[]{:S(2)}, u32[]{:S(2)}) %all-to-all-start.2) | async-done | bytes 294944 | tf_op jit(solution)/shard_map/y_out/all_to_all | solution.py:182
  43.6 0.0 copy-start
  43.6 7.2 %all-to-all-start.1 = ((bf16[16,5,8,128]{3,2,1,0:T(8,128)(2,1)}), bf16[16,5,8,128]{3,2,1,0:T(8,128)(2,1)S(1)}, u32[]{:S(2)}, u32[]{:S(2)}) async-start(bf16[16,5,8,128]{3,2,1,0:T(8,128)(2,1)} %z_terms.1), calls=%async_computation.1 | async-start | bytes 327680 | tf_op jit(solution)/shard_map/z_back/all_to_all | solution.py:193
  50.8 0.0 copy-done
  50.8 2.7 %y_terms.1 = bf16[32,24,128]{2,1,0:T(8,128)(2,1)} custom-call(bf16[32,36,128]{2,1,0:T(8,128)(2,1)} %copy-done, bf16[768,384]{1,0:T(8,128)(2,1)} %py_ref.1), custom_call_target="tpu_custom_call" | custom-call | tf_op jit(solution)/shard_map/y_terms/pallas_call | solution.py:194
  53.5 3.7 %all-to-all-done.1.rz_ref = bf16[16,5,8,128]{3,2,1,0:T(8,128)(2,1)S(1)} async-done(((bf16[16,5,8,128]{3,2,1,0:T(8,128)(2,1)}), bf16[16,5,8,128]{3,2,1,0:T(8,128)(2,1)S(1)}, u32[]{:S(2)}, u32[]{:S(2)}) %all-to-all-start.1) | async-done | bytes 163872 | tf_op jit(solution)/shard_map/z_back/all_to_all | solution.py:193
  57.2 0.0 copy-start.2
  57.2 0.7 copy-done.2
  57.9 4.8 %all-to-all-start.3 = ((bf16[32,24,128]{2,1,0:T(8,128)(2,1)}), bf16[32,24,128]{2,1,0:T(8,128)(2,1)S(1)}, u32[]{:S(2)}, u32[]{:S(2)}) async-start(bf16[32,24,128]{2,1,0:T(8,128)(2,1)} %y_terms.1), calls=%async_computation.3 | async-start | bytes 393216 | tf_op jit(solution)/shard_map/y_back/all_to_all | solution.py:207
  62.7 2.2 %x_terms.1.base_ref = f32[3,12,8,256]{3,2,1,0:T(8,128)} custom-call(f32[3,12,8,256]{3,2,1,0:T(8,128)} %bitcast.4, bf16[3,12,8,256]{3,2,1,0:T(8,128)(2,1)} %bitcast.6, bf16[512,256]{1,0:T(8,128)(2,1)} %px_ref.1), custom_call_target="tpu_custom_call" | custom-call | tf_op jit(solution)/shard_map/x_terms/pallas_call | solution.py:183
  64.9 9.3 %all-to-all-done.3.ry_ref = bf16[32,24,128]{2,1,0:T(8,128)(2,1)S(1)} async-done(((bf16[32,24,128]{2,1,0:T(8,128)(2,1)}), bf16[32,24,128]{2,1,0:T(8,128)(2,1)S(1)}, u32[]{:S(2)}, u32[]{:S(2)}) %all-to-all-start.3) | async-done | bytes 196640 | tf_op jit(solution)/shard_map/y_back/all_to_all | solution.py:207
  74.3 0.0 copy-start.1
  74.3 0.7 copy-done.1
  74.9 2.1 %final.1 = f32[3,12,8,256]{3,2,1,0:T(8,128)} custom-call(f32[3,12,8,256]{3,2,1,0:T(8,128)} %x_terms.1.base_ref, bf16[16,5,8,128]{3,2,1,0:T(8,128)(2,1)} %copy-done.2, bf16[32,24,128]{2,1,0:T(8,128)(2,1)} %copy-done.1), custom_call_target="tpu_custom_call" | custom-call | tf_op jit(solution)/shard_map/final/pallas_call | solution.py:208
Async XLA Ops:
  20.7 22.9 %all-to-all-start.2 = ((bf16[32,36,128]{2,1,0:T(8,128)(2,1)}), bf16[32,36,128]{2,1,0:T(8,128)(2,1)S(1)}, u32[]{:S(2)}, u32[]{:S(2)}) async-start(bf16[32,36,128]{2,1,0:T(8,128)(2,1)} %get-tuple-element.8), calls=%async_computation.2 | async-start | bytes 655360 | tf_op jit(solution)/shard_map/y_out/all_to_all | solution.py:182
  43.6 7.2 %copy-start = (bf16[32,36,128]{2,1,0:T(8,128)(2,1)}, bf16[32,36,128]{2,1,0:T(8,128)(2,1)S(1)}, u32[]{:S(2)}) copy-start(bf16[32,36,128]{2,1,0:T(8,128)(2,1)S(1)} %all-to-all-done.2.ry_ref) | copy-start | bytes 884740
  43.6 13.7 %all-to-all-start.1 = ((bf16[16,5,8,128]{3,2,1,0:T(8,128)(2,1)}), bf16[16,5,8,128]{3,2,1,0:T(8,128)(2,1)S(1)}, u32[]{:S(2)}, u32[]{:S(2)}) async-start(bf16[16,5,8,128]{3,2,1,0:T(8,128)(2,1)} %z_terms.1), calls=%async_computation.1 | async-start | bytes 327680 | tf_op jit(solution)/shard_map/z_back/all_to_all | solution.py:193
  57.2 0.7 copy-start.2
  57.9 16.4 %all-to-all-start.3 = ((bf16[32,24,128]{2,1,0:T(8,128)(2,1)}), bf16[32,24,128]{2,1,0:T(8,128)(2,1)S(1)}, u32[]{:S(2)}, u32[]{:S(2)}) async-start(bf16[32,24,128]{2,1,0:T(8,128)(2,1)} %y_terms.1), calls=%async_computation.3 | async-start | bytes 393216 | tf_op jit(solution)/shard_map/y_back/all_to_all | solution.py:207
  74.3 0.7 copy-start.1

commit v2 on v1

--- a/solution.py
+++ b/solution.py
@@ -22,26 +22,45 @@
     return pltpu.roll(value, HALF, value.ndim - 1)
 
 
-def pack_kernel(a_ref, u_ref, sz_ref, sy_ref, stage):
+def pair_up(a_ref, u_ref, j, t, h, left):
+    at = pl.ds(t * LANES, LANES)
+    a = a_ref[j, :, :, at]
+    u = u_ref[j, :, :, at].astype(jnp.float32)
+    return jnp.where(left, a, swap(u)) if h == 0 else jnp.where(left, swap(a), u)
+
+
+def pack_z_kernel(a_ref, u_ref, sz_ref):
     comps, y_own, z_own = a_ref.shape[:3]
     left = left_half((y_own, z_own, LANES))
     for j in range(comps):
-        for t in range(2):
-            a = a_ref[j, :, :, pl.ds(t * LANES, LANES)]
-            u = u_ref[j, :, :, pl.ds(t * LANES, LANES)].astype(jnp.float32)
-            for h in range(2):
-                q = 2 * t + h
-                pair = jnp.where(left, a, swap(u)) if h == 0 else jnp.where(left, swap(a), u)
-                for group in range(4):
-                    sz_ref[group * 4 + q, pl.ds(3 * j, 3)] = pair[3 * group : 3 * group + 3].astype(jnp.bfloat16)
-                for y in range(y_own):
-                    stage[pl.ds(q * PITCH + j * y_own + y, z_own, stride=4 * PITCH), :] = pair[y]
+        for q in range(4):
+            pair = pair_up(a_ref, u_ref, j, q // 2, q % 2, left).astype(jnp.bfloat16)
+            for group in range(4):
+                sz_ref[group * 4 + q, pl.ds(3 * j, 3)] = pair[3 * group : 3 * group + 3]
+
+
+def pack_y_kernel(a_ref, u_ref, sy_ref, stage):
+    comps, y_own, z_own = a_ref.shape[:3]
+    left = left_half((y_own, z_own, LANES))
+    for j in range(comps):
+        for q in range(4):
+            pair = pair_up(a_ref, u_ref, j, q // 2, q % 2, left)
+            for y in range(y_own):
+                stage[pl.ds(q * PITCH + j * y_own + y, z_own, stride=4 * PITCH), :] = pair[y]
     rows = comps * y_own
     for p in range(4 * z_own):
         sy_ref[p] = stage[pl.ds(p * PITCH, rows), :].astype(jnp.bfloat16)
 
 
-def x_kernel(a_ref, u_ref, px_ref, out_ref):
+def spread(even, odd, even_last, odd_last, left):
+    return (
+        jnp.where(left, even, swap(odd)),
+        jnp.where(left, swap(even), odd),
+        jnp.where(left, even_last, swap(odd_last)),
+    )
+
+
+def x_kernel(a_ref, u_ref, px_ref, rz_ref, out_ref):
     comps, y_own, z_own, length = a_ref.shape
     rows = y_own * z_own
     px = px_ref[...]
@@ -63,6 +82,22 @@
         if c == 0:
             term = term - transfer
         out_ref[c] = (adjoint[part] + section_step * term).reshape(y_own, z_own, length)
+    left = left_half((z_own, LANES))
+
+    def z_piece(q, y, m):
+        return rz_ref[(y // 3) * 4 + q, m].astype(jnp.float32)
+
+    for y in range(y_own):
+        w = y % 3
+        for t in range(2):
+            at = pl.ds(t * LANES, LANES)
+            even, odd = z_piece(2 * t, y, w), z_piece(2 * t + 1, y, w)
+            even_last, odd_last = z_piece(2 * t, y, 3 + w // 2), z_piece(2 * t + 1, y, 3 + w // 2)
+            if w == 1:
+                even_last, odd_last = swap(even_last), swap(odd_last)
+            sums = spread(even, odd, even_last, odd_last, left)
+            for c in range(comps):
+                out_ref[c, y, :, at] += section_step * sums[c]
 
 
 def z_kernel(rz_ref, pz_ref, oz_ref, result):
@@ -123,7 +158,7 @@
     oy_ref[...] = back[...].reshape(peers, 2 * y_own, LANES).astype(jnp.bfloat16)
 
 
-def final_kernel(base_ref, rz_ref, ry_ref, out_ref, stage):
+def final_kernel(base_ref, ry_ref, out_ref, stage):
     comps, y_own, z_own, _ = base_ref.shape
     left = left_half((z_own, LANES))
     pitch = 2 * y_own
@@ -132,24 +167,11 @@
     def y_piece(q, h, y):
         return stage[pl.ds(q * pitch + h * y_own + y, z_own, stride=4 * pitch), :]
 
-    def z_piece(q, y, m):
-        return rz_ref[(y // 3) * 4 + q, m].astype(jnp.float32)
-
     for y in range(y_own):
-        w = y % 3
         for t in range(2):
             at = pl.ds(t * LANES, LANES)
-            even = y_piece(2 * t, 0, y) + z_piece(2 * t, y, w)
-            odd = y_piece(2 * t + 1, 0, y) + z_piece(2 * t + 1, y, w)
-            even_last, odd_last = z_piece(2 * t, y, 3 + w // 2), z_piece(2 * t + 1, y, 3 + w // 2)
-            if w == 1:
-                even_last, odd_last = swap(even_last), swap(odd_last)
-            even_last = even_last + y_piece(2 * t, 1, y)
-            odd_last = odd_last + y_piece(2 * t + 1, 1, y)
-            sums = (
-                jnp.where(left, even, swap(odd)),
-                jnp.where(left, swap(even), odd),
-                jnp.where(left, even_last, swap(odd_last)),
+            sums = spread(
+                y_piece(2 * t, 0, y), y_piece(2 * t + 1, 0, y), y_piece(2 * t, 1, y), y_piece(2 * t + 1, 1, y), left
             )
             for c in range(comps):
                 out_ref[c, y, :, at] = base_ref[c, y, :, at] + section_step * sums[c]
@@ -167,28 +189,27 @@
     shape = jax.ShapeDtypeStruct
     exchange = functools.partial(lax.all_to_all, split_axis=0, concat_axis=0, tiled=True)
 
-    send_z, send_y = pl.pallas_call(
-        pack_kernel,
-        name="pack",
-        out_shape=(
-            shape((cols, 3 * comps, z_own, LANES), bf16),
-            shape((rows, comps * y_own, LANES), bf16),
-        ),
+    near = functools.partial(pltpu.with_memory_space_constraint, memory_space=pltpu.VMEM)
+
+    send_z = pl.pallas_call(
+        pack_z_kernel, name="pack_z", out_shape=shape((cols, 3 * comps, z_own, LANES), bf16)
+    )(a, u)
+    send_y = pl.pallas_call(
+        pack_y_kernel,
+        name="pack_y",
+        out_shape=shape((rows, comps * y_own, LANES), bf16),
         scratch_shapes=[pltpu.VMEM((rows * PITCH, LANES), f32)],
     )(a, u)
     with jax.named_scope("z_out"):
         recv_z = exchange(send_z, "cols")
     with jax.named_scope("y_out"):
         recv_y = exchange(send_y, "rows")
-    base = pl.pallas_call(
-        x_kernel, name="x_terms", out_shape=shape(a.shape, f32)
-    )(a, u, stream_pair)
     terms_z = pl.pallas_call(
         z_kernel,
         name="z_terms",
         out_shape=shape((cols, 5, z_own, LANES), bf16),
         scratch_shapes=[pltpu.VMEM((2 * length_z, 3 * comps * LANES), f32)],
-    )(recv_z, span_pair)
+    )(near(recv_z), span_pair)
     with jax.named_scope("z_back"):
         back_z = exchange(terms_z, "cols")
     terms_y = pl.pallas_call(
@@ -202,15 +223,18 @@
             pltpu.VMEM((2, length_y, LANES), f32),
             pltpu.VMEM((rows * 2 * y_own, LANES), f32),
         ],
-    )(recv_y, normal_pair)
+    )(near(recv_y), normal_pair)
     with jax.named_scope("y_back"):
         back_y = exchange(terms_y, "rows")
+    base = pl.pallas_call(x_kernel, name="x_terms", out_shape=pltpu.VMEM(a.shape, f32))(
+        a, u, stream_pair, near(back_z)
+    )
     out = pl.pallas_call(
         final_kernel,
         name="final",
         out_shape=shape(a.shape, f32),
         scratch_shapes=[pltpu.VMEM((rows * 2 * y_own, LANES), f32)],
-    )(base, back_z, back_y)
+    )(near(base), near(back_y))
     return out.transpose(0, 2, 1, 3)
 
 

time: 78 us -> 75.1 us (0.963)
  blocking collectives: 18.4 us -> 0 us
  starting transfers between devices: 22.9 us -> 33.6 us
  waiting for transfers between devices: 23.1 us -> 29.3 us
  local copies, waits for them, and re-layouts: 1.33 us -> 0 us
    all_to_all x1 -> x0, blocking collectives: 18.4 us -> none  [local(): recv_z = exchange(send_z, 'cols')]
    all_to_all x0 -> x1, starting transfers between devices: none -> 10.2 us  [local(): recv_z = exchange(send_z, 'cols')]
    all_to_all x0 -> x1, waiting for transfers between devices: none -> 5.31 us  [local(): recv_z = exchange(send_z, 'cols')]
    unnamed x6 -> x0, local copies, waits for them, and re-layouts: 1.33 us -> none
    pallas_call x1, Pallas kernels: 2.09 us -> 0.98 us  [local(): pl.pallas_call(final_kernel, name='final', out_shape=shape(a.shape, f32),...]
    pallas_call x2 -> x3, Pallas kernels: 4.47 us -> 5.52 us  [the longest x1 2.21 us: local(): pl.pallas_call(pack_y_kernel, name='pack_y', out_shape=shape((rows, comps...]
  transfers between devices with their start and end apart: 3 -> 4, of which waited for: 3 -> 4; matrix products, arithmetic and copies ran while one was open for 0% -> 0% of each run, Pallas kernels for 9% -> 11%
where the time goes in v2:
time: 75.1 us; the launch traced here: 74 us
  starting transfers between devices  33.6 us (45%)
  waiting for transfers between devices  29.3 us (39%)
  Pallas kernels  11 us (15%)
    all_to_all x1, starting transfers between devices, local(): recv_y = exchange(send_y, 'rows')  11.4 us
    all_to_all x1, starting transfers between devices, local(): recv_z = exchange(send_z, 'cols')  10.2 us
    all_to_all x1, waiting for transfers between devices, local(): recv_y = exchange(send_y, 'rows')  10.2 us
    all_to_all x1, waiting for transfers between devices, local(): back_y = exchange(terms_y, 'rows')  10 us
    all_to_all x1, starting transfers between devices, local(): back_z = exchange(terms_z, 'cols')  7.24 us
    all_to_all x1, waiting for transfers between devices, local(): recv_z = exchange(send_z, 'cols')  5.31 us
    all_to_all x1, starting transfers between devices, local(): back_y = exchange(terms_y, 'rows')  4.85 us
    all_to_all x1, waiting for transfers between devices, local(): back_z = exchange(terms_z, 'cols')  3.83 us
  transfers between devices with their start and end apart: 4, of which 4 were waited for; matrix products, arithmetic and copies ran while one was open for 0% of the time, Pallas kernels for 11%

profile of v2, /device:TPU:1, one launch (start us, length us, event | category | flops | bytes accessed | tf_op | source)
XLA Modules:
  0.0 74.0 jit_solution(3408130844025256729)
XLA Ops:
  0.0 1.9 %pack_z.1 = bf16[16,9,8,128]{3,2,1,0:T(8,128)(2,1)} custom-call(f32[3,12,8,256]{3,2,1,0:T(8,128)} %bitcast.3, bf16[3,12,8,256]{3,2,1,0:T(8,128)(2,1)} %bitcast.6), custom_call_target="tpu_custom_call" | custom-call | tf_op jit(solution)/shard_map/pack_z/pallas_call | solution.py:194
  1.9 10.2 %all-to-all-start = ((bf16[16,9,8,128]{3,2,1,0:T(8,128)(2,1)}), bf16[16,9,8,128]{3,2,1,0:T(8,128)(2,1)S(1)}, u32[]{:S(2)}, u32[]{:S(2)}) async-start(bf16[16,9,8,128]{3,2,1,0:T(8,128)(2,1)} %pack_z.1), calls=%async_computation | async-start | bytes 589824 | tf_op jit(solution)/shard_map/z_out/all_to_all | solution.py:204
  12.0 2.2 %pack_y.1 = bf16[32,36,128]{2,1,0:T(8,128)(2,1)} custom-call(f32[3,12,8,256]{3,2,1,0:T(8,128)} %bitcast.4, bf16[3,12,8,256]{3,2,1,0:T(8,128)(2,1)} %bitcast.7), custom_call_target="tpu_custom_call" | custom-call | tf_op jit(solution)/shard_map/pack_y/pallas_call | solution.py:197
  14.2 5.3 %all-to-all-done.rz_ref = bf16[16,9,8,128]{3,2,1,0:T(8,128)(2,1)S(1)} async-done(((bf16[16,9,8,128]{3,2,1,0:T(8,128)(2,1)}), bf16[16,9,8,128]{3,2,1,0:T(8,128)(2,1)S(1)}, u32[]{:S(2)}, u32[]{:S(2)}) %all-to-all-start) | async-done | bytes 294944 | tf_op jit(solution)/shard_map/z_out/all_to_all | solution.py:204
  19.5 11.4 %all-to-all-start.2 = ((bf16[32,36,128]{2,1,0:T(8,128)(2,1)}), bf16[32,36,128]{2,1,0:T(8,128)(2,1)S(1)}, u32[]{:S(2)}, u32[]{:S(2)}) async-start(bf16[32,36,128]{2,1,0:T(8,128)(2,1)} %pack_y.1), calls=%async_computation.2 | async-start | bytes 655360 | tf_op jit(solution)/shard_map/y_out/all_to_all | solution.py:206
  30.9 2.0 %z_terms.1 = bf16[16,5,8,128]{3,2,1,0:T(8,128)(2,1)} custom-call(bf16[16,9,8,128]{3,2,1,0:T(8,128)(2,1)S(1)} %all-to-all-done.rz_ref, bf16[256,128]{1,0:T(8,128)(2,1)} %pz_ref.1), custom_call_target="tpu_custom_call" | custom-call | tf_op jit(solution)/shard_map/z_terms/pallas_call | solution.py:207
  32.9 10.2 %all-to-all-done.2.ry_ref = bf16[32,36,128]{2,1,0:T(8,128)(2,1)S(1)} async-done(((bf16[32,36,128]{2,1,0:T(8,128)(2,1)}), bf16[32,36,128]{2,1,0:T(8,128)(2,1)S(1)}, u32[]{:S(2)}, u32[]{:S(2)}) %all-to-all-start.2) | async-done | bytes 294944 | tf_op jit(solution)/shard_map/y_out/all_to_all | solution.py:206
  43.0 7.2 %all-to-all-start.1 = ((bf16[16,5,8,128]{3,2,1,0:T(8,128)(2,1)}), bf16[16,5,8,128]{3,2,1,0:T(8,128)(2,1)S(1)}, u32[]{:S(2)}, u32[]{:S(2)}) async-start(bf16[16,5,8,128]{3,2,1,0:T(8,128)(2,1)} %z_terms.1), calls=%async_computation.1 | async-start | bytes 327680 | tf_op jit(solution)/shard_map/z_back/all_to_all | solution.py:214
  50.3 2.6 %y_terms.1 = bf16[32,24,128]{2,1,0:T(8,128)(2,1)} custom-call(bf16[32,36,128]{2,1,0:T(8,128)(2,1)S(1)} %all-to-all-done.2.ry_ref, bf16[768,384]{1,0:T(8,128)(2,1)} %py_ref.1), custom_call_target="tpu_custom_call" | custom-call | tf_op jit(solution)/shard_map/y_terms/pallas_call | solution.py:215
  52.9 3.8 %all-to-all-done.1.rz_ref = bf16[16,5,8,128]{3,2,1,0:T(8,128)(2,1)S(1)} async-done(((bf16[16,5,8,128]{3,2,1,0:T(8,128)(2,1)}), bf16[16,5,8,128]{3,2,1,0:T(8,128)(2,1)S(1)}, u32[]{:S(2)}, u32[]{:S(2)}) %all-to-all-start.1) | async-done | bytes 163872 | tf_op jit(solution)/shard_map/z_back/all_to_all | solution.py:214
  56.7 4.8 %all-to-all-start.3 = ((bf16[32,24,128]{2,1,0:T(8,128)(2,1)}), bf16[32,24,128]{2,1,0:T(8,128)(2,1)S(1)}, u32[]{:S(2)}, u32[]{:S(2)}) async-start(bf16[32,24,128]{2,1,0:T(8,128)(2,1)} %y_terms.1), calls=%async_computation.3 | async-start | bytes 393216 | tf_op jit(solution)/shard_map/y_back/all_to_all | solution.py:228
  61.6 1.5 %x_terms.1.base_ref = f32[3,12,8,256]{3,2,1,0:T(8,128)S(1)} custom-call(f32[3,12,8,256]{3,2,1,0:T(8,128)} %bitcast.5, bf16[3,12,8,256]{3,2,1,0:T(8,128)(2,1)} %bitcast.8, bf16[512,256]{1,0:T(8,128)(2,1)} %px_ref.1, bf16[16,5,8,128]{3,2,1,0:T(8,128)(2,1)S(1)} %all-to-all-done.1.rz_ref), custom_call_target="tpu_custom_call" | custom-call | tf_op jit(solution)/shard_map/x_terms/pallas_call | solution.py:229
  63.0 10.0 %all-to-all-done.3.ry_ref = bf16[32,24,128]{2,1,0:T(8,128)(2,1)S(1)} async-done(((bf16[32,24,128]{2,1,0:T(8,128)(2,1)}), bf16[32,24,128]{2,1,0:T(8,128)(2,1)S(1)}, u32[]{:S(2)}, u32[]{:S(2)}) %all-to-all-start.3) | async-done | bytes 196640 | tf_op jit(solution)/shard_map/y_back/all_to_all | solution.py:228
  73.1 1.0 %final.1 = f32[3,12,8,256]{3,2,1,0:T(8,128)} custom-call(f32[3,12,8,256]{3,2,1,0:T(8,128)S(1)} %x_terms.1.base_ref, bf16[32,24,128]{2,1,0:T(8,128)(2,1)S(1)} %all-to-all-done.3.ry_ref), custom_call_target="tpu_custom_call" | custom-call | tf_op jit(solution)/shard_map/final/pallas_call | solution.py:232
Async XLA Ops:
  1.9 17.7 %all-to-all-start = ((bf16[16,9,8,128]{3,2,1,0:T(8,128)(2,1)}), bf16[16,9,8,128]{3,2,1,0:T(8,128)(2,1)S(1)}, u32[]{:S(2)}, u32[]{:S(2)}) async-start(bf16[16,9,8,128]{3,2,1,0:T(8,128)(2,1)} %pack_z.1), calls=%async_computation | async-start | bytes 589824 | tf_op jit(solution)/shard_map/z_out/all_to_all | solution.py:204
  19.5 23.5 %all-to-all-start.2 = ((bf16[32,36,128]{2,1,0:T(8,128)(2,1)}), bf16[32,36,128]{2,1,0:T(8,128)(2,1)S(1)}, u32[]{:S(2)}, u32[]{:S(2)}) async-start(bf16[32,36,128]{2,1,0:T(8,128)(2,1)} %pack_y.1), calls=%async_computation.2 | async-start | bytes 655360 | tf_op jit(solution)/shard_map/y_out/all_to_all | solution.py:206
  43.0 13.7 %all-to-all-start.1 = ((bf16[16,5,8,128]{3,2,1,0:T(8,128)(2,1)}), bf16[16,5,8,128]{3,2,1,0:T(8,128)(2,1)S(1)}, u32[]{:S(2)}, u32[]{:S(2)}) async-start(bf16[16,5,8,128]{3,2,1,0:T(8,128)(2,1)} %z_terms.1), calls=%async_computation.1 | async-start | bytes 327680 | tf_op jit(solution)/shard_map/z_back/all_to_all | solution.py:214
  56.7 16.4 %all-to-all-start.3 = ((bf16[32,24,128]{2,1,0:T(8,128)(2,1)}), bf16[32,24,128]{2,1,0:T(8,128)(2,1)S(1)}, u32[]{:S(2)}, u32[]{:S(2)}) async-start(bf16[32,24,128]{2,1,0:T(8,128)(2,1)} %y_terms.1), calls=%async_computation.3 | async-start | bytes 393216 | tf_op jit(solution)/shard_map/y_back/all_to_all | solution.py:228

commit v3 on v0

v3 whole, which is shorter than its diff:
```python
import functools

import jax
import jax.numpy as jnp
from jax import lax
from jax.experimental import pallas as pl
from jax.experimental.pallas import tpu as pltpu
from jax.sharding import PartitionSpec as P

viscosity = 0.5
section_step = 0.5
LANES = 128
BACK = 40


def fields(a_ref, u_ref, f, half):
    at = pl.ds(half * LANES, LANES)
    if f < 3:
        return a_ref[f, :, :, at]
    return u_ref[f - 3, :, :, at].astype(jnp.float32)


def pack_y(a_ref, u_ref, out_ref, stage):
    y_own, z_own = a_ref.shape[1:3]
    rows = 6 * y_own
    for f in range(6):
        for half in range(2):
            value = fields(a_ref, u_ref, f, half)
            for y in range(y_own):
                stage[pl.ds(half * rows + f * y_own + y, z_own, stride=2 * rows), :] = value[y]
    out_ref[...] = stage[...].reshape(2 * z_own, rows, LANES).astype(jnp.bfloat16)


def pack_z(a_ref, u_ref, out_ref):
    y_own, z_own = a_ref.shape[1:3]
    for f in range(6):
        for half in range(2):
            value = fields(a_ref, u_ref, f, half).astype(jnp.bfloat16)
            for y in range(y_own):
                row = ((y // 3 * 2 + half) * 18 + f * 3 + y % 3) * z_own
                out_ref[row // 72, pl.ds(row % 72, z_own), :] = value[y]


def pack_kernel(y_core, a_ref, u_ref, out_ref, stage):
    is_y = lax.axis_index("cols") % 2 == y_core

    @pl.when(is_y)
    def _():
        pack_y(a_ref, u_ref, out_ref, stage)

    @pl.when(jnp.logical_not(is_y))
    def _():
        pack_z(a_ref, u_ref, out_ref)


def x_kernel(a_ref, u_ref, px_ref, out_ref):
    comps, y_own, z_own, length = a_ref.shape
    rows = y_own * z_own
    px = px_ref[...]
    dims = (((1,), (1,)), ((), ()))
    adjoint = a_ref[...].reshape(comps * rows, length)
    a_b = adjoint.astype(jnp.bfloat16)
    u_f = u_ref[...].astype(jnp.float32).reshape(comps * rows, length)
    derivs = lax.dot_general(a_b, px, dims, preferred_element_type=jnp.float32)
    base_deriv = lax.dot_general(
        u_f.astype(jnp.bfloat16), px[:length], dims, preferred_element_type=jnp.float32
    )
    products = a_b.astype(jnp.float32) * base_deriv
    transfer = products[:rows] + products[rows : 2 * rows] + products[2 * rows :]
    u_dir = u_f[:rows]
    for c in range(comps):
        part = slice(c * rows, (c + 1) * rows)
        term = u_dir * derivs[part, :length] + viscosity * derivs[part, length:]
        if c == 0:
            term = term - transfer
        out_ref[c] = (adjoint[part] + section_step * term).reshape(y_own, z_own, length)


def z_kernel(rz_ref, pz_ref, oz_ref, derivs, base_derivs):
    chips, _, slabs, z_own = rz_ref.shape[:4]
    length = chips * 2 * z_own
    lines = [rz_ref[:, :, k].astype(jnp.float32).reshape(length, LANES) for k in range(slabs)]
    packed = [v.astype(jnp.bfloat16) for v in lines]
    pz = pz_ref[...]
    derivs[...] = jnp.dot(pz, jnp.concatenate(packed[:9], axis=1), preferred_element_type=jnp.float32)
    base_derivs[...] = jnp.dot(
        pz[:length], jnp.concatenate(packed[9:], axis=1), preferred_element_type=jnp.float32
    )
    for y in range(3):
        at = [pl.ds((3 * j + y) * LANES, LANES) for j in range(3)]
        u_dir = lines[9 + 3 * 2 + y]
        transfer = sum(lines[3 * j + y] * base_derivs[:, at[j]] for j in range(3))
        for c in range(3):
            term = u_dir * derivs[:length, at[c]] + viscosity * derivs[length:, at[c]]
            if c == 2:
                term = term - transfer
            oz_ref[:, :, 3 * c + y] = term.reshape(chips, 2, z_own, LANES).astype(jnp.bfloat16)


def y_kernel(ry_ref, py_ref, oy_ref, stage, lines, derivs, base_derivs, terms, back):
    peers, rows = ry_ref.shape[:2]
    y_own = rows // 6
    length = peers * y_own
    stage[...] = ry_ref[...].astype(jnp.float32).reshape(stage.shape)
    for f in range(6):
        for y in range(y_own):
            for g in range(peers // 8):
                lines[f, pl.ds(8 * g * y_own + y, 8, stride=y_own), :] = stage[
                    pl.ds(8 * g * rows + f * y_own + y, 8, stride=rows), :
                ]
    packed = [lines[f].astype(jnp.bfloat16) for f in range(6)]
    derivs[...] = jnp.dot(
        py_ref[...], jnp.concatenate(packed[:3], axis=1), preferred_element_type=jnp.float32
    )
    base_derivs[...] = jnp.dot(
        py_ref[pl.ds(0, length), :], jnp.concatenate(packed[3:], axis=1), preferred_element_type=jnp.float32
    )
    block = 48
    for b in range(length // block):
        at = pl.ds(b * block, block)
        lane = [pl.ds(j * LANES, LANES) for j in range(3)]
        u_dir = lines[4, at, :]
        transfer = sum(lines[j, at, :] * base_derivs[at, lane[j]] for j in range(3))
        for c in range(3):
            term = u_dir * derivs[at, lane[c]] + viscosity * derivs[pl.ds(length + b * block, block), lane[c]]
            if c == 1:
                term = term - transfer
            terms[c, at, :] = term
    for c in range(3):
        for y in range(y_own):
            for g in range(peers // 8):
                back[pl.ds(8 * g * BACK + c * y_own + y, 8, stride=BACK), :] = terms[
                    c, pl.ds(8 * g * y_own + y, 8, stride=y_own), :
                ]
    for p in range(peers):
        used = 3 * y_own
        back[pl.ds(p * BACK + used, BACK - used), :] = jnp.zeros((BACK - used, LANES), jnp.float32)
    oy_ref[...] = back[...].reshape(peers, BACK, LANES).astype(jnp.bfloat16)


def order_kernel(rz_ref, out_ref):
    pieces, _, slabs, z_own = rz_ref.shape[:4]
    for side in range(2):
        for p in range(pieces):
            for k in range(slabs):
                row = (p * slabs + k) * z_own
                out_ref[16 * side + row // BACK, pl.ds(row % BACK, z_own), :] = rz_ref[p, 1 - side, k]
        for row in range(pieces * slabs * z_own, 16 * BACK, z_own):
            out_ref[16 * side + row // BACK, pl.ds(row % BACK, z_own), :] = jnp.zeros((z_own, LANES), jnp.bfloat16)


def add_kernel(y_core, base_ref, part_ref, out_ref, stage):
    comps, y_own, z_own, _ = base_ref.shape
    is_y = lax.axis_index("cols") % 2 == y_core

    @pl.when(is_y)
    def _():
        stage[...] = part_ref[pl.ds(0, 16)].astype(jnp.float32).reshape(stage.shape)
        for c in range(comps):
            for y in range(y_own):
                for half in range(2):
                    at = pl.ds(half * LANES, LANES)
                    piece = stage[pl.ds(half * BACK + c * y_own + y, z_own, stride=2 * BACK), :]
                    out_ref[c, y, :, at] = base_ref[c, y, :, at] + section_step * piece

    @pl.when(jnp.logical_not(is_y))
    def _():
        for c in range(comps):
            for y in range(y_own):
                for half in range(2):
                    at = pl.ds(half * LANES, LANES)
                    row = ((y // 3 * 2 + half) * 9 + c * 3 + y % 3) * z_own
                    piece = part_ref[row // BACK, pl.ds(row % BACK, z_own), :].astype(jnp.float32)
                    out_ref[c, y, :, at] = base_ref[c, y, :, at] + section_step * piece


def local(adjoint, base_flow, stream_pair, normal_pair, span_pair):
    f32, bf16 = jnp.float32, jnp.bfloat16
    rows = lax.axis_size("rows")
    cols = lax.axis_size("cols")
    chips = cols // 2
    _, z_own, y_own, length_x = adjoint.shape
    length_y = rows * y_own
    length_z = cols * z_own
    a = adjoint.transpose(0, 2, 1, 3)
    u = base_flow.transpose(0, 2, 1, 3)
    shape = jax.ShapeDtypeStruct
    near = functools.partial(pltpu.with_memory_space_constraint, memory_space=pltpu.VMEM)
    exchange = functools.partial(lax.all_to_all, split_axis=0, concat_axis=0, tiled=True)
    partner = [(i, i ^ 1) for i in range(cols)]
    alike = [list(range(core, cols, 2)) for core in range(2)]

    def pack(y_core, name):
        return pl.pallas_call(
            functools.partial(pack_kernel, y_core),
            name=name,
            out_shape=shape((2 * z_own, 6 * y_own, LANES), bf16),
            scratch_shapes=[pltpu.VMEM((2 * z_own * 6 * y_own, LANES), f32)],
        )(a, u)

    def x_terms():
        return pl.pallas_call(x_kernel, name="x_terms", out_shape=shape(a.shape, f32))(a, u, stream_pair)

    def add(y_core, name, base, part, near_base):
        return pl.pallas_call(
            functools.partial(add_kernel, y_core),
            name=name,
            out_shape=near_base(a.shape, f32),
            scratch_shapes=[pltpu.VMEM((16 * BACK, LANES), f32)],
        )(base, near(part))

    def along_y(keep, recv):
        base = x_terms()
        lines = exchange(jnp.concatenate([keep, recv], axis=0), "rows")
        terms = pl.pallas_call(
            y_kernel,
            name="y_terms",
            out_shape=shape((rows, BACK, LANES), bf16),
            scratch_shapes=[
                pltpu.VMEM((rows * 6 * y_own, LANES), f32),
                pltpu.VMEM((6, length_y, LANES), f32),
                pltpu.VMEM((2 * length_y, 3 * LANES), f32),
                pltpu.VMEM((length_y, 3 * LANES), f32),
                pltpu.VMEM((3, length_y, LANES), f32),
                pltpu.VMEM((rows * BACK, LANES), f32),
            ],
        )(near(lines), normal_pair)
        return exchange(terms, "rows"), base

    def along_z(keep, recv):
        base = x_terms()
        pair = [part.reshape(chips, 1, 18, z_own, LANES) for part in (recv, keep)]
        lines = exchange(jnp.concatenate(pair, axis=1), "cols", axis_index_groups=alike)
        terms = pl.pallas_call(
            z_kernel,
            name="z_terms",
            out_shape=shape((chips, 2, 9, z_own, LANES), bf16),
            scratch_shapes=[
                pltpu.VMEM((2 * length_z, 9 * LANES), f32),
                pltpu.VMEM((length_z, 9 * LANES), f32),
            ],
        )(lines, span_pair)
        back = exchange(terms, "cols", axis_index_groups=alike)
        ordered = pl.pallas_call(
            order_kernel, name="order_z", out_shape=shape((rows, BACK, LANES), bf16)
        )(back)
        return ordered, base

    core = lax.axis_index("cols") % 2
    recv = lax.ppermute(pack(1, "pack_send"), "cols", partner)
    keep = pack(0, "pack_keep")
    both, base = lax.cond(core == 0, along_y, along_z, keep, recv)
    other = lax.ppermute(both[rows // 2 :], "cols", partner)
    base = add(0, "add_own", base, both, pltpu.VMEM)
    out = add(1, "add_other", near(base), other, shape)
    return out.transpose(0, 2, 1, 3)


def solution(mesh):
    placed = (P(None, "cols", "rows", None), P(None, "cols", "rows", None), P(), P(), P())
    return jax.shard_map(
        local, mesh=mesh, in_specs=placed, out_specs=P(None, "cols", "rows", None), check_vma=False
    )
```

time: 153 us -> 64.5 us (0.42)
  the two profiles are of different devices: /device:TPU:8 before, /device:TPU:1 now
where the time goes in v3:
time: 64.5 us; the launch traced here: 64.1 us
  starting transfers between devices  34.8 us (54%)
  blocking collectives  11.1 us (17%)
  waiting for transfers between devices  8.17 us (13%)
  Pallas kernels  8.14 us (13%)
  local copies, waits for them, and re-layouts  1.67 us (3%)
    ppermute x1, starting transfers between devices, local(): other = lax.ppermute(both[rows // 2:], 'cols', partner)  22.8 us
    all_to_all x1, blocking collectives, along_z(): exchange(jnp.concatenate(pair, axis=1), 'cols', axis_index_groups=alike)  11.1 us
    ppermute x1, starting transfers between devices, local(): recv = lax.ppermute(pack(1, 'pack_send'), 'cols', partner)  8.58 us
    all_to_all x1, waiting for transfers between devices, along_z(): back = exchange(terms, 'cols', axis_index_groups=alike)  6.9 us
    all_to_all x1, starting transfers between devices, along_z(): back = exchange(terms, 'cols', axis_index_groups=alike)  3.42 us
    pallas_call x1, Pallas kernels, along_z(): pl.pallas_call(z_kernel, name='z_terms', out_shape=shape((chips, 2, 9, z_...  2.18 us
    pallas_call x2, Pallas kernels, pack(): pl.pallas_call(functools.partial(pack_kernel, y_core), name=name, out_sha...  2.05 us
    pallas_call x2, Pallas kernels, add(): pl.pallas_call(functools.partial(add_kernel, y_core), name=name, out_shap...  1.86 us
  transfers between devices with their start and end apart: 3, of which 2 were waited for; matrix products, arithmetic and copies ran while one was open for 0% of the time, Pallas kernels for 2%

profile of v3, /device:TPU:1, one launch (start us, length us, event | category | flops | bytes accessed | tf_op | source)
XLA Modules:
  0.0 64.1 jit_solution(1389975625921381023)
XLA Ops:
  0.0 2.0 %pack_send.1 = bf16[16,72,128]{2,1,0:T(8,128)(2,1)} custom-call(f32[3,12,8,256]{3,2,1,0:T(8,128)} %bitcast.5, bf16[3,12,8,256]{3,2,1,0:T(8,128)(2,1)} %bitcast.10), custom_call_target="tpu_custom_call" | custom-call | tf_op jit(solution)/shard_map/pack_send/pallas_call | solution.py:194
  2.0 8.6 %collective-permute-start = (bf16[16,72,128]{2,1,0:T(8,128)(2,1)}, bf16[16,72,128]{2,1,0:T(8,128)(2,1)S(1)}, u32[]{:S(2)}, u32[]{:S(2)}) collective-permute-start(bf16[16,72,128]{2,1,0:T(8,128)(2,1)} %pack_send.1), channel_id=1, source_target_pairs={{0,1},{1,0},{2,3},{3,2},{4,5},{5,4},{6,7},{7,6},{8,9},{9,8},{10,11... | collective-permute-start | bytes 884744 | tf_op jit(solution)/shard_map/ppermute | solution.py:250
  10.6 0.0 copy-done
  10.6 0.0 copy-done.1
  10.6 0.0 copy-start.3
  10.6 0.0 copy-start.5
  10.6 0.1 pack_keep.1
  10.7 1.3 %collective-permute-done = bf16[16,72,128]{2,1,0:T(8,128)(2,1)S(1)} collective-permute-done((bf16[16,72,128]{2,1,0:T(8,128)(2,1)}, bf16[16,72,128]{2,1,0:T(8,128)(2,1)S(1)}, u32[]{:S(2)}, u32[]{:S(2)}) %collective-permute-start) | collective-permute-done | bytes 294944 | tf_op jit(solution)/shard_map/ppermute | solution.py:250
  12.0 0.0 copy-done.4
  12.0 0.0 copy-done.3
  12.0 26.4 %conditional.1 = (bf16[32,40,128]{2,1,0:T(8,128)(2,1)}, f32[3,12,8,256]{3,2,1,0:T(8,128)S(1)}) conditional(s32[]{:T(128)} %convert_element_type.3, (bf16[16,72,128]{2,1,0:T(8,128)(2,1)S(1)}, bf16[16,72,128]{2,1,0:T(8,128)(2,1)S(1)}, bf16[256,128]{1,0:T(8,128)(2,1)S(1)}, f32[3,12,8,256]{3,2,1,0:T(8,128)S(1)}, bf16[3,12,8,256]{3,2,1,0:T(8,128)(2,1)S(1)}, ...), branch_computations={%region_0.1_spmd, %region_1.2_spmd} | conditional | flops 294912 | bytes 4423756 | solution.py:252
  12.0 0.1 pad_maximum_fusion
  12.1 11.1 %all_to_all.16.rz_ref = bf16[8,2,18,8,128]{4,3,2,1,0:T(8,128)(2,1)} all-to-all(bf16[8,2,18,8,128]{4,3,2,1,0:T(8,128)(2,1)S(1)} %pad_maximum_fusion), channel_id=1, replica_groups={{0,2,4,6,8,10,12,14},{1,3,5,7,9,11,13,15},{16,18,20,22,24,26,28,30},{17..., dimensions={0} | all-to-all | bytes 1179648 | tf_op jit(solution)/shard_map/cond/branch_0_fun/all_to_all | solution.py:233
  23.1 2.2 %z_terms.1 = bf16[8,2,9,8,128]{4,3,2,1,0:T(8,128)(2,1)} custom-call(bf16[8,2,18,8,128]{4,3,2,1,0:T(8,128)(2,1)} %all_to_all.16.rz_ref, bf16[256,128]{1,0:T(8,128)(2,1)S(1)} %get-tuple-element.46.pz_ref), custom_call_target="tpu_custom_call" | custom-call | tf_op jit(solution)/shard_map/cond/branch_0_fun/z_terms/pallas_call | solution.py:234
  25.3 3.4 %all-to-all-start.1 = ((bf16[8,2,9,8,128]{4,3,2,1,0:T(8,128)(2,1)}), bf16[8,2,9,8,128]{4,3,2,1,0:T(8,128)(2,1)S(1)}, u32[]{:S(2)}, u32[]{:S(2)}) async-start(bf16[8,2,9,8,128]{4,3,2,1,0:T(8,128)(2,1)} %z_terms.1), calls=%async_computation.1 | async-start | bytes 589824 | tf_op jit(solution)/shard_map/cond/branch_0_fun/all_to_all | solution.py:243
  28.7 0.3 x_terms.2
  29.1 6.9 %all-to-all-done.1.rz_ref = bf16[8,2,9,8,128]{4,3,2,1,0:T(8,128)(2,1)S(1)} async-done(((bf16[8,2,9,8,128]{4,3,2,1,0:T(8,128)(2,1)}), bf16[8,2,9,8,128]{4,3,2,1,0:T(8,128)(2,1)S(1)}, u32[]{:S(2)}, u32[]{:S(2)}) %all-to-all-start.1) | async-done | bytes 294944 | tf_op jit(solution)/shard_map/cond/branch_0_fun/all_to_all | solution.py:243
  36.0 0.7 %copy-done.2 = bf16[8,2,9,8,128]{4,3,2,1,0:T(8,128)(2,1)} copy-done((bf16[8,2,9,8,128]{4,3,2,1,0:T(8,128)(2,1)}, bf16[8,2,9,8,128]{4,3,2,1,0:T(8,128)(2,1)S(1)}, u32[]{:S(2)}) %copy-start.2) | copy-done | bytes 294936 | tf_op jit(solution)/shard_map/cond
  36.7 1.7 %order_z.1 = bf16[32,40,128]{2,1,0:T(8,128)(2,1)} custom-call(bf16[8,2,9,8,128]{4,3,2,1,0:T(8,128)(2,1)} %copy-done.2), custom_call_target="tpu_custom_call" | custom-call | tf_op jit(solution)/shard_map/cond/branch_0_fun/order_z/pallas_call | solution.py:244
  38.4 0.9 %slice.3 = bf16[16,40,128]{2,1,0:T(8,128)(2,1)S(1)} slice(bf16[32,40,128]{2,1,0:T(8,128)(2,1)} %get-tuple-element.44.part_ref), slice={[16:32], [0:40], [0:128]} | slice | bytes 327680 | tf_op jit(solution)/shard_map/slice | solution.py:253
  39.4 22.8 %collective-permute-start.1 = (bf16[16,40,128]{2,1,0:T(8,128)(2,1)S(1)}, bf16[16,40,128]{2,1,0:T(8,128)(2,1)S(1)}, u32[]{:S(2)}, u32[]{:S(2)}) collective-permute-start(bf16[16,40,128]{2,1,0:T(8,128)(2,1)S(1)} %slice.3), channel_id=1, source_target_pairs={{0,1},{1,0},{2,3},{3,2},{4,5},{5,4},{6,7},{7,6},{8,9},{9,8},{10,11... | collective-permute-start | bytes 491528 | tf_op jit(solution)/shard_map/ppermute | solution.py:253
  62.2 1.0 %add_own.1.base_ref = f32[3,12,8,256]{3,2,1,0:T(8,128)S(1)} custom-call(f32[3,12,8,256]{3,2,1,0:T(8,128)S(1)} %get-tuple-element.43.base_ref, bf16[32,40,128]{2,1,0:T(8,128)(2,1)} %get-tuple-element.44.part_ref), custom_call_target="tpu_custom_call" | custom-call | tf_op jit(solution)/shard_map/add_own/pallas_call | solution.py:205
  63.2 0.0 collective-permute-done.1.part_ref
  63.2 0.9 %add_other.1 = f32[3,12,8,256]{3,2,1,0:T(8,128)} custom-call(f32[3,12,8,256]{3,2,1,0:T(8,128)S(1)} %add_own.1.base_ref, bf16[16,40,128]{2,1,0:T(8,128)(2,1)S(1)} %collective-permute-done.1.part_ref), custom_call_target="tpu_custom_call" | custom-call | tf_op jit(solution)/shard_map/add_other/pallas_call | solution.py:205
  (5 shorter events, 0.0 us)
Async XLA Ops:
  0.0 10.6 %copy-start = (f32[3,8,12,256]{3,1,2,0:T(8,128)S(1)}, f32[3,8,12,256]{3,1,2,0:T(8,128)}, u32[]{:S(2)}) copy-start(f32[3,8,12,256]{3,1,2,0:T(8,128)} %param.7) | copy-start | bytes 884740
  0.0 10.6 %copy-start.1 = (bf16[3,8,12,256]{3,1,2,0:T(8,128)(2,1)S(1)}, bf16[3,8,12,256]{3,1,2,0:T(8,128)(2,1)}, u32[]{:S(2)}) copy-start(bf16[3,8,12,256]{3,1,2,0:T(8,128)(2,1)} %param.8) | copy-start | bytes 442372
  0.0 12.0 %copy-start.4 = (bf16[768,384]{1,0:T(8,128)(2,1)S(1)}, bf16[768,384]{1,0:T(8,128)(2,1)}, u32[]{:S(2)}) copy-start(bf16[768,384]{1,0:T(8,128)(2,1)} %param.10) | copy-start | bytes 1769476
  2.0 10.0 %collective-permute-start = (bf16[16,72,128]{2,1,0:T(8,128)(2,1)}, bf16[16,72,128]{2,1,0:T(8,128)(2,1)S(1)}, u32[]{:S(2)}, u32[]{:S(2)}) collective-permute-start(bf16[16,72,128]{2,1,0:T(8,128)(2,1)} %pack_send.1), channel_id=1, source_target_pairs={{0,1},{1,0},{2,3},{3,2},{4,5},{5,4},{6,7},{7,6},{8,9},{9,8},{10,11... | collective-permute-start | bytes 884744 | tf_op jit(solution)/shard_map/ppermute | solution.py:250
  10.6 1.4 %copy-start.3 = (bf16[512,256]{1,0:T(8,128)(2,1)S(1)}, bf16[512,256]{1,0:T(8,128)(2,1)}, u32[]{:S(2)}) copy-start(bf16[512,256]{1,0:T(8,128)(2,1)} %param.9) | copy-start | bytes 786436
  10.6 1.4 %copy-start.5 = (bf16[256,128]{1,0:T(8,128)(2,1)S(1)}, bf16[256,128]{1,0:T(8,128)(2,1)}, u32[]{:S(2)}) copy-start(bf16[256,128]{1,0:T(8,128)(2,1)} %param.11) | copy-start | bytes 196612
  25.3 10.7 %all-to-all-start.1 = ((bf16[8,2,9,8,128]{4,3,2,1,0:T(8,128)(2,1)}), bf16[8,2,9,8,128]{4,3,2,1,0:T(8,128)(2,1)S(1)}, u32[]{:S(2)}, u32[]{:S(2)}) async-start(bf16[8,2,9,8,128]{4,3,2,1,0:T(8,128)(2,1)} %z_terms.1), calls=%async_computation.1 | async-start | bytes 589824 | tf_op jit(solution)/shard_map/cond/branch_0_fun/all_to_all | solution.py:243
  36.0 0.7 %copy-start.2 = (bf16[8,2,9,8,128]{4,3,2,1,0:T(8,128)(2,1)}, bf16[8,2,9,8,128]{4,3,2,1,0:T(8,128)(2,1)S(1)}, u32[]{:S(2)}) copy-start(bf16[8,2,9,8,128]{4,3,2,1,0:T(8,128)(2,1)S(1)} %all-to-all-done.1.rz_ref) | copy-start | bytes 884740 | tf_op jit(solution)/shard_map/cond
  39.4 23.8 %collective-permute-start.1 = (bf16[16,40,128]{2,1,0:T(8,128)(2,1)S(1)}, bf16[16,40,128]{2,1,0:T(8,128)(2,1)S(1)}, u32[]{:S(2)}, u32[]{:S(2)}) collective-permute-start(bf16[16,40,128]{2,1,0:T(8,128)(2,1)S(1)} %slice.3), channel_id=1, source_target_pairs={{0,1},{1,0},{2,3},{3,2},{4,5},{5,4},{6,7},{7,6},{8,9},{9,8},{10,11... | collective-permute-start | bytes 491528 | tf_op jit(solution)/shard_map/ppermute | solution.py:253

commit v4 on v3

--- a/solution.py
+++ b/solution.py
@@ -184,38 +184,39 @@
     length_z = cols * z_own
     a = adjoint.transpose(0, 2, 1, 3)
     u = base_flow.transpose(0, 2, 1, 3)
-    shape = jax.ShapeDtypeStruct
+    local_shape = pltpu.VMEM
     near = functools.partial(pltpu.with_memory_space_constraint, memory_space=pltpu.VMEM)
     exchange = functools.partial(lax.all_to_all, split_axis=0, concat_axis=0, tiled=True)
     partner = [(i, i ^ 1) for i in range(cols)]
     alike = [list(range(core, cols, 2)) for core in range(2)]
 
-    def pack(y_core, name):
+    def pack(y_core, name, place):
         return pl.pallas_call(
             functools.partial(pack_kernel, y_core),
             name=name,
-            out_shape=shape((2 * z_own, 6 * y_own, LANES), bf16),
+            out_shape=local_shape((2 * z_own, 6 * y_own, LANES), bf16),
             scratch_shapes=[pltpu.VMEM((2 * z_own * 6 * y_own, LANES), f32)],
-        )(a, u)
+        )(place(a), place(u))
 
     def x_terms():
-        return pl.pallas_call(x_kernel, name="x_terms", out_shape=shape(a.shape, f32))(a, u, stream_pair)
-
-    def add(y_core, name, base, part, near_base):
+        return pl.pallas_call(x_kernel, name="x_terms", out_shape=local_shape(a.shape, f32))(
+            near(a), near(u), near(stream_pair)
+        )
+
+    def add(y_core, name, base, part, shape):
         return pl.pallas_call(
             functools.partial(add_kernel, y_core),
             name=name,
-            out_shape=near_base(a.shape, f32),
+            out_shape=shape(a.shape, f32),
             scratch_shapes=[pltpu.VMEM((16 * BACK, LANES), f32)],
-        )(base, near(part))
+        )(near(base), near(part))
 
     def along_y(keep, recv):
-        base = x_terms()
         lines = exchange(jnp.concatenate([keep, recv], axis=0), "rows")
         terms = pl.pallas_call(
             y_kernel,
             name="y_terms",
-            out_shape=shape((rows, BACK, LANES), bf16),
+            out_shape=local_shape((rows, BACK, LANES), bf16),
             scratch_shapes=[
                 pltpu.VMEM((rows * 6 * y_own, LANES), f32),
                 pltpu.VMEM((6, length_y, LANES), f32),
@@ -224,35 +225,35 @@
                 pltpu.VMEM((3, length_y, LANES), f32),
                 pltpu.VMEM((rows * BACK, LANES), f32),
             ],
-        )(near(lines), normal_pair)
-        return exchange(terms, "rows"), base
+        )(near(lines), near(normal_pair))
+        return exchange(terms, "rows")
 
     def along_z(keep, recv):
-        base = x_terms()
         pair = [part.reshape(chips, 1, 18, z_own, LANES) for part in (recv, keep)]
         lines = exchange(jnp.concatenate(pair, axis=1), "cols", axis_index_groups=alike)
         terms = pl.pallas_call(
             z_kernel,
             name="z_terms",
-            out_shape=shape((chips, 2, 9, z_own, LANES), bf16),
+            out_shape=local_shape((chips, 2, 9, z_own, LANES), bf16),
             scratch_shapes=[
                 pltpu.VMEM((2 * length_z, 9 * LANES), f32),
                 pltpu.VMEM((length_z, 9 * LANES), f32),
             ],
-        )(lines, span_pair)
+        )(near(lines), near(span_pair))
         back = exchange(terms, "cols", axis_index_groups=alike)
         ordered = pl.pallas_call(
-            order_kernel, name="order_z", out_shape=shape((rows, BACK, LANES), bf16)
-        )(back)
-        return ordered, base
+            order_kernel, name="order_z", out_shape=local_shape((rows, BACK, LANES), bf16)
+        )(near(back))
+        return ordered
 
     core = lax.axis_index("cols") % 2
-    recv = lax.ppermute(pack(1, "pack_send"), "cols", partner)
-    keep = pack(0, "pack_keep")
-    both, base = lax.cond(core == 0, along_y, along_z, keep, recv)
+    recv = lax.ppermute(pack(1, "pack_send", lambda x: x), "cols", partner)
+    keep = pack(0, "pack_keep", near)
+    base = x_terms()
+    both = lax.cond(core == 0, along_y, along_z, keep, recv)
     other = lax.ppermute(both[rows // 2 :], "cols", partner)
-    base = add(0, "add_own", base, both, pltpu.VMEM)
-    out = add(1, "add_other", near(base), other, shape)
+    base = add(0, "add_own", base, both, local_shape)
+    out = add(1, "add_other", base, other, jax.ShapeDtypeStruct)
     return out.transpose(0, 2, 1, 3)
 
 

time: 64.5 us -> 62.1 us (0.963)
  blocking collectives: 11.1 us -> 21.9 us
  waiting for transfers between devices: 8.17 us -> 1.67 us
  Pallas kernels: 8.14 us -> 2.99 us
  local copies, waits for them, and re-layouts: 1.67 us -> 0.04 us
    all_to_all x0 -> x1, blocking collectives: none -> 11.5 us  [along_z(): back = exchange(terms, 'cols', axis_index_groups=alike)]
    all_to_all x1 -> x0, waiting for transfers between devices: 6.9 us -> none  [along_z(): back = exchange(terms, 'cols', axis_index_groups=alike)]
    ppermute x1, starting transfers between devices: 22.8 us -> 26.4 us  [local(): other = lax.ppermute(both[rows // 2:], 'cols', partner)]
    pallas_call x3, Pallas kernels: 4.23 us -> 0.76 us  [the longest x1 0.4 us: along_z(): pl.pallas_call(z_kernel, name='z_terms', out_shape=local_shape((chips, 2,...]
    all_to_all x1 -> x0, starting transfers between devices: 3.42 us -> none  [along_z(): back = exchange(terms, 'cols', axis_index_groups=alike)]
    pallas_call x2, Pallas kernels: 1.86 us -> 0.89 us  [add(): pl.pallas_call(functools.partial(add_kernel, y_core), name=name, out_shap...]
    slice x1, local copies, waits for them, and re-layouts: 0.93 us -> 0.02 us  [local(): other = lax.ppermute(both[rows // 2:], 'cols', partner)]
    pallas_call x2, Pallas kernels: 2.05 us -> 1.34 us  [pack(): pl.pallas_call(functools.partial(pack_kernel, y_core), name=name, out_sha...]
  transfers between devices with their start and end apart: 3 -> 2, of which waited for: 2 -> 2; matrix products, arithmetic and copies ran while one was open for 0% -> 0% of each run, Pallas kernels for 2% -> 1%
where the time goes in v4:
time: 62.1 us; the launch traced here: 61.8 us
  starting transfers between devices  35 us (56%)
  blocking collectives  21.9 us (35%)
  Pallas kernels  2.99 us (5%)
  waiting for transfers between devices  1.67 us (3%)
    ppermute x1, starting transfers between devices, local(): other = lax.ppermute(both[rows // 2:], 'cols', partner)  26.4 us
    all_to_all x1, blocking collectives, along_z(): back = exchange(terms, 'cols', axis_index_groups=alike)  11.5 us
    all_to_all x1, blocking collectives, along_z(): exchange(jnp.concatenate(pair, axis=1), 'cols', axis_index_groups=alike)  10.4 us
    ppermute x1, starting transfers between devices, local(): recv = lax.ppermute(pack(1, 'pack_send', lambda x: x), 'cols', partner)  8.59 us
    pallas_call x2, Pallas kernels, pack(): pl.pallas_call(functools.partial(pack_kernel, y_core), name=name, out_sha...  1.34 us
  transfers between devices with their start and end apart: 2, of which 2 were waited for; matrix products, arithmetic and copies ran while one was open for 0% of the time, Pallas kernels for 1%

profile of v4, /device:TPU:1, one launch (start us, length us, event | category | flops | bytes accessed | tf_op | source)
XLA Modules:
  0.0 61.8 jit_solution(12369306608823125964)
XLA Ops:
  0.0 0.0 copy-start
  0.0 0.0 copy-start.1
  0.0 0.0 copy-start.2
  0.0 1.3 %pack_send.1 = bf16[16,72,128]{2,1,0:T(8,128)(2,1)S(1)} custom-call(f32[3,12,8,256]{3,2,1,0:T(8,128)} %bitcast.5, bf16[3,12,8,256]{3,2,1,0:T(8,128)(2,1)} %bitcast.9), custom_call_target="tpu_custom_call" | custom-call | tf_op jit(solution)/shard_map/pack_send/pallas_call | solution.py:194
  1.3 8.6 %collective-permute-start = (bf16[16,72,128]{2,1,0:T(8,128)(2,1)S(1)}, bf16[16,72,128]{2,1,0:T(8,128)(2,1)S(1)}, u32[]{:S(2)}, u32[]{:S(2)}) collective-permute-start(bf16[16,72,128]{2,1,0:T(8,128)(2,1)S(1)} %pack_send.1), channel_id=1, source_target_pairs={{0,1},{1,0},{2,3},{3,2},{4,5},{5,4},{6,7},{7,6},{8,9},{9,8},{10,11... | collective-permute-start | bytes 884744 | tf_op jit(solution)/shard_map/ppermute | solution.py:250
  9.9 0.0 copy-done
  9.9 0.0 copy-done.1
  9.9 0.0 copy-start.4
  9.9 0.1 pack_keep.1
  10.0 1.1 %collective-permute-done = bf16[16,72,128]{2,1,0:T(8,128)(2,1)S(1)} collective-permute-done((bf16[16,72,128]{2,1,0:T(8,128)(2,1)S(1)}, bf16[16,72,128]{2,1,0:T(8,128)(2,1)S(1)}, u32[]{:S(2)}, u32[]{:S(2)}) %collective-permute-start) | collective-permute-done | bytes 294944 | tf_op jit(solution)/shard_map/ppermute | solution.py:250
  11.1 0.0 copy-done.2
  11.1 0.0 copy-done.4
  11.1 22.4 %conditional.1 = (bf16[32,40,128]{2,1,0:T(8,128)(2,1)S(1)}) conditional(s32[]{:T(128)} %convert_element_type.3, (bf16[16,72,128]{2,1,0:T(8,128)(2,1)S(1)}, bf16[16,72,128]{2,1,0:T(8,128)(2,1)S(1)}, bf16[256,128]{1,0:T(8,128)(2,1)S(1)}) %tuple.16, (bf16[16,72,128]{2,1,0:T(8,128)(2,1)S(1)}, bf16[16,72,128]{2,1,0:T(8,128)(2,1)S(1)}, ...), branch_computations={%region_0.1_spmd, %region_1.2_spmd} | conditional | flops 294912 | bytes 3014664 | solution.py:253
  11.1 0.1 pad_maximum_fusion
  11.1 10.4 %all_to_all.16.rz_ref = bf16[8,2,18,8,128]{4,3,2,1,0:T(8,128)(2,1)S(1)} all-to-all(bf16[8,2,18,8,128]{4,3,2,1,0:T(8,128)(2,1)S(1)} %pad_maximum_fusion), channel_id=1, replica_groups={{0,2,4,6,8,10,12,14},{1,3,5,7,9,11,13,15},{16,18,20,22,24,26,28,30},{17..., dimensions={0} | all-to-all | bytes 1179648 | tf_op jit(solution)/shard_map/cond/branch_0_fun/all_to_all | solution.py:233
  21.5 0.4 z_terms.1
  21.9 11.5 %all_to_all.17.rz_ref = bf16[8,2,9,8,128]{4,3,2,1,0:T(8,128)(2,1)S(1)} all-to-all(bf16[8,2,9,8,128]{4,3,2,1,0:T(8,128)(2,1)S(1)} %z_terms.1), channel_id=1, replica_groups={{0,2,4,6,8,10,12,14},{1,3,5,7,9,11,13,15},{16,18,20,22,24,26,28,30},{17..., dimensions={0} | all-to-all | bytes 589824 | tf_op jit(solution)/shard_map/cond/branch_0_fun/all_to_all | solution.py:243
  33.5 0.0 copy-start.3
  33.5 26.4 %collective-permute-start.1 = (bf16[16,40,128]{2,1,0:T(8,128)(2,1)S(1)}, bf16[16,40,128]{2,1,0:T(8,128)(2,1)S(1)}, u32[]{:S(2)}, u32[]{:S(2)}) collective-permute-start(bf16[16,40,128]{2,1,0:T(8,128)(2,1)S(1)} %slice.4), channel_id=1, source_target_pairs={{0,1},{1,0},{2,3},{3,2},{4,5},{5,4},{6,7},{7,6},{8,9},{9,8},{10,11... | collective-permute-start | bytes 491528 | tf_op jit(solution)/shard_map/ppermute | solution.py:254
  60.0 0.0 copy-done.3
  60.0 0.3 x_terms.1.base_ref
  60.3 0.1 add_own.1.base_ref
  60.4 0.6 collective-permute-done.1.part_ref
  61.0 0.8 %add_other.1 = f32[3,12,8,256]{3,2,1,0:T(8,128)} custom-call(f32[3,12,8,256]{3,2,1,0:T(8,128)S(1)} %add_own.1.base_ref, bf16[16,40,128]{2,1,0:T(8,128)(2,1)S(1)} %collective-permute-done.1.part_ref), custom_call_target="tpu_custom_call" | custom-call | tf_op jit(solution)/shard_map/add_other/pallas_call | solution.py:207
  (2 shorter events, 0.0 us)
Async XLA Ops:
  0.0 9.9 %copy-start = (f32[3,8,12,256]{3,1,2,0:T(8,128)S(1)}, f32[3,8,12,256]{3,1,2,0:T(8,128)}, u32[]{:S(2)}) copy-start(f32[3,8,12,256]{3,1,2,0:T(8,128)} %param.7) | copy-start | bytes 884740
  0.0 9.9 %copy-start.1 = (bf16[3,8,12,256]{3,1,2,0:T(8,128)(2,1)S(1)}, bf16[3,8,12,256]{3,1,2,0:T(8,128)(2,1)}, u32[]{:S(2)}) copy-start(bf16[3,8,12,256]{3,1,2,0:T(8,128)(2,1)} %param.8) | copy-start | bytes 442372
  0.0 11.1 %copy-start.2 = (bf16[768,384]{1,0:T(8,128)(2,1)S(1)}, bf16[768,384]{1,0:T(8,128)(2,1)}, u32[]{:S(2)}) copy-start(bf16[768,384]{1,0:T(8,128)(2,1)} %param.10) | copy-start | bytes 1769476
  1.3 9.8 %collective-permute-start = (bf16[16,72,128]{2,1,0:T(8,128)(2,1)S(1)}, bf16[16,72,128]{2,1,0:T(8,128)(2,1)S(1)}, u32[]{:S(2)}, u32[]{:S(2)}) collective-permute-start(bf16[16,72,128]{2,1,0:T(8,128)(2,1)S(1)} %pack_send.1), channel_id=1, source_target_pairs={{0,1},{1,0},{2,3},{3,2},{4,5},{5,4},{6,7},{7,6},{8,9},{9,8},{10,11... | collective-permute-start | bytes 884744 | tf_op jit(solution)/shard_map/ppermute | solution.py:250
  9.9 1.2 %copy-start.4 = (bf16[256,128]{1,0:T(8,128)(2,1)S(1)}, bf16[256,128]{1,0:T(8,128)(2,1)}, u32[]{:S(2)}) copy-start(bf16[256,128]{1,0:T(8,128)(2,1)} %param.11) | copy-start | bytes 196612
  33.5 26.5 %copy-start.3 = (bf16[512,256]{1,0:T(8,128)(2,1)S(1)}, bf16[512,256]{1,0:T(8,128)(2,1)}, u32[]{:S(2)}) copy-start(bf16[512,256]{1,0:T(8,128)(2,1)} %px_ref.1) | copy-start | bytes 786436
  33.5 27.4 %collective-permute-start.1 = (bf16[16,40,128]{2,1,0:T(8,128)(2,1)S(1)}, bf16[16,40,128]{2,1,0:T(8,128)(2,1)S(1)}, u32[]{:S(2)}, u32[]{:S(2)}) collective-permute-start(bf16[16,40,128]{2,1,0:T(8,128)(2,1)S(1)} %slice.4), channel_id=1, source_target_pairs={{0,1},{1,0},{2,3},{3,2},{4,5},{5,4},{6,7},{7,6},{8,9},{9,8},{10,11... | collective-permute-start | bytes 491528 | tf_op jit(solution)/shard_map/ppermute | solution.py:254

commit v5 on v4

--- a/solution.py
+++ b/solution.py
@@ -144,7 +144,7 @@
         for p in range(pieces):
             for k in range(slabs):
                 row = (p * slabs + k) * z_own
-                out_ref[16 * side + row // BACK, pl.ds(row % BACK, z_own), :] = rz_ref[p, 1 - side, k]
+                out_ref[16 * side + row // BACK, pl.ds(row % BACK, z_own), :] = rz_ref[p, side, k]
         for row in range(pieces * slabs * z_own, 16 * BACK, z_own):
             out_ref[16 * side + row // BACK, pl.ds(row % BACK, z_own), :] = jnp.zeros((z_own, LANES), jnp.bfloat16)
 
@@ -229,7 +229,7 @@
         return exchange(terms, "rows")
 
     def along_z(keep, recv):
-        pair = [part.reshape(chips, 1, 18, z_own, LANES) for part in (recv, keep)]
+        pair = [part.reshape(chips, 1, 18, z_own, LANES) for part in (keep, recv)]
         lines = exchange(jnp.concatenate(pair, axis=1), "cols", axis_index_groups=alike)
         terms = pl.pallas_call(
             z_kernel,
@@ -247,13 +247,13 @@
         return ordered
 
     core = lax.axis_index("cols") % 2
-    recv = lax.ppermute(pack(1, "pack_send", lambda x: x), "cols", partner)
-    keep = pack(0, "pack_keep", near)
+    recv = lax.ppermute(pack(0, "pack_send", lambda x: x), "cols", partner)
+    keep = pack(1, "pack_keep", near)
     base = x_terms()
-    both = lax.cond(core == 0, along_y, along_z, keep, recv)
+    both = lax.cond(core == 1, along_y, along_z, keep, recv)
     other = lax.ppermute(both[rows // 2 :], "cols", partner)
-    base = add(0, "add_own", base, both, local_shape)
-    out = add(1, "add_other", base, other, jax.ShapeDtypeStruct)
+    base = add(1, "add_own", base, both, local_shape)
+    out = add(0, "add_other", base, other, jax.ShapeDtypeStruct)
     return out.transpose(0, 2, 1, 3)
 
 

time: 62.1 us -> 58.5 us (0.942)
  starting transfers between devices: 35 us -> 10.9 us
  blocking collectives: 21.9 us -> 41.8 us
    ppermute x1, starting transfers between devices: 26.4 us -> 2.05 us  [local(): other = lax.ppermute(both[rows // 2:], 'cols', partner)]
    all_to_all x2, blocking collectives: 21.9 us -> 41.8 us  [the longest x1 25.2 us: along_y(): lines = exchange(jnp.concatenate([keep, recv], axis=0), 'rows')]
where the time goes in v5:
time: 58.5 us; the launch traced here: 58.2 us
  blocking collectives  41.8 us (71%)
  starting transfers between devices  10.9 us (19%)
  Pallas kernels  3.52 us (6%)
  waiting for transfers between devices  1.78 us (3%)
    all_to_all x1, blocking collectives, along_y(): lines = exchange(jnp.concatenate([keep, recv], axis=0), 'rows')  25.2 us
    all_to_all x1, blocking collectives, along_y(): return exchange(terms, 'rows')  16.5 us
    ppermute x1, starting transfers between devices, local(): recv = lax.ppermute(pack(0, 'pack_send', lambda x: x), 'cols', partner)  8.9 us
    ppermute x1, starting transfers between devices, local(): other = lax.ppermute(both[rows // 2:], 'cols', partner)  2.05 us
    pallas_call x2, Pallas kernels, pack(): pl.pallas_call(functools.partial(pack_kernel, y_core), name=name, out_sha...  1.34 us
  transfers between devices with their start and end apart: 2, of which 2 were waited for; matrix products, arithmetic and copies ran while one was open for 0% of the time, Pallas kernels for 1%

profile of v5, /device:TPU:1, one launch (start us, length us, event | category | flops | bytes accessed | tf_op | source)
XLA Modules:
  0.0 58.2 jit_solution(9290975760287780906)
XLA Ops:
  0.0 0.0 copy-start
  0.0 0.0 copy-start.1
  0.0 0.0 copy-start.2
  0.0 1.1 %pack_send.1 = bf16[16,72,128]{2,1,0:T(8,128)(2,1)S(1)} custom-call(f32[3,12,8,256]{3,2,1,0:T(8,128)} %bitcast.5, bf16[3,12,8,256]{3,2,1,0:T(8,128)(2,1)} %bitcast.9), custom_call_target="tpu_custom_call" | custom-call | tf_op jit(solution)/shard_map/pack_send/pallas_call | solution.py:194
  1.1 8.9 %collective-permute-start = (bf16[16,72,128]{2,1,0:T(8,128)(2,1)S(1)}, bf16[16,72,128]{2,1,0:T(8,128)(2,1)S(1)}, u32[]{:S(2)}, u32[]{:S(2)}) collective-permute-start(bf16[16,72,128]{2,1,0:T(8,128)(2,1)S(1)} %pack_send.1), channel_id=1, source_target_pairs={{0,1},{1,0},{2,3},{3,2},{4,5},{5,4},{6,7},{7,6},{8,9},{9,8},{10,11... | collective-permute-start | bytes 884744 | tf_op jit(solution)/shard_map/ppermute | solution.py:250
  10.1 0.0 copy-done
  10.1 0.0 copy-done.1
  10.1 0.0 copy-start.4
  10.1 0.2 pack_keep.1
  10.3 0.9 %collective-permute-done = bf16[16,72,128]{2,1,0:T(8,128)(2,1)S(1)} collective-permute-done((bf16[16,72,128]{2,1,0:T(8,128)(2,1)S(1)}, bf16[16,72,128]{2,1,0:T(8,128)(2,1)S(1)}, u32[]{:S(2)}, u32[]{:S(2)}) %collective-permute-start) | collective-permute-done | bytes 294944 | tf_op jit(solution)/shard_map/ppermute | solution.py:250
  11.2 0.0 copy-done.2
  11.2 0.0 copy-done.4
  11.2 42.8 %conditional.1 = (bf16[32,40,128]{2,1,0:T(8,128)(2,1)S(1)}) conditional(s32[]{:T(128)} %convert_element_type.3, (bf16[16,72,128]{2,1,0:T(8,128)(2,1)S(1)}, bf16[16,72,128]{2,1,0:T(8,128)(2,1)S(1)}, bf16[256,128]{1,0:T(8,128)(2,1)S(1)}) %tuple.16, (bf16[16,72,128]{2,1,0:T(8,128)(2,1)S(1)}, bf16[16,72,128]{2,1,0:T(8,128)(2,1)S(1)}, ...), branch_computations={%region_0.1_spmd, %region_1.2_spmd} | conditional | flops 294912 | bytes 3014664 | solution.py:253
  11.2 0.1 pad_maximum_fusion.1
  11.3 25.2 %all_to_all.18.ry_ref = bf16[32,72,128]{2,1,0:T(8,128)(2,1)S(1)} all-to-all(bf16[32,72,128]{2,1,0:T(8,128)(2,1)S(1)} %pad_maximum_fusion.1), channel_id=1, replica_groups=mesh['rows'=32,'cols'=16] {'rows'}, dimensions={0} | all-to-all | bytes 1179648 | tf_op jit(solution)/shard_map/cond/branch_1_fun/all_to_all | solution.py:215
  36.5 1.0 %y_terms.1 = bf16[32,40,128]{2,1,0:T(8,128)(2,1)S(1)} custom-call(bf16[32,72,128]{2,1,0:T(8,128)(2,1)S(1)} %all_to_all.18.ry_ref, bf16[768,384]{1,0:T(8,128)(2,1)S(1)} %get-tuple-element.29.py_ref), custom_call_target="tpu_custom_call" | custom-call | tf_op jit(solution)/shard_map/cond/branch_1_fun/y_terms/pallas_call | solution.py:216
  37.5 16.5 %all_to_all.19 = bf16[32,40,128]{2,1,0:T(8,128)(2,1)S(1)} all-to-all(bf16[32,40,128]{2,1,0:T(8,128)(2,1)S(1)} %y_terms.1), channel_id=1, replica_groups=mesh['rows'=32,'cols'=16] {'rows'}, dimensions={0} | all-to-all | bytes 655360 | tf_op jit(solution)/shard_map/cond/branch_1_fun/all_to_all | solution.py:229
  54.0 0.0 copy-start.3
  54.1 2.1 %collective-permute-start.1 = (bf16[16,40,128]{2,1,0:T(8,128)(2,1)S(1)}, bf16[16,40,128]{2,1,0:T(8,128)(2,1)S(1)}, u32[]{:S(2)}, u32[]{:S(2)}) collective-permute-start(bf16[16,40,128]{2,1,0:T(8,128)(2,1)S(1)} %slice.4), channel_id=1, source_target_pairs={{0,1},{1,0},{2,3},{3,2},{4,5},{5,4},{6,7},{7,6},{8,9},{9,8},{10,11... | collective-permute-start | bytes 491528 | tf_op jit(solution)/shard_map/ppermute | solution.py:254
  56.1 0.0 copy-done.3
  56.1 0.3 x_terms.1.base_ref
  56.5 0.1 add_own.1.base_ref
  56.6 0.9 %collective-permute-done.1.part_ref = bf16[16,40,128]{2,1,0:T(8,128)(2,1)S(1)} collective-permute-done((bf16[16,40,128]{2,1,0:T(8,128)(2,1)S(1)}, bf16[16,40,128]{2,1,0:T(8,128)(2,1)S(1)}, u32[]{:S(2)}, u32[]{:S(2)}) %collective-permute-start.1) | collective-permute-done | bytes 163872 | tf_op jit(solution)/shard_map/ppermute | solution.py:254
  57.5 0.7 %add_other.1 = f32[3,12,8,256]{3,2,1,0:T(8,128)} custom-call(f32[3,12,8,256]{3,2,1,0:T(8,128)S(1)} %add_own.1.base_ref, bf16[16,40,128]{2,1,0:T(8,128)(2,1)S(1)} %collective-permute-done.1.part_ref), custom_call_target="tpu_custom_call" | custom-call | tf_op jit(solution)/shard_map/add_other/pallas_call | solution.py:207
  (1 shorter events, 0.0 us)
Async XLA Ops:
  0.0 10.1 %copy-start = (f32[3,8,12,256]{3,1,2,0:T(8,128)S(1)}, f32[3,8,12,256]{3,1,2,0:T(8,128)}, u32[]{:S(2)}) copy-start(f32[3,8,12,256]{3,1,2,0:T(8,128)} %param.7) | copy-start | bytes 884740
  0.0 10.1 %copy-start.1 = (bf16[3,8,12,256]{3,1,2,0:T(8,128)(2,1)S(1)}, bf16[3,8,12,256]{3,1,2,0:T(8,128)(2,1)}, u32[]{:S(2)}) copy-start(bf16[3,8,12,256]{3,1,2,0:T(8,128)(2,1)} %param.8) | copy-start | bytes 442372
  0.0 11.2 %copy-start.2 = (bf16[768,384]{1,0:T(8,128)(2,1)S(1)}, bf16[768,384]{1,0:T(8,128)(2,1)}, u32[]{:S(2)}) copy-start(bf16[768,384]{1,0:T(8,128)(2,1)} %param.10) | copy-start | bytes 1769476
  1.1 10.1 %collective-permute-start = (bf16[16,72,128]{2,1,0:T(8,128)(2,1)S(1)}, bf16[16,72,128]{2,1,0:T(8,128)(2,1)S(1)}, u32[]{:S(2)}, u32[]{:S(2)}) collective-permute-start(bf16[16,72,128]{2,1,0:T(8,128)(2,1)S(1)} %pack_send.1), channel_id=1, source_target_pairs={{0,1},{1,0},{2,3},{3,2},{4,5},{5,4},{6,7},{7,6},{8,9},{9,8},{10,11... | collective-permute-start | bytes 884744 | tf_op jit(solution)/shard_map/ppermute | solution.py:250
  10.1 1.2 %copy-start.4 = (bf16[256,128]{1,0:T(8,128)(2,1)S(1)}, bf16[256,128]{1,0:T(8,128)(2,1)}, u32[]{:S(2)}) copy-start(bf16[256,128]{1,0:T(8,128)(2,1)} %param.11) | copy-start | bytes 196612
  54.0 2.1 %copy-start.3 = (bf16[512,256]{1,0:T(8,128)(2,1)S(1)}, bf16[512,256]{1,0:T(8,128)(2,1)}, u32[]{:S(2)}) copy-start(bf16[512,256]{1,0:T(8,128)(2,1)} %px_ref.1) | copy-start | bytes 786436
  54.1 3.4 %collective-permute-start.1 = (bf16[16,40,128]{2,1,0:T(8,128)(2,1)S(1)}, bf16[16,40,128]{2,1,0:T(8,128)(2,1)S(1)}, u32[]{:S(2)}, u32[]{:S(2)}) collective-permute-start(bf16[16,40,128]{2,1,0:T(8,128)(2,1)S(1)} %slice.4), channel_id=1, source_target_pairs={{0,1},{1,0},{2,3},{3,2},{4,5},{5,4},{6,7},{7,6},{8,9},{9,8},{10,11... | collective-permute-start | bytes 491528 | tf_op jit(solution)/shard_map/ppermute | solution.py:254

commit v6 on v5

--- a/solution.py
+++ b/solution.py
@@ -13,44 +13,55 @@
 BACK = 40
 
 
-def fields(a_ref, u_ref, f, half):
-    at = pl.ds(half * LANES, LANES)
-    if f < 3:
-        return a_ref[f, :, :, at]
-    return u_ref[f - 3, :, :, at].astype(jnp.float32)
-
-
-def pack_y(a_ref, u_ref, out_ref, stage):
-    y_own, z_own = a_ref.shape[1:3]
+def pack_field(is_y, f, value, out_ref, stage, y_own, z_own):
     rows = 6 * y_own
+
+    @pl.when(is_y)
+    def _():
+        for half in range(2):
+            points = value(half)
+            for y in range(y_own):
+                stage[pl.ds(half * rows + f * y_own + y, z_own, stride=2 * rows), :] = points[y]
+
+    @pl.when(jnp.logical_not(is_y))
+    def _():
+        for half in range(2):
+            points = value(half).astype(jnp.bfloat16)
+            for y in range(y_own):
+                row = ((y // 3 * 2 + half) * 18 + f * 3 + y % 3) * z_own
+                out_ref[row // 72, pl.ds(row % 72, z_own), :] = points[y]
+
+
+def pack_fields(is_y, a_ref, u_ref, out_ref, stage, ready):
     for f in range(6):
-        for half in range(2):
-            value = fields(a_ref, u_ref, f, half)
-            for y in range(y_own):
-                stage[pl.ds(half * rows + f * y_own + y, z_own, stride=2 * rows), :] = value[y]
-    out_ref[...] = stage[...].reshape(2 * z_own, rows, LANES).astype(jnp.bfloat16)
-
-
-def pack_z(a_ref, u_ref, out_ref):
-    y_own, z_own = a_ref.shape[1:3]
-    for f in range(6):
-        for half in range(2):
-            value = fields(a_ref, u_ref, f, half).astype(jnp.bfloat16)
-            for y in range(y_own):
-                row = ((y // 3 * 2 + half) * 18 + f * 3 + y % 3) * z_own
-                out_ref[row // 72, pl.ds(row % 72, z_own), :] = value[y]
-
-
-def pack_kernel(y_core, a_ref, u_ref, out_ref, stage):
-    is_y = lax.axis_index("cols") % 2 == y_core
+        ready(f)
+        ref, j = (a_ref, f) if f < 3 else (u_ref, f - 3)
+        pack_field(
+            is_y,
+            f,
+            lambda half: ref[j, :, :, pl.ds(half * LANES, LANES)].astype(jnp.float32),
+            out_ref,
+            stage,
+            *ref.shape[1:3],
+        )
 
     @pl.when(is_y)
     def _():
-        pack_y(a_ref, u_ref, out_ref, stage)
-
-    @pl.when(jnp.logical_not(is_y))
-    def _():
-        pack_z(a_ref, u_ref, out_ref)
+        out_ref[...] = stage[...].reshape(out_ref.shape).astype(jnp.bfloat16)
+
+
+def pack_send_kernel(a_hbm, u_hbm, out_ref, a_ref, u_ref, stage, arrived):
+    copies = [pltpu.make_async_copy(a_hbm.at[j], a_ref.at[j], arrived.at[j]) for j in range(3)]
+    copies += [pltpu.make_async_copy(u_hbm.at[j], u_ref.at[j], arrived.at[3 + j]) for j in range(3)]
+    for copy in copies:
+        copy.start()
+    is_y = lax.axis_index("cols") % 2 == 0
+    pack_fields(is_y, a_ref, u_ref, out_ref, stage, lambda f: copies[f].wait())
+
+
+def pack_keep_kernel(a_ref, u_ref, out_ref, stage):
+    is_y = lax.axis_index("cols") % 2 == 1
+    pack_fields(is_y, a_ref, u_ref, out_ref, stage, lambda f: None)
 
 
 def x_kernel(a_ref, u_ref, px_ref, out_ref):
@@ -149,29 +160,46 @@
             out_ref[16 * side + row // BACK, pl.ds(row % BACK, z_own), :] = jnp.zeros((z_own, LANES), jnp.bfloat16)
 
 
-def add_kernel(y_core, base_ref, part_ref, out_ref, stage):
+def add_parts(is_y, base_ref, part_ref, out_ref, stage, done):
     comps, y_own, z_own, _ = base_ref.shape
-    is_y = lax.axis_index("cols") % 2 == y_core
 
     @pl.when(is_y)
     def _():
         stage[...] = part_ref[pl.ds(0, 16)].astype(jnp.float32).reshape(stage.shape)
-        for c in range(comps):
+
+    for c in range(comps):
+
+        @pl.when(is_y)
+        def _():
             for y in range(y_own):
                 for half in range(2):
                     at = pl.ds(half * LANES, LANES)
                     piece = stage[pl.ds(half * BACK + c * y_own + y, z_own, stride=2 * BACK), :]
                     out_ref[c, y, :, at] = base_ref[c, y, :, at] + section_step * piece
 
-    @pl.when(jnp.logical_not(is_y))
-    def _():
-        for c in range(comps):
+        @pl.when(jnp.logical_not(is_y))
+        def _():
             for y in range(y_own):
                 for half in range(2):
                     at = pl.ds(half * LANES, LANES)
                     row = ((y // 3 * 2 + half) * 9 + c * 3 + y % 3) * z_own
                     piece = part_ref[row // BACK, pl.ds(row % BACK, z_own), :].astype(jnp.float32)
                     out_ref[c, y, :, at] = base_ref[c, y, :, at] + section_step * piece
+
+        done(c)
+
+
+def add_own_kernel(base_ref, part_ref, out_ref, stage):
+    is_y = lax.axis_index("cols") % 2 == 1
+    add_parts(is_y, base_ref, part_ref, out_ref, stage, lambda c: None)
+
+
+def add_other_kernel(base_ref, part_ref, out_hbm, stage, total, left):
+    is_y = lax.axis_index("cols") % 2 == 0
+    copies = [pltpu.make_async_copy(total.at[c], out_hbm.at[c], left.at[c]) for c in range(3)]
+    add_parts(is_y, base_ref, part_ref, total, stage, lambda c: copies[c].start())
+    for copy in copies:
+        copy.wait()
 
 
 def local(adjoint, base_flow, stream_pair, normal_pair, span_pair):
@@ -189,27 +217,6 @@
     exchange = functools.partial(lax.all_to_all, split_axis=0, concat_axis=0, tiled=True)
     partner = [(i, i ^ 1) for i in range(cols)]
     alike = [list(range(core, cols, 2)) for core in range(2)]
-
-    def pack(y_core, name, place):
-        return pl.pallas_call(
-            functools.partial(pack_kernel, y_core),
-            name=name,
-            out_shape=local_shape((2 * z_own, 6 * y_own, LANES), bf16),
-            scratch_shapes=[pltpu.VMEM((2 * z_own * 6 * y_own, LANES), f32)],
-        )(place(a), place(u))
-
-    def x_terms():
-        return pl.pallas_call(x_kernel, name="x_terms", out_shape=local_shape(a.shape, f32))(
-            near(a), near(u), near(stream_pair)
-        )
-
-    def add(y_core, name, base, part, shape):
-        return pl.pallas_call(
-            functools.partial(add_kernel, y_core),
-            name=name,
-            out_shape=shape(a.shape, f32),
-            scratch_shapes=[pltpu.VMEM((16 * BACK, LANES), f32)],
-        )(near(base), near(part))
 
     def along_y(keep, recv):
         lines = exchange(jnp.concatenate([keep, recv], axis=0), "rows")
@@ -246,14 +253,36 @@
         )(near(back))
         return ordered
 
-    core = lax.axis_index("cols") % 2
-    recv = lax.ppermute(pack(0, "pack_send", lambda x: x), "cols", partner)
-    keep = pack(1, "pack_keep", near)
-    base = x_terms()
-    both = lax.cond(core == 1, along_y, along_z, keep, recv)
+    packed = (2 * z_own, 6 * y_own, LANES)
+    pack_stage = pltpu.VMEM((2 * z_own * 6 * y_own, LANES), f32)
+    send, a, u = pl.pallas_call(
+        pack_send_kernel,
+        name="pack_send",
+        in_specs=[pl.BlockSpec(memory_space=pl.ANY)] * 2,
+        out_shape=(local_shape(packed, bf16), local_shape(a.shape, f32), local_shape(u.shape, bf16)),
+        scratch_shapes=[pack_stage, pltpu.SemaphoreType.DMA((6,))],
+    )(a, u)
+    send, normal_pair = lax.optimization_barrier((send, normal_pair))
+    recv = lax.ppermute(send, "cols", partner)
+    keep = pl.pallas_call(
+        pack_keep_kernel, name="pack_keep", out_shape=local_shape(packed, bf16), scratch_shapes=[pack_stage]
+    )(near(a), near(u))
+    base = pl.pallas_call(x_kernel, name="x_terms", out_shape=local_shape(a.shape, f32))(
+        near(a), near(u), near(stream_pair)
+    )
+    both = lax.cond(lax.axis_index("cols") % 2 == 1, along_y, along_z, keep, recv)
     other = lax.ppermute(both[rows // 2 :], "cols", partner)
-    base = add(1, "add_own", base, both, local_shape)
-    out = add(0, "add_other", base, other, jax.ShapeDtypeStruct)
+    add_stage = pltpu.VMEM((16 * BACK, LANES), f32)
+    base = pl.pallas_call(
+        add_own_kernel, name="add_own", out_shape=local_shape(a.shape, f32), scratch_shapes=[add_stage]
+    )(near(base), near(both))
+    out = pl.pallas_call(
+        add_other_kernel,
+        name="add_other",
+        out_shape=jax.ShapeDtypeStruct(a.shape, f32),
+        out_specs=pl.BlockSpec(memory_space=pl.ANY),
+        scratch_shapes=[add_stage, pltpu.VMEM(a.shape, f32), pltpu.SemaphoreType.DMA((3,))],
+    )(near(base), near(other))
     return out.transpose(0, 2, 1, 3)
 
 

time: 58.5 us -> 58.4 us (level)
  no operation moved by 1% of the time
where the time goes in v6:
time: 58.4 us; the launch traced here: 58.2 us
  blocking collectives  41.8 us (72%)
  starting transfers between devices  10.9 us (19%)
  Pallas kernels  3.57 us (6%)
  waiting for transfers between devices  1.77 us (3%)
    all_to_all x1, blocking collectives, along_y(): lines = exchange(jnp.concatenate([keep, recv], axis=0), 'rows')  25.2 us
    all_to_all x1, blocking collectives, along_y(): return exchange(terms, 'rows')  16.5 us
    ppermute x1, starting transfers between devices, local(): recv = lax.ppermute(send, 'cols', partner)  8.86 us
    ppermute x1, starting transfers between devices, local(): other = lax.ppermute(both[rows // 2:], 'cols', partner)  2.05 us
  transfers between devices with their start and end apart: 2, of which 2 were waited for; matrix products, arithmetic and copies ran while one was open for 0% of the time, Pallas kernels for 1%

profile of v6, /device:TPU:1, one launch (start us, length us, event | category | flops | bytes accessed | tf_op | source)
XLA Modules:
  0.0 58.2 jit_solution(7820721132887267843)
XLA Ops:
  0.0 0.0 copy-start
  0.0 1.1 %pack_send.1 = (bf16[16,72,128]{2,1,0:T(8,128)(2,1)S(1)}, f32[3,12,8,256]{3,2,1,0:T(8,128)S(1)}, bf16[3,12,8,256]{3,2,1,0:T(8,128)(2,1)S(1)}) custom-call(f32[3,12,8,256]{3,2,1,0:T(8,128)} %bitcast.7, bf16[3,12,8,256]{3,2,1,0:T(8,128)(2,1)} %bitcast.8), custom_call_target="tpu_custom_call" | custom-call | tf_op jit(solution)/shard_map/pack_send/pallas_call | solution.py:258
  1.2 8.9 %collective-permute-start = (bf16[16,72,128]{2,1,0:T(8,128)(2,1)S(1)}, bf16[16,72,128]{2,1,0:T(8,128)(2,1)S(1)}, u32[]{:S(2)}, u32[]{:S(2)}) collective-permute-start(bf16[16,72,128]{2,1,0:T(8,128)(2,1)S(1)} %get-tuple-element.34), channel_id=1, source_target_pairs={{0,1},{1,0},{2,3},{3,2},{4,5},{5,4},{6,7},{7,6},{8,9},{9,8},{10,11... | collective-permute-start | bytes 884744 | tf_op jit(solution)/shard_map/ppermute | solution.py:266
  10.0 0.0 copy-start.2
  10.0 0.2 pack_keep.1
  10.3 0.9 %collective-permute-done = bf16[16,72,128]{2,1,0:T(8,128)(2,1)S(1)} collective-permute-done((bf16[16,72,128]{2,1,0:T(8,128)(2,1)S(1)}, bf16[16,72,128]{2,1,0:T(8,128)(2,1)S(1)}, u32[]{:S(2)}, u32[]{:S(2)}) %collective-permute-start) | collective-permute-done | bytes 294944 | tf_op jit(solution)/shard_map/ppermute | solution.py:266
  11.2 0.0 copy-done
  11.2 0.0 copy-done.2
  11.2 42.8 %conditional.1 = (bf16[32,40,128]{2,1,0:T(8,128)(2,1)S(1)}) conditional(s32[]{:T(128)} %convert_element_type.3, (bf16[16,72,128]{2,1,0:T(8,128)(2,1)S(1)}, bf16[16,72,128]{2,1,0:T(8,128)(2,1)S(1)}, bf16[256,128]{1,0:T(8,128)(2,1)S(1)}) %tuple.18, (bf16[16,72,128]{2,1,0:T(8,128)(2,1)S(1)}, bf16[16,72,128]{2,1,0:T(8,128)(2,1)S(1)}, ...), branch_computations={%region_0.1_spmd, %region_1.2_spmd} | conditional | flops 294912 | bytes 3014664 | solution.py:273
  11.2 0.1 pad_maximum_fusion.1
  11.3 25.2 %all_to_all.18.ry_ref = bf16[32,72,128]{2,1,0:T(8,128)(2,1)S(1)} all-to-all(bf16[32,72,128]{2,1,0:T(8,128)(2,1)S(1)} %pad_maximum_fusion.1), channel_id=1, replica_groups=mesh['rows'=32,'cols'=16] {'rows'}, dimensions={0} | all-to-all | bytes 1179648 | tf_op jit(solution)/shard_map/cond/branch_1_fun/all_to_all | solution.py:222
  36.5 1.0 %y_terms.1 = bf16[32,40,128]{2,1,0:T(8,128)(2,1)S(1)} custom-call(bf16[32,72,128]{2,1,0:T(8,128)(2,1)S(1)} %all_to_all.18.ry_ref, bf16[768,384]{1,0:T(8,128)(2,1)S(1)} %get-tuple-element.25.py_ref), custom_call_target="tpu_custom_call" | custom-call | tf_op jit(solution)/shard_map/cond/branch_1_fun/y_terms/pallas_call | solution.py:223
  37.5 16.5 %all_to_all.19 = bf16[32,40,128]{2,1,0:T(8,128)(2,1)S(1)} all-to-all(bf16[32,40,128]{2,1,0:T(8,128)(2,1)S(1)} %y_terms.1), channel_id=1, replica_groups=mesh['rows'=32,'cols'=16] {'rows'}, dimensions={0} | all-to-all | bytes 655360 | tf_op jit(solution)/shard_map/cond/branch_1_fun/all_to_all | solution.py:236
  54.0 0.0 copy-start.1
  54.0 2.1 %collective-permute-start.1 = (bf16[16,40,128]{2,1,0:T(8,128)(2,1)S(1)}, bf16[16,40,128]{2,1,0:T(8,128)(2,1)S(1)}, u32[]{:S(2)}, u32[]{:S(2)}) collective-permute-start(bf16[16,40,128]{2,1,0:T(8,128)(2,1)S(1)} %slice.4), channel_id=1, source_target_pairs={{0,1},{1,0},{2,3},{3,2},{4,5},{5,4},{6,7},{7,6},{8,9},{9,8},{10,11... | collective-permute-start | bytes 491528 | tf_op jit(solution)/shard_map/ppermute | solution.py:274
  56.1 0.0 copy-done.1
  56.1 0.3 x_terms.1.base_ref
  56.4 0.2 add_own.1.base_ref
  56.6 0.8 %collective-permute-done.1.part_ref = bf16[16,40,128]{2,1,0:T(8,128)(2,1)S(1)} collective-permute-done((bf16[16,40,128]{2,1,0:T(8,128)(2,1)S(1)}, bf16[16,40,128]{2,1,0:T(8,128)(2,1)S(1)}, u32[]{:S(2)}, u32[]{:S(2)}) %collective-permute-start.1) | collective-permute-done | bytes 163872 | tf_op jit(solution)/shard_map/ppermute | solution.py:274
  57.4 0.7 %add_other.1 = f32[3,12,8,256]{3,2,1,0:T(8,128)} custom-call(f32[3,12,8,256]{3,2,1,0:T(8,128)S(1)} %add_own.1.base_ref, bf16[16,40,128]{2,1,0:T(8,128)(2,1)S(1)} %collective-permute-done.1.part_ref), custom_call_target="tpu_custom_call" | custom-call | tf_op jit(solution)/shard_map/add_other/pallas_call | solution.py:279
  (1 shorter events, 0.0 us)
Async XLA Ops:
  0.0 11.2 %copy-start = (bf16[768,384]{1,0:T(8,128)(2,1)S(1)}, bf16[768,384]{1,0:T(8,128)(2,1)}, u32[]{:S(2)}) copy-start(bf16[768,384]{1,0:T(8,128)(2,1)} %param.10) | copy-start | bytes 1769476
  1.2 10.1 %collective-permute-start = (bf16[16,72,128]{2,1,0:T(8,128)(2,1)S(1)}, bf16[16,72,128]{2,1,0:T(8,128)(2,1)S(1)}, u32[]{:S(2)}, u32[]{:S(2)}) collective-permute-start(bf16[16,72,128]{2,1,0:T(8,128)(2,1)S(1)} %get-tuple-element.34), channel_id=1, source_target_pairs={{0,1},{1,0},{2,3},{3,2},{4,5},{5,4},{6,7},{7,6},{8,9},{9,8},{10,11... | collective-permute-start | bytes 884744 | tf_op jit(solution)/shard_map/ppermute | solution.py:266
  10.0 1.2 %copy-start.2 = (bf16[256,128]{1,0:T(8,128)(2,1)S(1)}, bf16[256,128]{1,0:T(8,128)(2,1)}, u32[]{:S(2)}) copy-start(bf16[256,128]{1,0:T(8,128)(2,1)} %param.11) | copy-start | bytes 196612
  54.0 2.1 %copy-start.1 = (bf16[512,256]{1,0:T(8,128)(2,1)S(1)}, bf16[512,256]{1,0:T(8,128)(2,1)}, u32[]{:S(2)}) copy-start(bf16[512,256]{1,0:T(8,128)(2,1)} %px_ref.1) | copy-start | bytes 786436
  54.0 3.4 %collective-permute-start.1 = (bf16[16,40,128]{2,1,0:T(8,128)(2,1)S(1)}, bf16[16,40,128]{2,1,0:T(8,128)(2,1)S(1)}, u32[]{:S(2)}, u32[]{:S(2)}) collective-permute-start(bf16[16,40,128]{2,1,0:T(8,128)(2,1)S(1)} %slice.4), channel_id=1, source_target_pairs={{0,1},{1,0},{2,3},{3,2},{4,5},{5,4},{6,7},{7,6},{8,9},{9,8},{10,11... | collective-permute-start | bytes 491528 | tf_op jit(solution)/shard_map/ppermute | solution.py:274

commit v7 on v6

--- a/solution.py
+++ b/solution.py
@@ -108,41 +108,49 @@
             oz_ref[:, :, 3 * c + y] = term.reshape(chips, 2, z_own, LANES).astype(jnp.bfloat16)
 
 
-def y_kernel(ry_ref, py_ref, oy_ref, stage, lines, derivs, base_derivs, terms, back):
+def permute_kernel(py_ref, out_ref):
+    length = py_ref.shape[1]
+    row = lax.broadcasted_iota(jnp.int32, (length, length), 0)
+    eight = row >> 3
+    group = (eight * 43) >> 9
+    source = group * 96 + (row & 7) * 12 + (eight - group * 12)
+    column = lax.broadcasted_iota(jnp.int32, (length, length), 1)
+    pick = jnp.where(source == column, 1.0, 0.0).astype(jnp.bfloat16)
+    dims = (((1,), (1,)), ((), ()))
+    for h in range(2):
+        at = pl.ds(h * length, length)
+        rows = jnp.dot(pick, py_ref[at, :], preferred_element_type=jnp.float32).astype(jnp.bfloat16)
+        both = lax.dot_general(rows, pick, dims, preferred_element_type=jnp.float32)
+        out_ref[at, :] = both.astype(jnp.bfloat16)
+
+
+def y_kernel(ry_ref, py_ref, oy_ref, stage, derivs, base_derivs, back):
     peers, rows = ry_ref.shape[:2]
     y_own = rows // 6
     length = peers * y_own
     stage[...] = ry_ref[...].astype(jnp.float32).reshape(stage.shape)
-    for f in range(6):
-        for y in range(y_own):
-            for g in range(peers // 8):
-                lines[f, pl.ds(8 * g * y_own + y, 8, stride=y_own), :] = stage[
-                    pl.ds(8 * g * rows + f * y_own + y, 8, stride=rows), :
-                ]
-    packed = [lines[f].astype(jnp.bfloat16) for f in range(6)]
+    order = [(g, w) for g in range(peers // 8) for w in range(y_own)]
+
+    def points(f, g, w):
+        return stage[pl.ds(8 * g * rows + f * y_own + w, 8, stride=rows), :]
+
+    packed = [jnp.concatenate([points(f, *at) for at in order], axis=0).astype(jnp.bfloat16) for f in range(6)]
     derivs[...] = jnp.dot(
         py_ref[...], jnp.concatenate(packed[:3], axis=1), preferred_element_type=jnp.float32
     )
     base_derivs[...] = jnp.dot(
         py_ref[pl.ds(0, length), :], jnp.concatenate(packed[3:], axis=1), preferred_element_type=jnp.float32
     )
-    block = 48
-    for b in range(length // block):
-        at = pl.ds(b * block, block)
-        lane = [pl.ds(j * LANES, LANES) for j in range(3)]
-        u_dir = lines[4, at, :]
-        transfer = sum(lines[j, at, :] * base_derivs[at, lane[j]] for j in range(3))
+    lane = [pl.ds(j * LANES, LANES) for j in range(3)]
+    for i, (g, w) in enumerate(order):
+        at, second = pl.ds(8 * i, 8), pl.ds(length + 8 * i, 8)
+        u_dir = points(4, g, w)
+        transfer = sum(points(j, g, w) * base_derivs[at, lane[j]] for j in range(3))
         for c in range(3):
-            term = u_dir * derivs[at, lane[c]] + viscosity * derivs[pl.ds(length + b * block, block), lane[c]]
+            term = u_dir * derivs[at, lane[c]] + viscosity * derivs[second, lane[c]]
             if c == 1:
                 term = term - transfer
-            terms[c, at, :] = term
-    for c in range(3):
-        for y in range(y_own):
-            for g in range(peers // 8):
-                back[pl.ds(8 * g * BACK + c * y_own + y, 8, stride=BACK), :] = terms[
-                    c, pl.ds(8 * g * y_own + y, 8, stride=y_own), :
-                ]
+            back[pl.ds(8 * g * BACK + c * y_own + w, 8, stride=BACK), :] = term
     for p in range(peers):
         used = 3 * y_own
         back[pl.ds(p * BACK + used, BACK - used), :] = jnp.zeros((BACK - used, LANES), jnp.float32)
@@ -226,10 +234,8 @@
             out_shape=local_shape((rows, BACK, LANES), bf16),
             scratch_shapes=[
                 pltpu.VMEM((rows * 6 * y_own, LANES), f32),
-                pltpu.VMEM((6, length_y, LANES), f32),
                 pltpu.VMEM((2 * length_y, 3 * LANES), f32),
                 pltpu.VMEM((length_y, 3 * LANES), f32),
-                pltpu.VMEM((3, length_y, LANES), f32),
                 pltpu.VMEM((rows * BACK, LANES), f32),
             ],
         )(near(lines), near(normal_pair))
@@ -262,11 +268,13 @@
         out_shape=(local_shape(packed, bf16), local_shape(a.shape, f32), local_shape(u.shape, bf16)),
         scratch_shapes=[pack_stage, pltpu.SemaphoreType.DMA((6,))],
     )(a, u)
-    send, normal_pair = lax.optimization_barrier((send, normal_pair))
     recv = lax.ppermute(send, "cols", partner)
     keep = pl.pallas_call(
         pack_keep_kernel, name="pack_keep", out_shape=local_shape(packed, bf16), scratch_shapes=[pack_stage]
     )(near(a), near(u))
+    normal_pair = pl.pallas_call(
+        permute_kernel, name="permute_y", out_shape=local_shape(normal_pair.shape, bf16)
+    )(near(normal_pair))
     base = pl.pallas_call(x_kernel, name="x_terms", out_shape=local_shape(a.shape, f32))(
         near(a), near(u), near(stream_pair)
     )

time: 58.4 us -> 60.4 us (1.034)
  local copies, waits for them, and re-layouts: 0.03 us -> 1.66 us
  waiting for transfers between devices: 1.77 us -> 0.85 us
  Pallas kernels: 3.57 us -> 4.45 us
    unnamed x6, local copies, waits for them, and re-layouts: 0.01 us -> 1.65 us
    pallas_call x0 -> x1, Pallas kernels: none -> 1.02 us  [local(): pl.pallas_call(permute_kernel, name='permute_y', out_shape=local_shape(no...]
    ppermute x1, waiting for transfers between devices: 0.92 us -> 0.01 us  [local(): recv = lax.ppermute(send, 'cols', partner)]
  transfers between devices with their start and end apart: 2 -> 2, of which waited for: 2 -> 1; matrix products, arithmetic and copies ran while one was open for 0% -> 0% of each run, Pallas kernels for 1% -> 3%
where the time goes in v7:
time: 60.4 us; the launch traced here: 60.1 us
  blocking collectives  42 us (70%)
  starting transfers between devices  10.9 us (18%)
  Pallas kernels  4.45 us (7%)
  local copies, waits for them, and re-layouts  1.66 us (3%)
  waiting for transfers between devices  0.85 us (1%)
    all_to_all x1, blocking collectives, along_y(): lines = exchange(jnp.concatenate([keep, recv], axis=0), 'rows')  25.2 us
    all_to_all x1, blocking collectives, along_y(): return exchange(terms, 'rows')  16.8 us
    ppermute x1, starting transfers between devices, local(): recv = lax.ppermute(send, 'cols', partner)  8.86 us
    ppermute x1, starting transfers between devices, local(): other = lax.ppermute(both[rows // 2:], 'cols', partner)  2.05 us
    unnamed x6, local copies, waits for them, and re-layouts  1.65 us
  transfers between devices with their start and end apart: 2, of which 1 were waited for; matrix products, arithmetic and copies ran while one was open for 0% of the time, Pallas kernels for 3%

profile of v7, /device:TPU:1, one launch (start us, length us, event | category | flops | bytes accessed | tf_op | source)
XLA Modules:
  0.0 60.1 jit_solution(5548727321420825339)
XLA Ops:
  0.0 1.1 %pack_send.1 = (bf16[16,72,128]{2,1,0:T(8,128)(2,1)S(1)}, f32[3,12,8,256]{3,2,1,0:T(8,128)S(1)}, bf16[3,12,8,256]{3,2,1,0:T(8,128)(2,1)S(1)}) custom-call(f32[3,12,8,256]{3,2,1,0:T(8,128)} %bitcast.7, bf16[3,12,8,256]{3,2,1,0:T(8,128)(2,1)} %bitcast.8), custom_call_target="tpu_custom_call" | custom-call | tf_op jit(solution)/shard_map/pack_send/pallas_call | solution.py:264
  1.1 8.9 %collective-permute-start = (bf16[16,72,128]{2,1,0:T(8,128)(2,1)S(1)}, bf16[16,72,128]{2,1,0:T(8,128)(2,1)S(1)}, u32[]{:S(2)}, u32[]{:S(2)}) collective-permute-start(bf16[16,72,128]{2,1,0:T(8,128)(2,1)S(1)} %get-tuple-element.31), channel_id=1, source_target_pairs={{0,1},{1,0},{2,3},{3,2},{4,5},{5,4},{6,7},{7,6},{8,9},{9,8},{10,11... | collective-permute-start | bytes 884744 | tf_op jit(solution)/shard_map/ppermute | solution.py:271
  10.0 0.0 copy-start
  10.0 1.1 %copy-done = bf16[768,384]{1,0:T(8,128)(2,1)S(1)} copy-done((bf16[768,384]{1,0:T(8,128)(2,1)S(1)}, bf16[768,384]{1,0:T(8,128)(2,1)}, u32[]{:S(2)}) %copy-start) | copy-done | bytes 589848
  11.0 1.0 %permute_y.1 = bf16[768,384]{1,0:T(8,128)(2,1)S(1)} custom-call(bf16[768,384]{1,0:T(8,128)(2,1)S(1)} %copy-done), custom_call_target="tpu_custom_call" | custom-call | tf_op jit(solution)/shard_map/permute_y/pallas_call | solution.py:275
  12.1 0.0 copy-start.2
  12.1 0.2 pack_keep.1
  12.3 0.0 collective-permute-done
  12.3 0.6 copy-done.2
  12.9 43.0 %conditional.1 = (bf16[32,40,128]{2,1,0:T(8,128)(2,1)S(1)}) conditional(s32[]{:T(128)} %convert_element_type.3, (bf16[16,72,128]{2,1,0:T(8,128)(2,1)S(1)}, bf16[16,72,128]{2,1,0:T(8,128)(2,1)S(1)}, bf16[256,128]{1,0:T(8,128)(2,1)S(1)}) %tuple.15, (bf16[16,72,128]{2,1,0:T(8,128)(2,1)S(1)}, bf16[16,72,128]{2,1,0:T(8,128)(2,1)S(1)}, ...), branch_computations={%region_0.1_spmd, %region_1.2_spmd} | conditional | flops 294912 | bytes 3014664 | solution.py:281
  12.9 0.1 pad_maximum_fusion.1
  13.0 25.2 %all_to_all.18.ry_ref = bf16[32,72,128]{2,1,0:T(8,128)(2,1)S(1)} all-to-all(bf16[32,72,128]{2,1,0:T(8,128)(2,1)S(1)} %pad_maximum_fusion.1), channel_id=1, replica_groups=mesh['rows'=32,'cols'=16] {'rows'}, dimensions={0} | all-to-all | bytes 1179648 | tf_op jit(solution)/shard_map/cond/branch_1_fun/all_to_all | solution.py:230
  38.2 0.9 %y_terms.1 = bf16[32,40,128]{2,1,0:T(8,128)(2,1)S(1)} custom-call(bf16[32,72,128]{2,1,0:T(8,128)(2,1)S(1)} %all_to_all.18.ry_ref, bf16[768,384]{1,0:T(8,128)(2,1)S(1)} %get-tuple-element.25.py_ref), custom_call_target="tpu_custom_call" | custom-call | tf_op jit(solution)/shard_map/cond/branch_1_fun/y_terms/pallas_call | solution.py:231
  39.1 16.8 %all_to_all.19 = bf16[32,40,128]{2,1,0:T(8,128)(2,1)S(1)} all-to-all(bf16[32,40,128]{2,1,0:T(8,128)(2,1)S(1)} %y_terms.1), channel_id=1, replica_groups=mesh['rows'=32,'cols'=16] {'rows'}, dimensions={0} | all-to-all | bytes 655360 | tf_op jit(solution)/shard_map/cond/branch_1_fun/all_to_all | solution.py:242
  55.9 0.0 copy-start.1
  55.9 2.1 %collective-permute-start.1 = (bf16[16,40,128]{2,1,0:T(8,128)(2,1)S(1)}, bf16[16,40,128]{2,1,0:T(8,128)(2,1)S(1)}, u32[]{:S(2)}, u32[]{:S(2)}) collective-permute-start(bf16[16,40,128]{2,1,0:T(8,128)(2,1)S(1)} %slice.4), channel_id=1, source_target_pairs={{0,1},{1,0},{2,3},{3,2},{4,5},{5,4},{6,7},{7,6},{8,9},{9,8},{10,11... | collective-permute-start | bytes 491528 | tf_op jit(solution)/shard_map/ppermute | solution.py:282
  58.0 0.0 copy-done.1
  58.0 0.3 x_terms.1.base_ref
  58.3 0.2 add_own.1.base_ref
  58.5 0.8 %collective-permute-done.1.part_ref = bf16[16,40,128]{2,1,0:T(8,128)(2,1)S(1)} collective-permute-done((bf16[16,40,128]{2,1,0:T(8,128)(2,1)S(1)}, bf16[16,40,128]{2,1,0:T(8,128)(2,1)S(1)}, u32[]{:S(2)}, u32[]{:S(2)}) %collective-permute-start.1) | collective-permute-done | bytes 163872 | tf_op jit(solution)/shard_map/ppermute | solution.py:282
  59.3 0.7 %add_other.1 = f32[3,12,8,256]{3,2,1,0:T(8,128)} custom-call(f32[3,12,8,256]{3,2,1,0:T(8,128)S(1)} %add_own.1.base_ref, bf16[16,40,128]{2,1,0:T(8,128)(2,1)S(1)} %collective-permute-done.1.part_ref), custom_call_target="tpu_custom_call" | custom-call | tf_op jit(solution)/shard_map/add_other/pallas_call | solution.py:287
  (1 shorter events, 0.0 us)
Async XLA Ops:
  1.1 11.2 %collective-permute-start = (bf16[16,72,128]{2,1,0:T(8,128)(2,1)S(1)}, bf16[16,72,128]{2,1,0:T(8,128)(2,1)S(1)}, u32[]{:S(2)}, u32[]{:S(2)}) collective-permute-start(bf16[16,72,128]{2,1,0:T(8,128)(2,1)S(1)} %get-tuple-element.31), channel_id=1, source_target_pairs={{0,1},{1,0},{2,3},{3,2},{4,5},{5,4},{6,7},{7,6},{8,9},{9,8},{10,11... | collective-permute-start | bytes 884744 | tf_op jit(solution)/shard_map/ppermute | solution.py:271
  10.0 1.1 %copy-start = (bf16[768,384]{1,0:T(8,128)(2,1)S(1)}, bf16[768,384]{1,0:T(8,128)(2,1)}, u32[]{:S(2)}) copy-start(bf16[768,384]{1,0:T(8,128)(2,1)} %py_ref.1) | copy-start | bytes 1769476
  12.1 0.8 %copy-start.2 = (bf16[256,128]{1,0:T(8,128)(2,1)S(1)}, bf16[256,128]{1,0:T(8,128)(2,1)}, u32[]{:S(2)}) copy-start(bf16[256,128]{1,0:T(8,128)(2,1)} %param.11) | copy-start | bytes 196612
  55.9 2.1 %copy-start.1 = (bf16[512,256]{1,0:T(8,128)(2,1)S(1)}, bf16[512,256]{1,0:T(8,128)(2,1)}, u32[]{:S(2)}) copy-start(bf16[512,256]{1,0:T(8,128)(2,1)} %px_ref.1) | copy-start | bytes 786436
  55.9 3.4 %collective-permute-start.1 = (bf16[16,40,128]{2,1,0:T(8,128)(2,1)S(1)}, bf16[16,40,128]{2,1,0:T(8,128)(2,1)S(1)}, u32[]{:S(2)}, u32[]{:S(2)}) collective-permute-start(bf16[16,40,128]{2,1,0:T(8,128)(2,1)S(1)} %slice.4), channel_id=1, source_target_pairs={{0,1},{1,0},{2,3},{3,2},{4,5},{5,4},{6,7},{7,6},{8,9},{9,8},{10,11... | collective-permute-start | bytes 491528 | tf_op jit(solution)/shard_map/ppermute | solution.py:282

commit v8 on v6

--- a/solution.py
+++ b/solution.py
@@ -108,17 +108,13 @@
             oz_ref[:, :, 3 * c + y] = term.reshape(chips, 2, z_own, LANES).astype(jnp.bfloat16)
 
 
-def y_kernel(ry_ref, py_ref, oy_ref, stage, lines, derivs, base_derivs, terms, back):
+def y_kernel(ry_ref, py_ref, oy_ref, lines, derivs, base_derivs, terms):
     peers, rows = ry_ref.shape[:2]
     y_own = rows // 6
     length = peers * y_own
-    stage[...] = ry_ref[...].astype(jnp.float32).reshape(stage.shape)
     for f in range(6):
-        for y in range(y_own):
-            for g in range(peers // 8):
-                lines[f, pl.ds(8 * g * y_own + y, 8, stride=y_own), :] = stage[
-                    pl.ds(8 * g * rows + f * y_own + y, 8, stride=rows), :
-                ]
+        for p in range(peers):
+            lines[f, pl.ds(p * y_own, y_own), :] = ry_ref[p, pl.ds(f * y_own, y_own), :].astype(jnp.float32)
     packed = [lines[f].astype(jnp.bfloat16) for f in range(6)]
     derivs[...] = jnp.dot(
         py_ref[...], jnp.concatenate(packed[:3], axis=1), preferred_element_type=jnp.float32
@@ -137,16 +133,10 @@
             if c == 1:
                 term = term - transfer
             terms[c, at, :] = term
-    for c in range(3):
-        for y in range(y_own):
-            for g in range(peers // 8):
-                back[pl.ds(8 * g * BACK + c * y_own + y, 8, stride=BACK), :] = terms[
-                    c, pl.ds(8 * g * y_own + y, 8, stride=y_own), :
-                ]
     for p in range(peers):
-        used = 3 * y_own
-        back[pl.ds(p * BACK + used, BACK - used), :] = jnp.zeros((BACK - used, LANES), jnp.float32)
-    oy_ref[...] = back[...].reshape(peers, BACK, LANES).astype(jnp.bfloat16)
+        parts = [terms[c, pl.ds(p * y_own, y_own), :] for c in range(3)]
+        parts.append(jnp.zeros((BACK - 3 * y_own, LANES), jnp.float32))
+        oy_ref[p] = jnp.concatenate(parts, axis=0).astype(jnp.bfloat16)
 
 
 def order_kernel(rz_ref, out_ref):
@@ -225,12 +215,10 @@
             name="y_terms",
             out_shape=local_shape((rows, BACK, LANES), bf16),
             scratch_shapes=[
-                pltpu.VMEM((rows * 6 * y_own, LANES), f32),
                 pltpu.VMEM((6, length_y, LANES), f32),
                 pltpu.VMEM((2 * length_y, 3 * LANES), f32),
                 pltpu.VMEM((length_y, 3 * LANES), f32),
                 pltpu.VMEM((3, length_y, LANES), f32),
-                pltpu.VMEM((rows * BACK, LANES), f32),
             ],
         )(near(lines), near(normal_pair))
         return exchange(terms, "rows")

time: 58.4 us -> 58.3 us (level)
  no operation moved by 1% of the time
where the time goes in v8:
time: 58.3 us; the launch traced here: 58 us
  blocking collectives  41.8 us (72%)
  starting transfers between devices  10.9 us (19%)
  Pallas kernels  3.42 us (6%)
  waiting for transfers between devices  1.77 us (3%)
    all_to_all x1, blocking collectives, along_y(): lines = exchange(jnp.concatenate([keep, recv], axis=0), 'rows')  25.2 us
    all_to_all x1, blocking collectives, along_y(): return exchange(terms, 'rows')  16.5 us
    ppermute x1, starting transfers between devices, local(): recv = lax.ppermute(send, 'cols', partner)  8.86 us
    ppermute x1, starting transfers between devices, local(): other = lax.ppermute(both[rows // 2:], 'cols', partner)  2.05 us
  transfers between devices with their start and end apart: 2, of which 2 were waited for; matrix products, arithmetic and copies ran while one was open for 0% of the time, Pallas kernels for 1%

profile of v8, /device:TPU:1, one launch (start us, length us, event | category | flops | bytes accessed | tf_op | source)
XLA Modules:
  0.0 58.0 jit_solution(3266515115738211360)
XLA Ops:
  0.0 0.0 copy-start
  0.0 1.1 %pack_send.1 = (bf16[16,72,128]{2,1,0:T(8,128)(2,1)S(1)}, f32[3,12,8,256]{3,2,1,0:T(8,128)S(1)}, bf16[3,12,8,256]{3,2,1,0:T(8,128)(2,1)S(1)}) custom-call(f32[3,12,8,256]{3,2,1,0:T(8,128)} %bitcast.7, bf16[3,12,8,256]{3,2,1,0:T(8,128)(2,1)} %bitcast.8), custom_call_target="tpu_custom_call" | custom-call | tf_op jit(solution)/shard_map/pack_send/pallas_call | solution.py:246
  1.2 8.9 %collective-permute-start = (bf16[16,72,128]{2,1,0:T(8,128)(2,1)S(1)}, bf16[16,72,128]{2,1,0:T(8,128)(2,1)S(1)}, u32[]{:S(2)}, u32[]{:S(2)}) collective-permute-start(bf16[16,72,128]{2,1,0:T(8,128)(2,1)S(1)} %get-tuple-element.34), channel_id=1, source_target_pairs={{0,1},{1,0},{2,3},{3,2},{4,5},{5,4},{6,7},{7,6},{8,9},{9,8},{10,11... | collective-permute-start | bytes 884744 | tf_op jit(solution)/shard_map/ppermute | solution.py:254
  10.0 0.0 copy-start.2
  10.0 0.2 pack_keep.1
  10.3 0.9 %collective-permute-done = bf16[16,72,128]{2,1,0:T(8,128)(2,1)S(1)} collective-permute-done((bf16[16,72,128]{2,1,0:T(8,128)(2,1)S(1)}, bf16[16,72,128]{2,1,0:T(8,128)(2,1)S(1)}, u32[]{:S(2)}, u32[]{:S(2)}) %collective-permute-start) | collective-permute-done | bytes 294944 | tf_op jit(solution)/shard_map/ppermute | solution.py:254
  11.2 0.0 copy-done
  11.2 0.0 copy-done.2
  11.2 42.6 %conditional.1 = (bf16[32,40,128]{2,1,0:T(8,128)(2,1)S(1)}) conditional(s32[]{:T(128)} %convert_element_type.3, (bf16[16,72,128]{2,1,0:T(8,128)(2,1)S(1)}, bf16[16,72,128]{2,1,0:T(8,128)(2,1)S(1)}, bf16[256,128]{1,0:T(8,128)(2,1)S(1)}) %tuple.18, (bf16[16,72,128]{2,1,0:T(8,128)(2,1)S(1)}, bf16[16,72,128]{2,1,0:T(8,128)(2,1)S(1)}, ...), branch_computations={%region_0.1_spmd, %region_1.2_spmd} | conditional | flops 294912 | bytes 3014664 | solution.py:261
  11.2 0.1 pad_maximum_fusion.1
  11.3 25.2 %all_to_all.18.ry_ref = bf16[32,72,128]{2,1,0:T(8,128)(2,1)S(1)} all-to-all(bf16[32,72,128]{2,1,0:T(8,128)(2,1)S(1)} %pad_maximum_fusion.1), channel_id=1, replica_groups=mesh['rows'=32,'cols'=16] {'rows'}, dimensions={0} | all-to-all | bytes 1179648 | tf_op jit(solution)/shard_map/cond/branch_1_fun/all_to_all | solution.py:212
  36.5 0.8 %y_terms.1 = bf16[32,40,128]{2,1,0:T(8,128)(2,1)S(1)} custom-call(bf16[32,72,128]{2,1,0:T(8,128)(2,1)S(1)} %all_to_all.18.ry_ref, bf16[768,384]{1,0:T(8,128)(2,1)S(1)} %get-tuple-element.25.py_ref), custom_call_target="tpu_custom_call" | custom-call | tf_op jit(solution)/shard_map/cond/branch_1_fun/y_terms/pallas_call | solution.py:213
  37.3 16.5 %all_to_all.19 = bf16[32,40,128]{2,1,0:T(8,128)(2,1)S(1)} all-to-all(bf16[32,40,128]{2,1,0:T(8,128)(2,1)S(1)} %y_terms.1), channel_id=1, replica_groups=mesh['rows'=32,'cols'=16] {'rows'}, dimensions={0} | all-to-all | bytes 655360 | tf_op jit(solution)/shard_map/cond/branch_1_fun/all_to_all | solution.py:224
  53.9 0.0 copy-start.1
  53.9 2.1 %collective-permute-start.1 = (bf16[16,40,128]{2,1,0:T(8,128)(2,1)S(1)}, bf16[16,40,128]{2,1,0:T(8,128)(2,1)S(1)}, u32[]{:S(2)}, u32[]{:S(2)}) collective-permute-start(bf16[16,40,128]{2,1,0:T(8,128)(2,1)S(1)} %slice.4), channel_id=1, source_target_pairs={{0,1},{1,0},{2,3},{3,2},{4,5},{5,4},{6,7},{7,6},{8,9},{9,8},{10,11... | collective-permute-start | bytes 491528 | tf_op jit(solution)/shard_map/ppermute | solution.py:262
  55.9 0.0 copy-done.1
  55.9 0.3 x_terms.1.base_ref
  56.3 0.2 add_own.1.base_ref
  56.5 0.8 %collective-permute-done.1.part_ref = bf16[16,40,128]{2,1,0:T(8,128)(2,1)S(1)} collective-permute-done((bf16[16,40,128]{2,1,0:T(8,128)(2,1)S(1)}, bf16[16,40,128]{2,1,0:T(8,128)(2,1)S(1)}, u32[]{:S(2)}, u32[]{:S(2)}) %collective-permute-start.1) | collective-permute-done | bytes 163872 | tf_op jit(solution)/shard_map/ppermute | solution.py:262
  57.3 0.7 %add_other.1 = f32[3,12,8,256]{3,2,1,0:T(8,128)} custom-call(f32[3,12,8,256]{3,2,1,0:T(8,128)S(1)} %add_own.1.base_ref, bf16[16,40,128]{2,1,0:T(8,128)(2,1)S(1)} %collective-permute-done.1.part_ref), custom_call_target="tpu_custom_call" | custom-call | tf_op jit(solution)/shard_map/add_other/pallas_call | solution.py:267
  (1 shorter events, 0.0 us)
Async XLA Ops:
  0.0 11.2 %copy-start = (bf16[768,384]{1,0:T(8,128)(2,1)S(1)}, bf16[768,384]{1,0:T(8,128)(2,1)}, u32[]{:S(2)}) copy-start(bf16[768,384]{1,0:T(8,128)(2,1)} %param.10) | copy-start | bytes 1769476
  1.2 10.1 %collective-permute-start = (bf16[16,72,128]{2,1,0:T(8,128)(2,1)S(1)}, bf16[16,72,128]{2,1,0:T(8,128)(2,1)S(1)}, u32[]{:S(2)}, u32[]{:S(2)}) collective-permute-start(bf16[16,72,128]{2,1,0:T(8,128)(2,1)S(1)} %get-tuple-element.34), channel_id=1, source_target_pairs={{0,1},{1,0},{2,3},{3,2},{4,5},{5,4},{6,7},{7,6},{8,9},{9,8},{10,11... | collective-permute-start | bytes 884744 | tf_op jit(solution)/shard_map/ppermute | solution.py:254
  10.0 1.2 %copy-start.2 = (bf16[256,128]{1,0:T(8,128)(2,1)S(1)}, bf16[256,128]{1,0:T(8,128)(2,1)}, u32[]{:S(2)}) copy-start(bf16[256,128]{1,0:T(8,128)(2,1)} %param.11) | copy-start | bytes 196612
  53.9 2.1 %copy-start.1 = (bf16[512,256]{1,0:T(8,128)(2,1)S(1)}, bf16[512,256]{1,0:T(8,128)(2,1)}, u32[]{:S(2)}) copy-start(bf16[512,256]{1,0:T(8,128)(2,1)} %px_ref.1) | copy-start | bytes 786436
  53.9 3.4 %collective-permute-start.1 = (bf16[16,40,128]{2,1,0:T(8,128)(2,1)S(1)}, bf16[16,40,128]{2,1,0:T(8,128)(2,1)S(1)}, u32[]{:S(2)}, u32[]{:S(2)}) collective-permute-start(bf16[16,40,128]{2,1,0:T(8,128)(2,1)S(1)} %slice.4), channel_id=1, source_target_pairs={{0,1},{1,0},{2,3},{3,2},{4,5},{5,4},{6,7},{7,6},{8,9},{9,8},{10,11... | collective-permute-start | bytes 491528 | tf_op jit(solution)/shard_map/ppermute | solution.py:262

commit v9 on v8

--- a/solution.py
+++ b/solution.py
@@ -10,7 +10,7 @@
 viscosity = 0.5
 section_step = 0.5
 LANES = 128
-BACK = 40
+QUAD = 4
 
 
 def pack_field(is_y, f, value, out_ref, stage, y_own, z_own):
@@ -135,23 +135,27 @@
             terms[c, at, :] = term
     for p in range(peers):
         parts = [terms[c, pl.ds(p * y_own, y_own), :] for c in range(3)]
-        parts.append(jnp.zeros((BACK - 3 * y_own, LANES), jnp.float32))
-        oy_ref[p] = jnp.concatenate(parts, axis=0).astype(jnp.bfloat16)
+        oy_ref[p] = jnp.concatenate(parts, axis=0).reshape(oy_ref.shape[1:]).astype(jnp.bfloat16)
 
 
 def order_kernel(rz_ref, out_ref):
     pieces, _, slabs, z_own = rz_ref.shape[:4]
+    quads = out_ref.shape[1]
     for side in range(2):
         for p in range(pieces):
             for k in range(slabs):
-                row = (p * slabs + k) * z_own
-                out_ref[16 * side + row // BACK, pl.ds(row % BACK, z_own), :] = rz_ref[p, side, k]
-        for row in range(pieces * slabs * z_own, 16 * BACK, z_own):
-            out_ref[16 * side + row // BACK, pl.ds(row % BACK, z_own), :] = jnp.zeros((z_own, LANES), jnp.bfloat16)
+                value = rz_ref[p, side, k].astype(jnp.float32)
+                for part in range(2):
+                    quad = (p * slabs + k) * 2 + part
+                    out_ref[16 * side + quad // quads, quad % quads] = value[QUAD * part : QUAD * (part + 1)].astype(
+                        jnp.bfloat16
+                    )
 
 
 def add_parts(is_y, base_ref, part_ref, out_ref, stage, done):
     comps, y_own, z_own, _ = base_ref.shape
+    quads = part_ref.shape[1]
+    pitch = quads * QUAD
 
     @pl.when(is_y)
     def _():
@@ -164,7 +168,7 @@
             for y in range(y_own):
                 for half in range(2):
                     at = pl.ds(half * LANES, LANES)
-                    piece = stage[pl.ds(half * BACK + c * y_own + y, z_own, stride=2 * BACK), :]
+                    piece = stage[pl.ds(half * pitch + c * y_own + y, z_own, stride=2 * pitch), :]
                     out_ref[c, y, :, at] = base_ref[c, y, :, at] + section_step * piece
 
         @pl.when(jnp.logical_not(is_y))
@@ -172,8 +176,10 @@
             for y in range(y_own):
                 for half in range(2):
                     at = pl.ds(half * LANES, LANES)
-                    row = ((y // 3 * 2 + half) * 9 + c * 3 + y % 3) * z_own
-                    piece = part_ref[row // BACK, pl.ds(row % BACK, z_own), :].astype(jnp.float32)
+                    quad = ((y // 3 * 2 + half) * 9 + c * 3 + y % 3) * 2
+                    piece = jnp.concatenate(
+                        [part_ref[at_q // quads, at_q % quads].astype(jnp.float32) for at_q in (quad, quad + 1)], axis=0
+                    )
                     out_ref[c, y, :, at] = base_ref[c, y, :, at] + section_step * piece
 
         done(c)
@@ -213,7 +219,7 @@
         terms = pl.pallas_call(
             y_kernel,
             name="y_terms",
-            out_shape=local_shape((rows, BACK, LANES), bf16),
+            out_shape=local_shape((rows, 3 * y_own // QUAD, QUAD, LANES), bf16),
             scratch_shapes=[
                 pltpu.VMEM((6, length_y, LANES), f32),
                 pltpu.VMEM((2 * length_y, 3 * LANES), f32),
@@ -237,7 +243,7 @@
         )(near(lines), near(span_pair))
         back = exchange(terms, "cols", axis_index_groups=alike)
         ordered = pl.pallas_call(
-            order_kernel, name="order_z", out_shape=local_shape((rows, BACK, LANES), bf16)
+            order_kernel, name="order_z", out_shape=local_shape((rows, 3 * y_own // QUAD, QUAD, LANES), bf16)
         )(near(back))
         return ordered
 
@@ -260,7 +266,7 @@
     )
     both = lax.cond(lax.axis_index("cols") % 2 == 1, along_y, along_z, keep, recv)
     other = lax.ppermute(both[rows // 2 :], "cols", partner)
-    add_stage = pltpu.VMEM((16 * BACK, LANES), f32)
+    add_stage = pltpu.VMEM((16 * 3 * y_own, LANES), f32)
     base = pl.pallas_call(
         add_own_kernel, name="add_own", out_shape=local_shape(a.shape, f32), scratch_shapes=[add_stage]
     )(near(base), near(both))

time: 58.3 us -> 58.1 us (level)
  no operation moved by 1% of the time
where the time goes in v9:
time: 58.1 us; the launch traced here: 57.9 us
  blocking collectives  41.5 us (71%)
  starting transfers between devices  10.9 us (19%)
  Pallas kernels  3.45 us (6%)
  waiting for transfers between devices  1.76 us (3%)
    all_to_all x1, blocking collectives, along_y(): lines = exchange(jnp.concatenate([keep, recv], axis=0), 'rows')  25.2 us
    all_to_all x1, blocking collectives, along_y(): return exchange(terms, 'rows')  16.3 us
    ppermute x1, starting transfers between devices, local(): recv = lax.ppermute(send, 'cols', partner)  8.86 us
    ppermute x1, starting transfers between devices, local(): other = lax.ppermute(both[rows // 2:], 'cols', partner)  2.05 us
  transfers between devices with their start and end apart: 2, of which 2 were waited for; matrix products, arithmetic and copies ran while one was open for 0% of the time, Pallas kernels for 1%

profile of v9, /device:TPU:1, one launch (start us, length us, event | category | flops | bytes accessed | tf_op | source)
XLA Modules:
  0.0 57.9 jit_solution(10849919449788667672)
XLA Ops:
  0.0 0.0 copy-start
  0.0 1.1 %pack_send.1 = (bf16[16,72,128]{2,1,0:T(8,128)(2,1)S(1)}, f32[3,12,8,256]{3,2,1,0:T(8,128)S(1)}, bf16[3,12,8,256]{3,2,1,0:T(8,128)(2,1)S(1)}) custom-call(f32[3,12,8,256]{3,2,1,0:T(8,128)} %bitcast.7, bf16[3,12,8,256]{3,2,1,0:T(8,128)(2,1)} %bitcast.8), custom_call_target="tpu_custom_call" | custom-call | tf_op jit(solution)/shard_map/pack_send/pallas_call | solution.py:252
  1.2 8.9 %collective-permute-start = (bf16[16,72,128]{2,1,0:T(8,128)(2,1)S(1)}, bf16[16,72,128]{2,1,0:T(8,128)(2,1)S(1)}, u32[]{:S(2)}, u32[]{:S(2)}) collective-permute-start(bf16[16,72,128]{2,1,0:T(8,128)(2,1)S(1)} %get-tuple-element.34), channel_id=1, source_target_pairs={{0,1},{1,0},{2,3},{3,2},{4,5},{5,4},{6,7},{7,6},{8,9},{9,8},{10,11... | collective-permute-start | bytes 884744 | tf_op jit(solution)/shard_map/ppermute | solution.py:260
  10.0 0.0 copy-start.2
  10.0 0.2 pack_keep.1
  10.3 0.9 %collective-permute-done = bf16[16,72,128]{2,1,0:T(8,128)(2,1)S(1)} collective-permute-done((bf16[16,72,128]{2,1,0:T(8,128)(2,1)S(1)}, bf16[16,72,128]{2,1,0:T(8,128)(2,1)S(1)}, u32[]{:S(2)}, u32[]{:S(2)}) %collective-permute-start) | collective-permute-done | bytes 294944 | tf_op jit(solution)/shard_map/ppermute | solution.py:260
  11.2 0.0 copy-done
  11.2 0.0 copy-done.2
  11.2 42.4 %conditional.1 = (bf16[32,9,4,128]{3,2,1,0:T(4,128)(2,1)S(1)}) conditional(s32[]{:T(128)} %convert_element_type.3, (bf16[16,72,128]{2,1,0:T(8,128)(2,1)S(1)}, bf16[16,72,128]{2,1,0:T(8,128)(2,1)S(1)}, bf16[256,128]{1,0:T(8,128)(2,1)S(1)}) %tuple.18, (bf16[16,72,128]{2,1,0:T(8,128)(2,1)S(1)}, bf16[16,72,128]{2,1,0:T(8,128)(2,1)S(1)}, ...), branch_computations={%region_0.1_spmd, %region_1.2_spmd} | conditional | flops 294912 | bytes 2949128 | solution.py:267
  11.2 0.1 pad_maximum_fusion.1
  11.3 25.2 %all_to_all.18.ry_ref = bf16[32,72,128]{2,1,0:T(8,128)(2,1)S(1)} all-to-all(bf16[32,72,128]{2,1,0:T(8,128)(2,1)S(1)} %pad_maximum_fusion.1), channel_id=1, replica_groups=mesh['rows'=32,'cols'=16] {'rows'}, dimensions={0} | all-to-all | bytes 1179648 | tf_op jit(solution)/shard_map/cond/branch_1_fun/all_to_all | solution.py:218
  36.5 0.8 %y_terms.1 = bf16[32,9,4,128]{3,2,1,0:T(4,128)(2,1)S(1)} custom-call(bf16[32,72,128]{2,1,0:T(8,128)(2,1)S(1)} %all_to_all.18.ry_ref, bf16[768,384]{1,0:T(8,128)(2,1)S(1)} %get-tuple-element.25.py_ref), custom_call_target="tpu_custom_call" | custom-call | tf_op jit(solution)/shard_map/cond/branch_1_fun/y_terms/pallas_call | solution.py:219
  37.4 16.3 %all_to_all.19 = bf16[32,9,4,128]{3,2,1,0:T(4,128)(2,1)S(1)} all-to-all(bf16[32,9,4,128]{3,2,1,0:T(4,128)(2,1)S(1)} %y_terms.1), channel_id=1, replica_groups=mesh['rows'=32,'cols'=16] {'rows'}, dimensions={0} | all-to-all | bytes 589824 | tf_op jit(solution)/shard_map/cond/branch_1_fun/all_to_all | solution.py:230
  53.6 0.0 copy-start.1
  53.6 0.1 slice.4
  53.7 2.1 %collective-permute-start.1 = (bf16[16,9,4,128]{3,2,1,0:T(4,128)(2,1)S(1)}, bf16[16,9,4,128]{3,2,1,0:T(4,128)(2,1)S(1)}, u32[]{:S(2)}, u32[]{:S(2)}) collective-permute-start(bf16[16,9,4,128]{3,2,1,0:T(4,128)(2,1)S(1)} %slice.4), channel_id=1, source_target_pairs={{0,1},{1,0},{2,3},{3,2},{4,5},{5,4},{6,7},{7,6},{8,9},{9,8},{10,11... | collective-permute-start | bytes 442376 | tf_op jit(solution)/shard_map/ppermute | solution.py:268
  55.8 0.0 copy-done.1
  55.8 0.3 x_terms.1.base_ref
  56.1 0.1 add_own.1.base_ref
  56.3 0.8 %collective-permute-done.1.part_ref = bf16[16,9,4,128]{3,2,1,0:T(4,128)(2,1)S(1)} collective-permute-done((bf16[16,9,4,128]{3,2,1,0:T(4,128)(2,1)S(1)}, bf16[16,9,4,128]{3,2,1,0:T(4,128)(2,1)S(1)}, u32[]{:S(2)}, u32[]{:S(2)}) %collective-permute-start.1) | collective-permute-done | bytes 147488 | tf_op jit(solution)/shard_map/ppermute | solution.py:268
  57.1 0.8 %add_other.1 = f32[3,12,8,256]{3,2,1,0:T(8,128)} custom-call(f32[3,12,8,256]{3,2,1,0:T(8,128)S(1)} %add_own.1.base_ref, bf16[16,9,4,128]{3,2,1,0:T(4,128)(2,1)S(1)} %collective-permute-done.1.part_ref), custom_call_target="tpu_custom_call" | custom-call | tf_op jit(solution)/shard_map/add_other/pallas_call | solution.py:273
Async XLA Ops:
  0.0 11.2 %copy-start = (bf16[768,384]{1,0:T(8,128)(2,1)S(1)}, bf16[768,384]{1,0:T(8,128)(2,1)}, u32[]{:S(2)}) copy-start(bf16[768,384]{1,0:T(8,128)(2,1)} %param.10) | copy-start | bytes 1769476
  1.2 10.1 %collective-permute-start = (bf16[16,72,128]{2,1,0:T(8,128)(2,1)S(1)}, bf16[16,72,128]{2,1,0:T(8,128)(2,1)S(1)}, u32[]{:S(2)}, u32[]{:S(2)}) collective-permute-start(bf16[16,72,128]{2,1,0:T(8,128)(2,1)S(1)} %get-tuple-element.34), channel_id=1, source_target_pairs={{0,1},{1,0},{2,3},{3,2},{4,5},{5,4},{6,7},{7,6},{8,9},{9,8},{10,11... | collective-permute-start | bytes 884744 | tf_op jit(solution)/shard_map/ppermute | solution.py:260
  10.0 1.2 %copy-start.2 = (bf16[256,128]{1,0:T(8,128)(2,1)S(1)}, bf16[256,128]{1,0:T(8,128)(2,1)}, u32[]{:S(2)}) copy-start(bf16[256,128]{1,0:T(8,128)(2,1)} %param.11) | copy-start | bytes 196612
  53.6 2.1 %copy-start.1 = (bf16[512,256]{1,0:T(8,128)(2,1)S(1)}, bf16[512,256]{1,0:T(8,128)(2,1)}, u32[]{:S(2)}) copy-start(bf16[512,256]{1,0:T(8,128)(2,1)} %px_ref.1) | copy-start | bytes 786436
  53.7 3.4 %collective-permute-start.1 = (bf16[16,9,4,128]{3,2,1,0:T(4,128)(2,1)S(1)}, bf16[16,9,4,128]{3,2,1,0:T(4,128)(2,1)S(1)}, u32[]{:S(2)}, u32[]{:S(2)}) collective-permute-start(bf16[16,9,4,128]{3,2,1,0:T(4,128)(2,1)S(1)} %slice.4), channel_id=1, source_target_pairs={{0,1},{1,0},{2,3},{3,2},{4,5},{5,4},{6,7},{7,6},{8,9},{9,8},{10,11... | collective-permute-start | bytes 442376 | tf_op jit(solution)/shard_map/ppermute | solution.py:268

commit v10 on v9

--- a/solution.py
+++ b/solution.py
@@ -108,7 +108,7 @@
             oz_ref[:, :, 3 * c + y] = term.reshape(chips, 2, z_own, LANES).astype(jnp.bfloat16)
 
 
-def y_kernel(ry_ref, py_ref, oy_ref, lines, derivs, base_derivs, terms):
+def y_kernel(ry_ref, py_ref, oy_ref, lines, first, second, terms):
     peers, rows = ry_ref.shape[:2]
     y_own = rows // 6
     length = peers * y_own
@@ -116,20 +116,20 @@
         for p in range(peers):
             lines[f, pl.ds(p * y_own, y_own), :] = ry_ref[p, pl.ds(f * y_own, y_own), :].astype(jnp.float32)
     packed = [lines[f].astype(jnp.bfloat16) for f in range(6)]
-    derivs[...] = jnp.dot(
-        py_ref[...], jnp.concatenate(packed[:3], axis=1), preferred_element_type=jnp.float32
-    )
-    base_derivs[...] = jnp.dot(
-        py_ref[pl.ds(0, length), :], jnp.concatenate(packed[3:], axis=1), preferred_element_type=jnp.float32
+    first[...] = jnp.dot(
+        py_ref[pl.ds(0, length), :], jnp.concatenate(packed, axis=1), preferred_element_type=jnp.float32
+    )
+    second[...] = jnp.dot(
+        py_ref[pl.ds(length, length), :], jnp.concatenate(packed[:3], axis=1), preferred_element_type=jnp.float32
     )
     block = 48
     for b in range(length // block):
         at = pl.ds(b * block, block)
-        lane = [pl.ds(j * LANES, LANES) for j in range(3)]
+        lane = [pl.ds(j * LANES, LANES) for j in range(6)]
         u_dir = lines[4, at, :]
-        transfer = sum(lines[j, at, :] * base_derivs[at, lane[j]] for j in range(3))
+        transfer = sum(lines[j, at, :] * first[at, lane[3 + j]] for j in range(3))
         for c in range(3):
-            term = u_dir * derivs[at, lane[c]] + viscosity * derivs[pl.ds(length + b * block, block), lane[c]]
+            term = u_dir * first[at, lane[c]] + viscosity * second[at, lane[c]]
             if c == 1:
                 term = term - transfer
             terms[c, at, :] = term
@@ -222,7 +222,7 @@
             out_shape=local_shape((rows, 3 * y_own // QUAD, QUAD, LANES), bf16),
             scratch_shapes=[
                 pltpu.VMEM((6, length_y, LANES), f32),
-                pltpu.VMEM((2 * length_y, 3 * LANES), f32),
+                pltpu.VMEM((length_y, 6 * LANES), f32),
                 pltpu.VMEM((length_y, 3 * LANES), f32),
                 pltpu.VMEM((3, length_y, LANES), f32),
             ],

time: 58.1 us -> 58 us (level)
  no operation moved by 1% of the time
where the time goes in v10:
time: 58 us; the launch traced here: 57.8 us
  blocking collectives  41.5 us (72%)
  starting transfers between devices  10.9 us (19%)
  Pallas kernels  3.37 us (6%)
  waiting for transfers between devices  1.76 us (3%)
    all_to_all x1, blocking collectives, along_y(): lines = exchange(jnp.concatenate([keep, recv], axis=0), 'rows')  25.2 us
    all_to_all x1, blocking collectives, along_y(): return exchange(terms, 'rows')  16.3 us
    ppermute x1, starting transfers between devices, local(): recv = lax.ppermute(send, 'cols', partner)  8.86 us
    ppermute x1, starting transfers between devices, local(): other = lax.ppermute(both[rows // 2:], 'cols', partner)  2.05 us
  transfers between devices with their start and end apart: 2, of which 2 were waited for; matrix products, arithmetic and copies ran while one was open for 0% of the time, Pallas kernels for 1%

profile of v10, /device:TPU:1, one launch (start us, length us, event | category | flops | bytes accessed | tf_op | source)
XLA Modules:
  0.0 57.8 jit_solution(724571935003119390)
XLA Ops:
  0.0 0.0 copy-start
  0.0 1.1 %pack_send.1 = (bf16[16,72,128]{2,1,0:T(8,128)(2,1)S(1)}, f32[3,12,8,256]{3,2,1,0:T(8,128)S(1)}, bf16[3,12,8,256]{3,2,1,0:T(8,128)(2,1)S(1)}) custom-call(f32[3,12,8,256]{3,2,1,0:T(8,128)} %bitcast.7, bf16[3,12,8,256]{3,2,1,0:T(8,128)(2,1)} %bitcast.8), custom_call_target="tpu_custom_call" | custom-call | tf_op jit(solution)/shard_map/pack_send/pallas_call | solution.py:252
  1.2 8.9 %collective-permute-start = (bf16[16,72,128]{2,1,0:T(8,128)(2,1)S(1)}, bf16[16,72,128]{2,1,0:T(8,128)(2,1)S(1)}, u32[]{:S(2)}, u32[]{:S(2)}) collective-permute-start(bf16[16,72,128]{2,1,0:T(8,128)(2,1)S(1)} %get-tuple-element.34), channel_id=1, source_target_pairs={{0,1},{1,0},{2,3},{3,2},{4,5},{5,4},{6,7},{7,6},{8,9},{9,8},{10,11... | collective-permute-start | bytes 884744 | tf_op jit(solution)/shard_map/ppermute | solution.py:260
  10.0 0.0 copy-start.2
  10.0 0.2 pack_keep.1
  10.3 0.9 %collective-permute-done = bf16[16,72,128]{2,1,0:T(8,128)(2,1)S(1)} collective-permute-done((bf16[16,72,128]{2,1,0:T(8,128)(2,1)S(1)}, bf16[16,72,128]{2,1,0:T(8,128)(2,1)S(1)}, u32[]{:S(2)}, u32[]{:S(2)}) %collective-permute-start) | collective-permute-done | bytes 294944 | tf_op jit(solution)/shard_map/ppermute | solution.py:260
  11.2 0.0 copy-done
  11.2 0.0 copy-done.2
  11.2 42.3 %conditional.1 = (bf16[32,9,4,128]{3,2,1,0:T(4,128)(2,1)S(1)}) conditional(s32[]{:T(128)} %convert_element_type.3, (bf16[16,72,128]{2,1,0:T(8,128)(2,1)S(1)}, bf16[16,72,128]{2,1,0:T(8,128)(2,1)S(1)}, bf16[256,128]{1,0:T(8,128)(2,1)S(1)}) %tuple.18, (bf16[16,72,128]{2,1,0:T(8,128)(2,1)S(1)}, bf16[16,72,128]{2,1,0:T(8,128)(2,1)S(1)}, ...), branch_computations={%region_0.1_spmd, %region_1.2_spmd} | conditional | flops 294912 | bytes 2949128 | solution.py:267
  11.2 0.1 pad_maximum_fusion.1
  11.3 25.2 %all_to_all.18.ry_ref = bf16[32,72,128]{2,1,0:T(8,128)(2,1)S(1)} all-to-all(bf16[32,72,128]{2,1,0:T(8,128)(2,1)S(1)} %pad_maximum_fusion.1), channel_id=1, replica_groups=mesh['rows'=32,'cols'=16] {'rows'}, dimensions={0} | all-to-all | bytes 1179648 | tf_op jit(solution)/shard_map/cond/branch_1_fun/all_to_all | solution.py:218
  36.5 0.8 %y_terms.1 = bf16[32,9,4,128]{3,2,1,0:T(4,128)(2,1)S(1)} custom-call(bf16[32,72,128]{2,1,0:T(8,128)(2,1)S(1)} %all_to_all.18.ry_ref, bf16[768,384]{1,0:T(8,128)(2,1)S(1)} %get-tuple-element.25.py_ref), custom_call_target="tpu_custom_call" | custom-call | tf_op jit(solution)/shard_map/cond/branch_1_fun/y_terms/pallas_call | solution.py:219
  37.3 16.3 %all_to_all.19 = bf16[32,9,4,128]{3,2,1,0:T(4,128)(2,1)S(1)} all-to-all(bf16[32,9,4,128]{3,2,1,0:T(4,128)(2,1)S(1)} %y_terms.1), channel_id=1, replica_groups=mesh['rows'=32,'cols'=16] {'rows'}, dimensions={0} | all-to-all | bytes 589824 | tf_op jit(solution)/shard_map/cond/branch_1_fun/all_to_all | solution.py:230
  53.6 0.0 copy-start.1
  53.6 0.1 slice.4
  53.6 2.1 %collective-permute-start.1 = (bf16[16,9,4,128]{3,2,1,0:T(4,128)(2,1)S(1)}, bf16[16,9,4,128]{3,2,1,0:T(4,128)(2,1)S(1)}, u32[]{:S(2)}, u32[]{:S(2)}) collective-permute-start(bf16[16,9,4,128]{3,2,1,0:T(4,128)(2,1)S(1)} %slice.4), channel_id=1, source_target_pairs={{0,1},{1,0},{2,3},{3,2},{4,5},{5,4},{6,7},{7,6},{8,9},{9,8},{10,11... | collective-permute-start | bytes 442376 | tf_op jit(solution)/shard_map/ppermute | solution.py:268
  55.7 0.0 copy-done.1
  55.7 0.3 x_terms.1.base_ref
  56.0 0.1 add_own.1.base_ref
  56.2 0.8 %collective-permute-done.1.part_ref = bf16[16,9,4,128]{3,2,1,0:T(4,128)(2,1)S(1)} collective-permute-done((bf16[16,9,4,128]{3,2,1,0:T(4,128)(2,1)S(1)}, bf16[16,9,4,128]{3,2,1,0:T(4,128)(2,1)S(1)}, u32[]{:S(2)}, u32[]{:S(2)}) %collective-permute-start.1) | collective-permute-done | bytes 147488 | tf_op jit(solution)/shard_map/ppermute | solution.py:268
  57.0 0.8 %add_other.1 = f32[3,12,8,256]{3,2,1,0:T(8,128)} custom-call(f32[3,12,8,256]{3,2,1,0:T(8,128)S(1)} %add_own.1.base_ref, bf16[16,9,4,128]{3,2,1,0:T(4,128)(2,1)S(1)} %collective-permute-done.1.part_ref), custom_call_target="tpu_custom_call" | custom-call | tf_op jit(solution)/shard_map/add_other/pallas_call | solution.py:273
Async XLA Ops:
  0.0 11.2 %copy-start = (bf16[768,384]{1,0:T(8,128)(2,1)S(1)}, bf16[768,384]{1,0:T(8,128)(2,1)}, u32[]{:S(2)}) copy-start(bf16[768,384]{1,0:T(8,128)(2,1)} %param.10) | copy-start | bytes 1769476
  1.2 10.1 %collective-permute-start = (bf16[16,72,128]{2,1,0:T(8,128)(2,1)S(1)}, bf16[16,72,128]{2,1,0:T(8,128)(2,1)S(1)}, u32[]{:S(2)}, u32[]{:S(2)}) collective-permute-start(bf16[16,72,128]{2,1,0:T(8,128)(2,1)S(1)} %get-tuple-element.34), channel_id=1, source_target_pairs={{0,1},{1,0},{2,3},{3,2},{4,5},{5,4},{6,7},{7,6},{8,9},{9,8},{10,11... | collective-permute-start | bytes 884744 | tf_op jit(solution)/shard_map/ppermute | solution.py:260
  10.0 1.2 %copy-start.2 = (bf16[256,128]{1,0:T(8,128)(2,1)S(1)}, bf16[256,128]{1,0:T(8,128)(2,1)}, u32[]{:S(2)}) copy-start(bf16[256,128]{1,0:T(8,128)(2,1)} %param.11) | copy-start | bytes 196612
  53.6 2.1 %copy-start.1 = (bf16[512,256]{1,0:T(8,128)(2,1)S(1)}, bf16[512,256]{1,0:T(8,128)(2,1)}, u32[]{:S(2)}) copy-start(bf16[512,256]{1,0:T(8,128)(2,1)} %px_ref.1) | copy-start | bytes 786436
  53.6 3.4 %collective-permute-start.1 = (bf16[16,9,4,128]{3,2,1,0:T(4,128)(2,1)S(1)}, bf16[16,9,4,128]{3,2,1,0:T(4,128)(2,1)S(1)}, u32[]{:S(2)}, u32[]{:S(2)}) collective-permute-start(bf16[16,9,4,128]{3,2,1,0:T(4,128)(2,1)S(1)} %slice.4), channel_id=1, source_target_pairs={{0,1},{1,0},{2,3},{3,2},{4,5},{5,4},{6,7},{7,6},{8,9},{9,8},{10,11... | collective-permute-start | bytes 442376 | tf_op jit(solution)/shard_map/ppermute | solution.py:268

commit v11 on v10

--- a/solution.py
+++ b/solution.py
@@ -108,7 +108,7 @@
             oz_ref[:, :, 3 * c + y] = term.reshape(chips, 2, z_own, LANES).astype(jnp.bfloat16)
 
 
-def y_kernel(ry_ref, py_ref, oy_ref, lines, first, second, terms):
+def y_kernel(ry_ref, py_ref, oy_ref, lines, first, second):
     peers, rows = ry_ref.shape[:2]
     y_own = rows // 6
     length = peers * y_own
@@ -122,20 +122,17 @@
     second[...] = jnp.dot(
         py_ref[pl.ds(length, length), :], jnp.concatenate(packed[:3], axis=1), preferred_element_type=jnp.float32
     )
-    block = 48
+    block = 2 * y_own
     for b in range(length // block):
         at = pl.ds(b * block, block)
         lane = [pl.ds(j * LANES, LANES) for j in range(6)]
         u_dir = lines[4, at, :]
         transfer = sum(lines[j, at, :] * first[at, lane[3 + j]] for j in range(3))
-        for c in range(3):
-            term = u_dir * first[at, lane[c]] + viscosity * second[at, lane[c]]
-            if c == 1:
-                term = term - transfer
-            terms[c, at, :] = term
-    for p in range(peers):
-        parts = [terms[c, pl.ds(p * y_own, y_own), :] for c in range(3)]
-        oy_ref[p] = jnp.concatenate(parts, axis=0).reshape(oy_ref.shape[1:]).astype(jnp.bfloat16)
+        terms = [u_dir * first[at, lane[c]] + viscosity * second[at, lane[c]] for c in range(3)]
+        terms[1] = terms[1] - transfer
+        for p in range(2):
+            parts = [term[p * y_own : (p + 1) * y_own] for term in terms]
+            oy_ref[2 * b + p] = jnp.concatenate(parts, axis=0).reshape(oy_ref.shape[1:]).astype(jnp.bfloat16)
 
 
 def order_kernel(rz_ref, out_ref):
@@ -224,7 +221,6 @@
                 pltpu.VMEM((6, length_y, LANES), f32),
                 pltpu.VMEM((length_y, 6 * LANES), f32),
                 pltpu.VMEM((length_y, 3 * LANES), f32),
-                pltpu.VMEM((3, length_y, LANES), f32),
             ],
         )(near(lines), near(normal_pair))
         return exchange(terms, "rows")

time: 58 us -> 58 us (level)
  no operation moved by 1% of the time
where the time goes in v11:
time: 58 us; the launch traced here: 57.7 us
  blocking collectives  41.5 us (72%)
  starting transfers between devices  10.9 us (19%)
  Pallas kernels  3.32 us (6%)
  waiting for transfers between devices  1.76 us (3%)
    all_to_all x1, blocking collectives, along_y(): lines = exchange(jnp.concatenate([keep, recv], axis=0), 'rows')  25.2 us
    all_to_all x1, blocking collectives, along_y(): return exchange(terms, 'rows')  16.3 us
    ppermute x1, starting transfers between devices, local(): recv = lax.ppermute(send, 'cols', partner)  8.86 us
    ppermute x1, starting transfers between devices, local(): other = lax.ppermute(both[rows // 2:], 'cols', partner)  2.05 us
  transfers between devices with their start and end apart: 2, of which 2 were waited for; matrix products, arithmetic and copies ran while one was open for 0% of the time, Pallas kernels for 1%

profile of v11, /device:TPU:1, one launch (start us, length us, event | category | flops | bytes accessed | tf_op | source)
XLA Modules:
  0.0 57.7 jit_solution(4836275406583359541)
XLA Ops:
  0.0 0.0 copy-start
  0.0 1.1 %pack_send.1 = (bf16[16,72,128]{2,1,0:T(8,128)(2,1)S(1)}, f32[3,12,8,256]{3,2,1,0:T(8,128)S(1)}, bf16[3,12,8,256]{3,2,1,0:T(8,128)(2,1)S(1)}) custom-call(f32[3,12,8,256]{3,2,1,0:T(8,128)} %bitcast.7, bf16[3,12,8,256]{3,2,1,0:T(8,128)(2,1)} %bitcast.8), custom_call_target="tpu_custom_call" | custom-call | tf_op jit(solution)/shard_map/pack_send/pallas_call | solution.py:248
  1.2 8.9 %collective-permute-start = (bf16[16,72,128]{2,1,0:T(8,128)(2,1)S(1)}, bf16[16,72,128]{2,1,0:T(8,128)(2,1)S(1)}, u32[]{:S(2)}, u32[]{:S(2)}) collective-permute-start(bf16[16,72,128]{2,1,0:T(8,128)(2,1)S(1)} %get-tuple-element.34), channel_id=1, source_target_pairs={{0,1},{1,0},{2,3},{3,2},{4,5},{5,4},{6,7},{7,6},{8,9},{9,8},{10,11... | collective-permute-start | bytes 884744 | tf_op jit(solution)/shard_map/ppermute | solution.py:256
  10.0 0.0 copy-start.2
  10.0 0.2 pack_keep.1
  10.3 0.9 %collective-permute-done = bf16[16,72,128]{2,1,0:T(8,128)(2,1)S(1)} collective-permute-done((bf16[16,72,128]{2,1,0:T(8,128)(2,1)S(1)}, bf16[16,72,128]{2,1,0:T(8,128)(2,1)S(1)}, u32[]{:S(2)}, u32[]{:S(2)}) %collective-permute-start) | collective-permute-done | bytes 294944 | tf_op jit(solution)/shard_map/ppermute | solution.py:256
  11.2 0.0 copy-done
  11.2 0.0 copy-done.2
  11.2 42.3 %conditional.1 = (bf16[32,9,4,128]{3,2,1,0:T(4,128)(2,1)S(1)}) conditional(s32[]{:T(128)} %convert_element_type.3, (bf16[16,72,128]{2,1,0:T(8,128)(2,1)S(1)}, bf16[16,72,128]{2,1,0:T(8,128)(2,1)S(1)}, bf16[256,128]{1,0:T(8,128)(2,1)S(1)}) %tuple.18, (bf16[16,72,128]{2,1,0:T(8,128)(2,1)S(1)}, bf16[16,72,128]{2,1,0:T(8,128)(2,1)S(1)}, ...), branch_computations={%region_0.1_spmd, %region_1.2_spmd} | conditional | flops 294912 | bytes 2949128 | solution.py:263
  11.2 0.1 pad_maximum_fusion.1
  11.3 25.2 %all_to_all.18.ry_ref = bf16[32,72,128]{2,1,0:T(8,128)(2,1)S(1)} all-to-all(bf16[32,72,128]{2,1,0:T(8,128)(2,1)S(1)} %pad_maximum_fusion.1), channel_id=1, replica_groups=mesh['rows'=32,'cols'=16] {'rows'}, dimensions={0} | all-to-all | bytes 1179648 | tf_op jit(solution)/shard_map/cond/branch_1_fun/all_to_all | solution.py:215
  36.5 0.7 %y_terms.1 = bf16[32,9,4,128]{3,2,1,0:T(4,128)(2,1)S(1)} custom-call(bf16[32,72,128]{2,1,0:T(8,128)(2,1)S(1)} %all_to_all.18.ry_ref, bf16[768,384]{1,0:T(8,128)(2,1)S(1)} %get-tuple-element.25.py_ref), custom_call_target="tpu_custom_call" | custom-call | tf_op jit(solution)/shard_map/cond/branch_1_fun/y_terms/pallas_call | solution.py:216
  37.2 16.3 %all_to_all.19 = bf16[32,9,4,128]{3,2,1,0:T(4,128)(2,1)S(1)} all-to-all(bf16[32,9,4,128]{3,2,1,0:T(4,128)(2,1)S(1)} %y_terms.1), channel_id=1, replica_groups=mesh['rows'=32,'cols'=16] {'rows'}, dimensions={0} | all-to-all | bytes 589824 | tf_op jit(solution)/shard_map/cond/branch_1_fun/all_to_all | solution.py:226
  53.5 0.0 copy-start.1
  53.5 0.1 slice.4
  53.6 2.1 %collective-permute-start.1 = (bf16[16,9,4,128]{3,2,1,0:T(4,128)(2,1)S(1)}, bf16[16,9,4,128]{3,2,1,0:T(4,128)(2,1)S(1)}, u32[]{:S(2)}, u32[]{:S(2)}) collective-permute-start(bf16[16,9,4,128]{3,2,1,0:T(4,128)(2,1)S(1)} %slice.4), channel_id=1, source_target_pairs={{0,1},{1,0},{2,3},{3,2},{4,5},{5,4},{6,7},{7,6},{8,9},{9,8},{10,11... | collective-permute-start | bytes 442376 | tf_op jit(solution)/shard_map/ppermute | solution.py:264
  55.6 0.0 copy-done.1
  55.6 0.3 x_terms.1.base_ref
  56.0 0.1 add_own.1.base_ref
  56.1 0.8 %collective-permute-done.1.part_ref = bf16[16,9,4,128]{3,2,1,0:T(4,128)(2,1)S(1)} collective-permute-done((bf16[16,9,4,128]{3,2,1,0:T(4,128)(2,1)S(1)}, bf16[16,9,4,128]{3,2,1,0:T(4,128)(2,1)S(1)}, u32[]{:S(2)}, u32[]{:S(2)}) %collective-permute-start.1) | collective-permute-done | bytes 147488 | tf_op jit(solution)/shard_map/ppermute | solution.py:264
  57.0 0.8 %add_other.1 = f32[3,12,8,256]{3,2,1,0:T(8,128)} custom-call(f32[3,12,8,256]{3,2,1,0:T(8,128)S(1)} %add_own.1.base_ref, bf16[16,9,4,128]{3,2,1,0:T(4,128)(2,1)S(1)} %collective-permute-done.1.part_ref), custom_call_target="tpu_custom_call" | custom-call | tf_op jit(solution)/shard_map/add_other/pallas_call | solution.py:269
Async XLA Ops:
  0.0 11.2 %copy-start = (bf16[768,384]{1,0:T(8,128)(2,1)S(1)}, bf16[768,384]{1,0:T(8,128)(2,1)}, u32[]{:S(2)}) copy-start(bf16[768,384]{1,0:T(8,128)(2,1)} %param.10) | copy-start | bytes 1769476
  1.2 10.1 %collective-permute-start = (bf16[16,72,128]{2,1,0:T(8,128)(2,1)S(1)}, bf16[16,72,128]{2,1,0:T(8,128)(2,1)S(1)}, u32[]{:S(2)}, u32[]{:S(2)}) collective-permute-start(bf16[16,72,128]{2,1,0:T(8,128)(2,1)S(1)} %get-tuple-element.34), channel_id=1, source_target_pairs={{0,1},{1,0},{2,3},{3,2},{4,5},{5,4},{6,7},{7,6},{8,9},{9,8},{10,11... | collective-permute-start | bytes 884744 | tf_op jit(solution)/shard_map/ppermute | solution.py:256
  10.0 1.2 %copy-start.2 = (bf16[256,128]{1,0:T(8,128)(2,1)S(1)}, bf16[256,128]{1,0:T(8,128)(2,1)}, u32[]{:S(2)}) copy-start(bf16[256,128]{1,0:T(8,128)(2,1)} %param.11) | copy-start | bytes 196612
  53.5 2.1 %copy-start.1 = (bf16[512,256]{1,0:T(8,128)(2,1)S(1)}, bf16[512,256]{1,0:T(8,128)(2,1)}, u32[]{:S(2)}) copy-start(bf16[512,256]{1,0:T(8,128)(2,1)} %px_ref.1) | copy-start | bytes 786436
  53.6 3.4 %collective-permute-start.1 = (bf16[16,9,4,128]{3,2,1,0:T(4,128)(2,1)S(1)}, bf16[16,9,4,128]{3,2,1,0:T(4,128)(2,1)S(1)}, u32[]{:S(2)}, u32[]{:S(2)}) collective-permute-start(bf16[16,9,4,128]{3,2,1,0:T(4,128)(2,1)S(1)} %slice.4), channel_id=1, source_target_pairs={{0,1},{1,0},{2,3},{3,2},{4,5},{5,4},{6,7},{7,6},{8,9},{9,8},{10,11... | collective-permute-start | bytes 442376 | tf_op jit(solution)/shard_map/ppermute | solution.py:264
